TPU v7x, 32 devices: a whole 2x2x4 slice. The times are simulated.
32 devices in a mesh: tm: 4 (over y, x), inner: 8 (over z, core).
Axes of the slice: x: 2, y: 2, z: 4, core: 2. Of those that a mesh axis runs over, the one named last changes fastest.
Arguments:
- frames: bfloat16 [32, 256, 768], P(('tm', 'inner')), may hold values from -6 to 6
- norm_gain: float32 [768], replicated, may hold values from 0.25 to 1.75
- w_qkv: bfloat16 [768, 2304], replicated, may hold values from -16 to 16
- w_out: bfloat16 [768, 768], replicated, may hold values from -0.21875 to 0.21875
- cotangent: bfloat16 [32, 256, 768], P(('tm', 'inner')), may hold values from -6 to 6
Outputs:
- block_out: bfloat16 [32, 256, 768], P(('tm', 'inner'))
- frames_grad: bfloat16 [32, 256, 768], P(('tm', 'inner'))
- qkv_weight_grad: float32 [768, 2304], P('inner', 'tm')
- out_weight_grad: float32 [768, 768], P('inner', 'tm')
- gain_grad: float32 [768], P('inner')
All inputs are finite; a program needn't handle non-finite values.
Results may differ from a plain program's by a relative error of at most 0.012.
The roundings to bfloat16 on the way count: a program that leaves them out, or rounds other values in their place, can miss the bound.
Values may be sent and summed in bfloat16 or wider, within the bound.
No kernel may reach another device: no remote copies, remote signals or barrier semaphores. Data moves between devices by JAX's collectives and lax.ppermute only.
A program may use at most 128 MiB of HBM per device.

v0:
```python
import math

import jax
import jax.numpy as jnp
from jax import lax
from jax.sharding import PartitionSpec as P

HEADS = 12
HEAD_DIM = 64
WINDOW = 4
CLIP_MAX = 256


EPSILON = 1e-06


def padded_2(cells, sides, width):
    for axis, dim in sides:
        count = lax.axis_size(axis)
        ends = count - 1
        head = lax.slice_in_dim(cells, 0, width, axis=dim)
        tail = lax.slice_in_dim(cells, cells.shape[dim] - width, cells.shape[dim], axis=dim)
        cells = jnp.concatenate(
            [
                lax.ppermute(tail, axis, [(i, (i + 1) % count) for i in range(ends)]),
                cells,
                lax.ppermute(head, axis, [((i + 1) % count, i) for i in range(ends)]),
            ],
            axis=dim,
        )
    return cells


def normalize(row_data, norm_gain):
    wide_vals = row_data.astype(jnp.float32)
    center = wide_vals - jnp.mean(wide_vals, axis=-1, keepdims=True)
    spread = lax.rsqrt(jnp.mean(center * center, axis=-1, keepdims=True) + EPSILON)
    unit_rows = center * spread
    return ((unit_rows * norm_gain).astype(jnp.bfloat16), unit_rows, spread)


def norm_back(normed_grad, unit_rows, spread, norm_gain):
    scaled = normed_grad * norm_gain
    mean_one = jnp.mean(scaled, axis=-1, keepdims=True)
    second = jnp.mean(scaled * unit_rows, axis=-1, keepdims=True)
    return spread * (scaled - mean_one - unit_rows * second)


def project(row_data, weight):
    flat_rows = row_data.reshape(-1, row_data.shape[-1])
    result = jnp.dot(flat_rows, weight, preferred_element_type=jnp.float32)
    return result.reshape(row_data.shape[:-1] + (weight.shape[1],))


def project_back(row_data, weight):
    flat_rows = row_data.reshape(-1, row_data.shape[-1])
    result = lax.dot_general(
        flat_rows, weight, (((1,), (1,)), ((), ())), preferred_element_type=jnp.float32
    )
    return result.reshape(row_data.shape[:-1] + (weight.shape[0],))


def contract(left_rows, right_rows):
    left_flat = left_rows.reshape(-1, left_rows.shape[-1])
    right_flat = right_rows.reshape(-1, right_rows.shape[-1])
    return lax.dot_general(
        left_flat, right_flat, (((0,), (0,)), ((), ())), preferred_element_type=jnp.float32
    )


def heads_of(row_data):
    return row_data.reshape(row_data.shape[:-1] + (HEADS, HEAD_DIM))


def attend(query_rows, key_pad, value_pad, first_frame, all_frames, clip_len):
    held_frames = query_rows.shape[0]
    span_len = 2 * WINDOW + 1
    score_scale = HEAD_DIM ** (-0.5)
    query_h = heads_of(query_rows)
    score_list = []
    for offset in range(span_len):
        key_h = heads_of(key_pad[offset : offset + held_frames])
        score_list.append(
            jnp.einsum("ftnd,ftnd->ftn", query_h, key_h, preferred_element_type=jnp.float32)
        )
    scores = jnp.stack(score_list) * score_scale
    query_at = first_frame + jnp.arange(held_frames)[None, :]
    frame_at = query_at + jnp.arange(span_len)[:, None] - WINDOW
    inside = (
        (frame_at >= 0) & (frame_at < all_frames) & (frame_at // clip_len == query_at // clip_len)
    )
    inside = inside[:, :, None, None]
    scores = jnp.where(inside, scores, -1e30)
    row_top = jnp.max(scores, axis=0, keepdims=True)
    exp_scores = jnp.exp(scores - row_top)
    soft_probs = exp_scores / jnp.sum(exp_scores, axis=0, keepdims=True)
    weights_b = soft_probs.astype(jnp.bfloat16)
    mixed_rows = jnp.zeros(query_h.shape, jnp.float32)
    for offset in range(span_len):
        value_h = heads_of(value_pad[offset : offset + held_frames]).astype(jnp.float32)
        mixed_rows = mixed_rows + weights_b[offset][..., None].astype(jnp.float32) * value_h
    mixed_rows = mixed_rows.reshape(query_rows.shape).astype(jnp.bfloat16)
    return (mixed_rows, soft_probs, weights_b)


def attend_back(query_rows, key_pad, value_pad, soft_probs, weights_b, grad_mix):
    held_frames = query_rows.shape[0]
    span_len = 2 * WINDOW + 1
    score_scale = HEAD_DIM ** (-0.5)
    query_h = heads_of(query_rows).astype(jnp.float32)
    grad_h = heads_of(grad_mix)
    dot_list = []
    for offset in range(span_len):
        value_h = heads_of(value_pad[offset : offset + held_frames])
        dot_list.append(
            jnp.einsum("ftnd,ftnd->ftn", grad_h, value_h, preferred_element_type=jnp.float32)
        )
    grad_dots = jnp.stack(dot_list)
    centre = jnp.sum(soft_probs * grad_dots, axis=0, keepdims=True)
    score_grad = (soft_probs * (grad_dots - centre) * score_scale).astype(jnp.bfloat16)
    grad_wide = grad_h.astype(jnp.float32)
    pad_shape = (key_pad.shape[0],) + query_h.shape[1:]
    query_grad = jnp.zeros(query_h.shape, jnp.float32)
    key_grad = jnp.zeros(pad_shape, jnp.float32)
    value_grad = jnp.zeros(pad_shape, jnp.float32)
    for offset in range(span_len):
        key_h = heads_of(key_pad[offset : offset + held_frames]).astype(jnp.float32)
        score_w = score_grad[offset][..., None].astype(jnp.float32)
        query_grad = query_grad + score_w * key_h
        key_grad = key_grad.at[offset : offset + held_frames].add(score_w * query_h)
        value_grad = value_grad.at[offset : offset + held_frames].add(
            weights_b[offset][..., None].astype(jnp.float32) * grad_wide
        )
    flat_shape = (key_pad.shape[0],) + query_rows.shape[1:]
    pad_grad = jnp.concatenate([key_grad.reshape(flat_shape), value_grad.reshape(flat_shape)], -1)
    return (query_grad.reshape(query_rows.shape), pad_grad)


def settle_rims(pad_grad, held_frames):
    edge_rows = jnp.concatenate([pad_grad[:WINDOW], pad_grad[WINDOW + held_frames :]], 0)
    returned = padded_2(edge_rows.astype(jnp.bfloat16), (("tm", 0),), WINDOW).astype(
        edge_rows.dtype
    )
    middle = pad_grad[WINDOW : WINDOW + held_frames]
    middle = middle.at[:WINDOW].add(returned[:WINDOW])
    middle = middle.at[held_frames - WINDOW :].add(returned[3 * WINDOW :])
    return middle


def shards(frames, norm_gain, w_qkv, w_out, cotangent):
    feat_width = frames.shape[-1]
    held_frames = frames.shape[0] * lax.axis_size("inner")
    all_frames = held_frames * lax.axis_size("tm")
    clip_len = min(CLIP_MAX, all_frames)
    first_frame = lax.axis_index("tm") * held_frames
    tokens_all = all_frames * frames.shape[1]
    tube_x = lax.all_to_all(frames, "inner", split_axis=1, concat_axis=0, tiled=True)
    padded = padded_2(tube_x, (("tm", 0),), WINDOW)
    normed_pad, unit_pad, spread_pad = normalize(padded, norm_gain)
    normed = normed_pad[WINDOW : WINDOW + held_frames]
    unit_rows = unit_pad[WINDOW : WINDOW + held_frames]
    spread = spread_pad[WINDOW : WINDOW + held_frames]
    qkv_rows = project(normed, w_qkv).astype(jnp.bfloat16)
    rim_rows = jnp.concatenate([normed_pad[:WINDOW], normed_pad[WINDOW + held_frames :]], 0)
    rim_kv = project(rim_rows, w_qkv[:, feat_width:]).astype(jnp.bfloat16)
    kv_pad = jnp.concatenate([rim_kv[:WINDOW], qkv_rows[..., feat_width:], rim_kv[WINDOW:]], 0)
    query_rows = qkv_rows[..., :feat_width]
    mixed_rows, soft_probs, weights_b = attend(
        query_rows,
        kv_pad[..., :feat_width],
        kv_pad[..., feat_width:],
        first_frame,
        all_frames,
        clip_len,
    )
    block_tube = (tube_x.astype(jnp.float32) + project(mixed_rows, w_out)).astype(jnp.bfloat16)
    block_out = lax.all_to_all(block_tube, "inner", split_axis=0, concat_axis=1, tiled=True)
    tube_cot = lax.all_to_all(cotangent, "inner", split_axis=1, concat_axis=0, tiled=True)
    out_grad = contract(mixed_rows, tube_cot)
    grad_mix = project_back(tube_cot, w_out).astype(jnp.bfloat16)
    query_grad, pad_grad = attend_back(
        query_rows,
        kv_pad[..., :feat_width],
        kv_pad[..., feat_width:],
        soft_probs,
        weights_b,
        grad_mix,
    )
    kv_grad = settle_rims(pad_grad, held_frames)
    qkv_rows_grad = jnp.concatenate([query_grad, kv_grad], -1).astype(jnp.bfloat16)
    qkv_grad = contract(normed, qkv_rows_grad)
    normed_grad = project_back(qkv_rows_grad, w_qkv)
    gain_part = jnp.sum(normed_grad * unit_rows, axis=(0, 1))
    grad_tube = (
        tube_cot.astype(jnp.float32) + norm_back(normed_grad, unit_rows, spread, norm_gain)
    ).astype(jnp.bfloat16)
    frames_grad = lax.all_to_all(grad_tube, "inner", split_axis=0, concat_axis=1, tiled=True)
    row_sums = (
        lax.psum_scatter(qkv_grad, "inner", scatter_dimension=0, tiled=True),
        lax.psum_scatter(out_grad, "inner", scatter_dimension=0, tiled=True),
        lax.psum_scatter(gain_part, "inner", scatter_dimension=0, tiled=True),
    )
    qkv_total, out_total = (
        lax.psum_scatter(row_sums[0], "tm", scatter_dimension=1, tiled=True),
        lax.psum_scatter(row_sums[1], "tm", scatter_dimension=1, tiled=True),
    )
    gain_share = lax.psum(row_sums[2], "tm")
    inv_root = 1.0 / math.sqrt(tokens_all)
    return (
        block_out,
        frames_grad,
        qkv_total * inv_root,
        out_total * inv_root,
        gain_share * inv_root,
    )


def solution(mesh):
    in_specs = (P(("tm", "inner"), None, None), P(), P(), P(), P(("tm", "inner"), None, None))
    out_specs = (
        P(("tm", "inner"), None, None),
        P(("tm", "inner"), None, None),
        P("inner", "tm"),
        P("inner", "tm"),
        P("inner"),
    )
    return jax.shard_map(shards, mesh=mesh, in_specs=in_specs, out_specs=out_specs, check_vma=False)
```

profile of v0, /device:TPU:0, one launch (start us, length us, event | category | flops | bytes accessed | tf_op | source)
XLA Modules:
  0.0 525.0 jit_solution(632729269858302665)
XLA Ops:
  9.4 3.0 reduce.76
  13.3 6.4 %all-to-all-start = ((bf16[8,2,12288]{2,1,0:T(2,128)(2,1)}), bf16[8,2,12288]{2,1,0:T(2,128)(2,1)S(1)}, u32[]{:S(2)}, u32[]{:S(2)}) async-start(bf16[8,2,12288]{2,1,0:T(2,128)(2,1)} %reshape.1216), calls=%async_computation | async-start | bytes 786432 | tf_op jit(solution)/shard_map/all_to_all | solution.py:157
  20.3 3.0 reduce.77
  24.1 8.0 %all-to-all-done = bf16[8,2,12288]{2,1,0:T(2,128)(2,1)S(1)} async-done(((bf16[8,2,12288]{2,1,0:T(2,128)(2,1)}), bf16[8,2,12288]{2,1,0:T(2,128)(2,1)S(1)}, u32[]{:S(2)}, u32[]{:S(2)}) %all-to-all-start) | async-done | bytes 393248 | tf_op jit(solution)/shard_map/all_to_all | solution.py:157
  32.2 3.5 all-to-all-start.2
  39.7 5.7 %collective-permute-start = (bf16[4,32,768]{2,1,0:T(8,128)(2,1)}, bf16[4,32,768]{2,1,0:T(8,128)(2,1)}, u32[]{:S(2)}, u32[]{:S(2)}) collective-permute-start(bf16[4,32,768]{2,1,0:T(8,128)(2,1)} %bitcast), channel_id=1, source_target_pairs={{0,8},{8,16},{16,24},{1,9},{9,17},{17,25},{2,10},{10,18},{18,26},{... | collective-permute-start | bytes 589832 | tf_op jit(solution)/shard_map/ppermute | solution.py:25
  66.1 3.9 fusion.71
  89.7 8.5 %fusion.13 = (f32[8,32,12]{2,1,0:T(8,128)}, f32[8,32,12]{2,1,0:T(8,128)}, f32[8,32,12]{2,1,0:T(8,128)}, f32[8,32,12]{2,1,0:T(8,128)}, f32[8,32,12]{2,1,0:T(8,128...) fusion(bf16[8,32,12,64]{3,2,1,0:T(8,128)(2,1)S(1)} %reshape.1111, ...), kind=kLoop, calls=%fused_computation.66 | loop fusion | flops 5477376 | bytes 4042752
  181.9 6.2 %add_convert_fusion.2 = (bf16[8,32,768]{2,1,0:T(8,128)(2,1)}, bf16[8,32,768]{2,1,0:T(8,128)(2,1)}, bf16[8,32,768]{2,1,0:T(8,128)(2,1)}, bf16[8,32,768]{2,1,0:T(8...) fusion(f32[8,32,768]{2,1,0:T(8,128)} %mul.420, ...), kind=kLoop, calls=%fused_computation.143 | loop fusion | flops 11599872 | bytes 12582912 | tf_op jit(solution)/shard_map/convert_element_type | solution.py:102
  207.8 4.0 scatter-add.81
  211.7 3.0 fusion.40
  214.7 3.0 fusion.42
  217.7 3.0 fusion.44
  220.6 3.0 fusion.46
  223.6 2.9 fusion.48
  226.6 3.1 fusion.50
  229.7 3.1 fusion.52
  233.6 9.7 %fusion.38 = (f32[8,32,12]{2,1,0:T(8,128)}, f32[8,32,12]{2,1,0:T(8,128)}, f32[8,32,12]{2,1,0:T(8,128)}, f32[8,32,12]{2,1,0:T(8,128)}, f32[8,32,12]{2,1,0:T(8,128...) fusion(bf16[8,32,12,64]{3,2,1,0:T(8,128)(2,1)S(1)} %reshape.112, ...), kind=kLoop, calls=%fused_computation.91 | loop fusion | flops 5870592 | bytes 9318400
  257.7 4.5 reshape.1132
  276.0 3.0 fusion.21
  281.9 3.0 fusion.25
  290.7 3.4 reshape.1131
  305.6 4.2 collective-permute-start.2
  355.9 5.0 add_convert_fusion.1
  364.7 4.0 convolution_bitcast_fusion
  372.1 4.5 all-to-all-start.1
  376.6 78.9 %reduce-scatter.9.cloned.1.call-done = f32[96,2304]{1,0:T(8,128)} async-done(((f32[768,2304]{1,0:T(8,128)}), f32[96,2304]{1,0:T(8,128)}) %reduce-scatter.9.cloned.1.call-update) | async-done | bytes 884752 | tf_op jit(solution)/shard_map/reduce_scatter | solution.py:199
  458.2 3.6 multiply_reduce_fusion
  462.8 3.5 all-to-all-start.3
  467.5 17.5 %all-reduce.2 = f32[768]{0:T(1024)S(1)} all-reduce(f32[768]{0:T(1024)S(1)} %get-tuple-element.245), channel_id=6, replica_groups=mesh['tm'=4,'inner'=8] {'inner'}, use_global_device_ids=true, to_apply=%region_12.13.clone | all-reduce | flops 768 | bytes 6144
  485.1 10.6 %psum.7 = f32[96]{0:T(128)S(1)} all-reduce(f32[96]{0:T(128)S(1)} %dynamic-slice.159), channel_id=1, replica_groups=mesh['tm'=4,'inner'=8] {'tm'}, use_global_device_ids=true, to_apply=%region_13.14 | all-reduce | flops 96 | bytes 768 | tf_op jit(solution)/shard_map/psum | solution.py:207
  497.9 17.1 %reduce-scatter.13.cloned.1.call-done = f32[576,96]{1,0:T(8,128)} async-done(((f32[2304,96]{1,0:T(8,128)}), f32[576,96]{1,0:T(8,128)}) %reduce-scatter.13.cloned.1.call-update) | async-done | bytes 221200
  (300 shorter events, 263.9 us)
Async XLA Ops:
  7.2 42.1 %copy-start = (bf16[768,768]{1,0:T(8,128)(2,1)S(1)}, bf16[768,768]{1,0:T(8,128)(2,1)}, u32[]{:S(2)}) copy-start(bf16[768,768]{1,0:T(8,128)(2,1)} %param.48) | copy-start | bytes 3538948
  7.2 12.5 %copy-start.43 = (bf16[1,256,768]{2,1,0:T(8,128)(2,1)S(1)}, bf16[1,256,768]{2,1,0:T(8,128)(2,1)}, u32[]{:S(2)}) copy-start(bf16[1,256,768]{2,1,0:T(8,128)(2,1)} %param.49) | copy-start | bytes 1179652
  13.3 18.9 %all-to-all-start = ((bf16[8,2,12288]{2,1,0:T(2,128)(2,1)}), bf16[8,2,12288]{2,1,0:T(2,128)(2,1)S(1)}, u32[]{:S(2)}, u32[]{:S(2)}) async-start(bf16[8,2,12288]{2,1,0:T(2,128)(2,1)} %reshape.1216), calls=%async_computation | async-start | bytes 786432 | tf_op jit(solution)/shard_map/all_to_all | solution.py:157
  32.2 15.9 %all-to-all-start.2 = ((bf16[8,2,12288]{2,1,0:T(2,128)(2,1)}), bf16[8,2,12288]{2,1,0:T(2,128)(2,1)S(1)}, u32[]{:S(2)}, u32[]{:S(2)}) async-start(bf16[8,2,12288]{2,1,0:T(2,128)(2,1)} %reshape.1218), calls=%async_computation.2 | async-start | bytes 786432 | tf_op jit(solution)/shard_map/all_to_all | solution.py:178
  35.6 333.3 %reduce-scatter.11.cloned.1.call-start = ((), (), s32[]{:S(2)}) async-start(), calls=%async_computation.9 | async-start | bytes 2654208 | tf_op jit(solution)/shard_map/reduce_scatter | solution.py:200
  35.7 81.5 %copy-start.44 = (pred[9,8]{1,0:T(8,128)(4,1)}, pred[9,8]{1,0:T(8,128)(4,1)S(1)}, u32[]{:S(2)}) copy-start(pred[9,8]{1,0:T(8,128)(4,1)S(1)} %fusion.109) | copy-start | bytes 220
  36.2 16.7 %copy-start.4 = (bf16[1,256,768]{2,1,0:T(8,128)(2,1)}, bf16[1,256,768]{2,1,0:T(8,128)(2,1)S(1)}, u32[]{:S(2)}) copy-start(bf16[1,256,768]{2,1,0:T(8,128)(2,1)S(1)} %copy.164) | copy-start | bytes 1179652
  38.4 12.0 %collective-permute-start.1 = (bf16[4,32,768]{2,1,0:T(8,128)(2,1)}, bf16[4,32,768]{2,1,0:T(8,128)(2,1)S(1)}, u32[]{:S(2)}, u32[]{:S(2)}) collective-permute-start(bf16[4,32,768]{2,1,0:T(8,128)(2,1)} %bitcast.1), channel_id=1, source_target_pairs={{8,0},{16,8},{24,16},{9,1},{17,9},{25,17},{10,2},{18,10},{26,18},{... | collective-permute-start | bytes 589832 | tf_op jit(solution)/shard_map/ppermute | solution.py:27
  39.7 10.7 %collective-permute-start = (bf16[4,32,768]{2,1,0:T(8,128)(2,1)}, bf16[4,32,768]{2,1,0:T(8,128)(2,1)}, u32[]{:S(2)}, u32[]{:S(2)}) collective-permute-start(bf16[4,32,768]{2,1,0:T(8,128)(2,1)} %bitcast), channel_id=1, source_target_pairs={{0,8},{8,16},{16,24},{1,9},{9,17},{17,25},{2,10},{10,18},{18,26},{... | collective-permute-start | bytes 589832 | tf_op jit(solution)/shard_map/ppermute | solution.py:25
  52.8 3.7 copy-start.46
  207.8 4.0 copy-start.40
  226.5 6.2 %copy-start.15 = (bf16[8,32,12,64]{3,2,1,0:T(8,128)(2,1)S(1)}, bf16[8,32,12,64]{3,2,1,0:T(8,128)(2,1)}, u32[]{:S(2)}) copy-start(bf16[8,32,12,64]{3,2,1,0:T(8,128)(2,1)} %reshape.1127) | copy-start | bytes 1179652
  226.5 6.2 %copy-start.16 = (bf16[8,32,12,64]{3,2,1,0:T(8,128)(2,1)S(1)}, bf16[8,32,12,64]{3,2,1,0:T(8,128)(2,1)}, u32[]{:S(2)}) copy-start(bf16[8,32,12,64]{3,2,1,0:T(8,128)(2,1)} %reshape.1128) | copy-start | bytes 1179652
  226.6 6.2 %copy-start.17 = (bf16[8,32,12,64]{3,2,1,0:T(8,128)(2,1)S(1)}, bf16[8,32,12,64]{3,2,1,0:T(8,128)(2,1)}, u32[]{:S(2)}) copy-start(bf16[8,32,12,64]{3,2,1,0:T(8,128)(2,1)} %reshape.1129) | copy-start | bytes 1179652
  226.6 6.2 %copy-start.18 = (bf16[8,32,12,64]{3,2,1,0:T(8,128)(2,1)S(1)}, bf16[8,32,12,64]{3,2,1,0:T(8,128)(2,1)}, u32[]{:S(2)}) copy-start(bf16[8,32,12,64]{3,2,1,0:T(8,128)(2,1)} %reshape.1130) | copy-start | bytes 1179652
  229.7 3.9 copy-start.14
  243.3 9.4 %copy-start.3 = (f32[9,8,32,12]{2,1,3,0:T(8,128)S(1)}, f32[9,8,32,12]{2,1,3,0:T(8,128)}, u32[]{:S(2)}) copy-start(f32[9,8,32,12]{2,1,3,0:T(8,128)} %copy-done.2) | copy-start | bytes 331780
  243.3 9.5 %copy-start.45 = (pred[9,8]{1,0:T(8,128)(4,1)S(1)}, pred[9,8]{1,0:T(8,128)(4,1)}, u32[]{:S(2)}) copy-start(pred[9,8]{1,0:T(8,128)(4,1)} %copy-done.44) | copy-start | bytes 220
  257.3 15.8 %copy-start.31 = (f32[8,32,12]{2,1,0:T(8,128)}, f32[8,32,12]{2,1,0:T(8,128)S(1)}, u32[]{:S(2)}) copy-start(f32[8,32,12]{2,1,0:T(8,128)S(1)} %copy.46) | copy-start | bytes 36868
  257.4 12.7 %copy-start.29 = (f32[8,32,12]{2,1,0:T(8,128)}, f32[8,32,12]{2,1,0:T(8,128)S(1)}, u32[]{:S(2)}) copy-start(f32[8,32,12]{2,1,0:T(8,128)S(1)} %copy.45) | copy-start | bytes 36868
  257.6 9.7 %copy-start.28 = (f32[8,32,12]{2,1,0:T(8,128)}, f32[8,32,12]{2,1,0:T(8,128)S(1)}, u32[]{:S(2)}) copy-start(f32[8,32,12]{2,1,0:T(8,128)S(1)} %copy.44) | copy-start | bytes 36868
  257.7 4.5 copy-start.23
  267.2 188.4 %reduce-scatter.9.cloned.1.call-start = ((), (), s32[]{:S(2)}) async-start(), calls=%async_computation.8 | async-start | bytes 7962624 | tf_op jit(solution)/shard_map/reduce_scatter | solution.py:199
  305.6 55.4 %collective-permute-start.2 = (bf16[4,32,1536]{2,1,0:T(8,128)(2,1)}, bf16[4,32,1536]{2,1,0:T(8,128)(2,1)}, u32[]{:S(2)}, u32[]{:S(2)}) collective-permute-start(bf16[4,32,1536]{2,1,0:T(8,128)(2,1)} %get-tuple-element.275), channel_id=1, source_target_pairs={{0,8},{8,16},{16,24},{1,9},{9,17},{17,25},{2,10},{10,18},{18,26},{... | collective-permute-start | bytes 1179656 | tf_op jit(solution)/shard_map/ppermute | solution.py:25
  309.7 51.3 %collective-permute-start.3 = (bf16[4,32,1536]{2,1,0:T(8,128)(2,1)}, bf16[4,32,1536]{2,1,0:T(8,128)(2,1)}, u32[]{:S(2)}, u32[]{:S(2)}) collective-permute-start(bf16[4,32,1536]{2,1,0:T(8,128)(2,1)} %get-tuple-element.276), channel_id=1, source_target_pairs={{8,0},{16,8},{24,16},{9,1},{17,9},{25,17},{10,2},{18,10},{26,18},{... | collective-permute-start | bytes 1179656 | tf_op jit(solution)/shard_map/ppermute | solution.py:27
  368.8 127.4 %reduce-scatter.15.cloned.1.call-start = ((), (), s32[]{:S(2)}) async-start(), calls=%async_computation.11 | async-start | bytes 491520
  372.1 86.0 %copy-start.20 = (f32[16,32,768]{2,1,0:T(8,128)S(1)}, f32[16,32,768]{2,1,0:T(8,128)}, u32[]{:S(2)}) copy-start(f32[16,32,768]{2,1,0:T(8,128)} %get-tuple-element.289) | copy-start | bytes 4718596
  372.1 86.1 %copy-start.49 = (f32[768]{0:T(1024)S(1)}, f32[768]{0:T(1024)}, u32[]{:S(2)}) copy-start(f32[768]{0:T(1024)} %param.46) | copy-start | bytes 9220
  372.1 90.7 %all-to-all-start.1 = ((bf16[8,32,768]{2,1,0:T(8,128)(2,1)}), bf16[8,32,768]{2,1,0:T(8,128)(2,1)S(1)}, u32[]{:S(2)}, u32[]{:S(2)}) async-start(bf16[8,32,768]{2,1,0:T(8,128)(2,1)} %fusion.58), calls=%async_computation.1 | async-start | bytes 786432 | tf_op jit(solution)/shard_map/all_to_all | solution.py:177
  376.6 138.4 %reduce-scatter.13.cloned.1.call-start = ((), (), s32[]{:S(2)}) async-start(), calls=%async_computation.10 | async-start | bytes 1474560
  461.8 4.5 copy-start.51
  462.8 33.4 %all-to-all-start.3 = ((bf16[8,32,768]{2,1,0:T(8,128)(2,1)}), bf16[8,32,768]{2,1,0:T(8,128)(2,1)S(1)}, u32[]{:S(2)}, u32[]{:S(2)}) async-start(bf16[8,32,768]{2,1,0:T(8,128)(2,1)} %add_convert_fusion), calls=%async_computation.3 | async-start | bytes 786432 | tf_op jit(solution)/shard_map/all_to_all | solution.py:197
  (32 other events, 79.2 us)
Sparse Core Ops, SparseCore 0:
  267.3 39.7 reduce-scatter.10
  368.9 86.5 reduce-scatter.8
  458.4 25.0 reduce-scatter.14
  486.2 28.6 reduce-scatter.12
where the time goes:
time: 535 us; the launch traced here: 525 us
  local copies, waits for them, and re-layouts  230 us (43%)
  waiting for transfers between devices  107 us (20%)
  other arithmetic  101 us (19%)
  starting transfers between devices  30.3 us (6%)
  blocking collectives  28.1 us (5%)
  between operations  15.5 us (3%)
  matrix products  13.3 us (2%)
    reduce_scatter x1, waiting for transfers between devices, shards(): lax.psum_scatter(qkv_grad, 'inner', scatter_dimension=0, tiled=True)  78.9 us
    mul x18, local copies, waits for them, and re-layouts, attend_back(): query_grad = query_grad + score_w * key_h  49.6 us
    mul x18, local copies, waits for them, and re-layouts, attend(): weights_b[offset][..., None].astype(jnp.float32) * value_h  48.5 us
    reshape x20, local copies, waits for them, and re-layouts, heads_of(): return row_data.reshape(row_data.shape[:-1] + (HEADS, HEAD_DIM))  45.6 us
    unnamed x140, local copies, waits for them, and re-layouts  27 us
    unnamed x4, other arithmetic  24.3 us
    scatter-add x8, other arithmetic, attend_back(): key_grad = key_grad.at[offset:offset + held_frames].add(score_w * query_h)  23.4 us
    scatter-add x7, other arithmetic, attend_back(): value_grad.at[offset:offset + held_frames]  20.9 us
  transfers between devices with their start and end apart: 12, of which 4 were waited for; matrix products, arithmetic and copies ran while one was open for 22% of the time, Pallas kernels for 0%

commit v1 on v0

v1 whole, which is shorter than its diff:
```python
import functools
import math

import jax
import jax.numpy as jnp
from jax import lax
from jax.experimental import pallas as pl
from jax.experimental.pallas import tpu as pltpu
from jax.sharding import PartitionSpec as P

HEADS = 12
HEAD_DIM = 64
WINDOW = 4
CLIP_MAX = 256
EPSILON = 1e-06

BF = jnp.bfloat16
F32 = jnp.float32
AXES = ("tm", "inner")
VMEM_LIMIT = 60 * 1024 * 1024


def mm(a, b):
    return lax.dot_general(a, b, (((1,), (0,)), ((), ())), preferred_element_type=F32)


def mm_t(a, b):
    return lax.dot_general(a, b, (((1,), (1,)), ((), ())), preferred_element_type=F32)


def params():
    return pltpu.CompilerParams(vmem_limit_bytes=VMEM_LIMIT)


def row_stats(x):
    center = x - jnp.mean(x, axis=-1, keepdims=True)
    spread = lax.rsqrt(jnp.mean(center * center, axis=-1, keepdims=True) + EPSILON)
    return center * spread, spread


def forward_kernel(x_ref, gain_ref, wqkv_ref, wout_ref, bias_ref, nt_ref, q_ref, kt_ref, v_ref, prob_ref, mixt_ref, block_ref, n_ref, qkv_ref):
    tokens, width = x_ref.shape
    x = x_ref[...].astype(F32)
    unit, _ = row_stats(x)
    normed = unit * gain_ref[...]
    n_ref[...] = normed.astype(BF)
    nt_ref[...] = normed.T.astype(BF)
    step = 256

    def project(i, carry):
        cols = pl.ds(pl.multiple_of(i * step, step), step)
        qkv_ref[:, cols] = mm(n_ref[...], wqkv_ref[:, cols]).astype(BF)
        return carry

    lax.fori_loop(0, 3 * width // step, project, 0)
    q_ref[...] = qkv_ref[:, :width]
    v_ref[...] = qkv_ref[:, 2 * width :]
    scale = HEAD_DIM ** (-0.5)

    def pair(i, carry):
        cols = pl.ds(pl.multiple_of(i * 128, 128), 128)
        q2 = qkv_ref[:, cols]
        k2 = qkv_ref[:, pl.ds(pl.multiple_of(width + i * 128, 128), 128)]
        v2 = qkv_ref[:, pl.ds(pl.multiple_of(2 * width + i * 128, 128), 128)]
        kt_ref[cols, :] = k2.astype(F32).T.astype(BF)
        v2t = v2.astype(F32).T.astype(BF)
        for half in range(2):
            span = slice(half * 64, half * 64 + 64)
            scores = mm_t(k2[:, span], q2[:, span]) * scale + bias_ref[...]
            grown = jnp.exp(scores - jnp.max(scores, axis=0, keepdims=True))
            probs = grown / jnp.sum(grown, axis=0, keepdims=True)
            prob_ref[2 * i + half] = probs
            mixt = mm(v2t[span, :], probs.astype(BF))
            mixt_ref[pl.ds(pl.multiple_of(i * 128 + half * 64, 64), 64), :] = mixt.astype(BF)
        return carry

    lax.fori_loop(0, HEADS // 2, pair, 0)
    mixed = mixt_ref[...].astype(F32).T.astype(BF)
    block_ref[...] = (x + mm(mixed, wout_ref[...])).astype(BF)


def put_blocks(dst_ref, src):
    parts, _, wide = dst_ref.shape
    for j in range(parts):
        dst_ref[j] = src[:, j * wide : (j + 1) * wide]


def backward_kernel(cot_ref, wout_ref, q_ref, kt_ref, v_ref, prob_ref, dqkv_ref, dblk_ref, cblk_ref, gm_ref, dqt_ref):
    tokens, width = cot_ref.shape
    gm_ref[...] = mm_t(cot_ref[...], wout_ref[...]).astype(BF)
    put_blocks(cblk_ref, cot_ref[...])
    scale = HEAD_DIM ** (-0.5)

    def pair(i, carry):
        cols = pl.ds(pl.multiple_of(i * 128, 128), 128)
        q2 = q_ref[:, cols]
        g2 = gm_ref[:, cols]
        v2 = v_ref[:, cols]
        dks, dvs = [], []
        for half in range(2):
            span = slice(half * 64, half * 64 + 64)
            probs = prob_ref[2 * i + half]
            dots = mm_t(v2[:, span], g2[:, span])
            centre = jnp.sum(probs * dots, axis=0, keepdims=True)
            sgrad = (probs * (dots - centre) * scale).astype(BF)
            rows = pl.ds(pl.multiple_of(i * 128 + half * 64, 64), 64)
            dqt_ref[rows, :] = mm(kt_ref[rows, :], sgrad)
            dks.append(mm(sgrad, q2[:, span]))
            dvs.append(mm(probs.astype(BF), g2[:, span]))
        dqkv_ref[:, pl.ds(pl.multiple_of(width + i * 128, 128), 128)] = jnp.concatenate(dks, 1).astype(BF)
        dqkv_ref[:, pl.ds(pl.multiple_of(2 * width + i * 128, 128), 128)] = jnp.concatenate(dvs, 1).astype(BF)
        return carry

    lax.fori_loop(0, HEADS // 2, pair, 0)
    dqkv_ref[:, :width] = dqt_ref[...].T.astype(BF)
    put_blocks(dblk_ref, dqkv_ref[...])


def norm_kernel(x_ref, cot_ref, gain_ref, dqkv_ref, wqkv_ref, fgrad_ref, gpart_ref):
    x = x_ref[...].astype(F32)
    unit, spread = row_stats(x)
    ngrad = mm_t(dqkv_ref[...], wqkv_ref[...])
    gpart_ref[...] = jnp.sum(ngrad * unit, axis=0, keepdims=True)
    scaled = ngrad * gain_ref[...]
    mean_one = jnp.mean(scaled, axis=-1, keepdims=True)
    second = jnp.mean(scaled * unit, axis=-1, keepdims=True)
    fgrad_ref[...] = (cot_ref[...].astype(F32) + spread * (scaled - mean_one - unit * second)).astype(BF)


def block_sum(table, got, o, nt_ref, mt_ref, db_ref, cb_ref):
    row, run = table[o, 0], table[o, 1]
    left = mm(nt_ref[row], db_ref[run])
    right = mm(mt_ref[row], cb_ref[run])
    half = left.shape[0] // 2
    folded = jnp.concatenate([left[:half], left[half:], right[:half], right[half:]], 1)
    for s, ref in enumerate(got):
        folded = folded + ref[table[o, 2 + s]].astype(F32)
    return folded


def send_kernel(table, nt_ref, mt_ref, db_ref, cb_ref, *rest):
    got, out_ref = rest[:-1], rest[-1]

    def one(o, carry):
        out_ref[o] = block_sum(table, got, o, nt_ref, mt_ref, db_ref, cb_ref).astype(BF)
        return carry

    lax.fori_loop(0, out_ref.shape[0], one, 0)


def last_kernel(inv_root, table, nt_ref, mt_ref, db_ref, cb_ref, *rest):
    got, (q_ref, o_ref) = rest[:-2], rest[-2:]
    total = block_sum(table, got, 0, nt_ref, mt_ref, db_ref, cb_ref) * inv_root
    half = q_ref.shape[0] // 2
    wide, thin = q_ref.shape[1], o_ref.shape[1]
    q_ref[:half] = total[:, :wide]
    q_ref[half:] = total[:, wide : 2 * wide]
    o_ref[:half] = total[:, 2 * wide : 2 * wide + thin]
    o_ref[half:] = total[:, 2 * wide + thin :]


def squeeze_bits(value, bits):
    for b in sorted(bits, reverse=True):
        value = (value >> (b + 1) << b) | (value & ((1 << b) - 1))
    return value


def spread_bits(value, bits):
    for b in sorted(bits):
        value = (value >> b << (b + 1)) | (value & ((1 << b) - 1))
    return value


def reduce_weights(nt, mixt, dblk, cblk, inv_root):
    runs, inner = lax.axis_size("tm"), lax.axis_size("inner")
    row_bits, run_bits = (inner // 2).bit_length() - 1, runs.bit_length() - 1
    me_t, me_i = lax.axis_index("tm"), lax.axis_index("inner")
    core = me_i & 1
    mine = (me_t << row_bits) | (me_i >> 1)
    run_order = [row_bits + b for b in range(run_bits)]
    tail = list(range(row_bits))
    order = [run_order + tail, run_order[1:] + run_order[:1] + tail]
    rows = nt.shape[0] // inner
    tokens = nt.shape[1]
    nt = nt.reshape(inner, rows, tokens)
    mixt = mixt.reshape(inner, rows, tokens)
    wide, thin = dblk.shape[2], cblk.shape[2]
    folded = (rows // 2, 2 * (wide + thin))
    stages = len(order[0])
    got = []

    def table_of(stage):
        entries = []
        for c in range(2):
            past = order[c][: max(stage, 0)]
            here = [] if stage < 0 or stage == stages else [order[c][stage]]
            ids = jnp.arange(1 << (len(order[c]) - len(past) - len(here)), dtype=jnp.int32)
            ids = spread_bits(ids, past + here)
            for b in past:
                ids = ids | (mine & (1 << b))
            for b in here:
                ids = ids | ((mine ^ (1 << b)) & (1 << b))
            row = (ids & ((1 << row_bits) - 1)) * 2 + (1 - c if stage < 0 else c)
            cols = [row, ids >> row_bits]
            if stage >= 0:
                for s in range(stage + 1):
                    cols.append(squeeze_bits(ids, order[c][:s]))
            entries.append(jnp.stack(cols, 1))
        return jnp.where(core == 0, entries[0], entries[1]).astype(jnp.int32)

    def call(kernel, table, out_shape):
        args = [nt, mixt, dblk, cblk, *got]
        return pl.pallas_call(
            kernel,
            out_shape=out_shape,
            in_specs=[pl.BlockSpec(memory_space=pltpu.SMEM)] + [pl.BlockSpec(memory_space=pltpu.VMEM)] * len(args),
            compiler_params=params(),
        )(table, *args)

    for stage in range(-1, stages):
        table = table_of(stage)
        out = call(send_kernel, table, jax.ShapeDtypeStruct((table.shape[0],) + folded, BF))
        perm = []
        for t in range(runs):
            for i in range(inner):
                if stage < 0:
                    t2, i2 = t, i ^ 1
                else:
                    b = order[i & 1][stage]
                    t2 = t ^ (1 << (b - row_bits)) if b >= row_bits else t
                    i2 = i ^ (2 << b) if b < row_bits else i
                perm.append((t * inner + i, t2 * inner + i2))
        got.append(lax.ppermute(out, AXES, perm))
    return call(
        functools.partial(last_kernel, inv_root),
        table_of(stages),
        (jax.ShapeDtypeStruct((rows, wide), F32), jax.ShapeDtypeStruct((rows, thin), F32)),
    )


def to_tubes(rows, count):
    held, patches, width = rows.shape
    parts = jnp.moveaxis(rows.reshape(held, count, patches // count, width), 1, 0)
    parts = lax.all_to_all(parts, AXES, split_axis=0, concat_axis=0, tiled=True)
    return parts.reshape(-1, width)


def to_frames(tubes, count, held, patches):
    width = tubes.shape[1]
    parts = tubes.reshape(count, held, patches // count, width)
    parts = lax.all_to_all(parts, AXES, split_axis=0, concat_axis=0, tiled=True)
    return jnp.moveaxis(parts, 0, 1).reshape(held, patches, width)


def window_bias(all_frames, patches, clip_len):
    tokens = all_frames * patches
    key = lax.broadcasted_iota(jnp.int32, (tokens, tokens), 0)
    query = lax.broadcasted_iota(jnp.int32, (tokens, tokens), 1)
    key_f, query_f = key // patches, query // patches
    inside = (key % patches == query % patches) & (abs(key_f - query_f) <= WINDOW)
    inside = inside & (key_f // clip_len == query_f // clip_len)
    return jnp.where(inside, 0.0, -1e30).astype(F32)


def shards(frames, norm_gain, w_qkv, w_out, cotangent):
    held, patches, width = frames.shape
    runs, inner = lax.axis_size("tm"), lax.axis_size("inner")
    count = runs * inner
    all_frames = held * count
    clip_len = min(CLIP_MAX, all_frames)
    inv_root = 1.0 / math.sqrt(all_frames * patches)
    tokens = all_frames * patches // count
    gain = norm_gain.reshape(1, width)
    bias = window_bias(all_frames, patches // count, clip_len)

    x = to_tubes(frames, count)
    cot = to_tubes(cotangent, count)
    sds = jax.ShapeDtypeStruct
    nt, q, kt, v, prob, mixt, block = pl.pallas_call(
        forward_kernel,
        out_shape=(
            sds((width, tokens), BF),
            sds((tokens, width), BF),
            sds((width, tokens), BF),
            sds((tokens, width), BF),
            sds((HEADS, tokens, tokens), F32),
            sds((width, tokens), BF),
            sds((tokens, width), BF),
        ),
        scratch_shapes=[pltpu.VMEM((tokens, width), BF), pltpu.VMEM((tokens, 3 * width), BF)],
        compiler_params=params(),
    )(x, gain, w_qkv, w_out, bias)
    block_out = to_frames(block, count, held, patches)
    dqkv, dblk, cblk = pl.pallas_call(
        backward_kernel,
        out_shape=(
            sds((tokens, 3 * width), BF),
            sds((runs, tokens, 3 * width // runs), BF),
            sds((runs, tokens, width // runs), BF),
        ),
        scratch_shapes=[pltpu.VMEM((tokens, width), BF), pltpu.VMEM((width, tokens), F32)],
        compiler_params=params(),
    )(cot, w_out, q, kt, v, prob)
    fgrad, gpart = pl.pallas_call(
        norm_kernel,
        out_shape=(sds((tokens, width), BF), sds((1, width), F32)),
        compiler_params=params(),
    )(x, cot, gain, dqkv, w_qkv)
    frames_grad = to_frames(fgrad, count, held, patches)
    shares = jnp.broadcast_to(gpart.reshape(1, inner, width // inner), (runs, inner, width // inner))
    shares = lax.all_to_all(shares.reshape(count, 1, -1), AXES, split_axis=0, concat_axis=0, tiled=True)
    gain_grad = jnp.sum(shares, axis=(0, 1)) * inv_root
    qkv_grad, out_grad = reduce_weights(nt, mixt, dblk, cblk, inv_root)
    return block_out, frames_grad, qkv_grad, out_grad, gain_grad


def solution(mesh):
    in_specs = (P(AXES, None, None), P(), P(), P(), P(AXES, None, None))
    out_specs = (P(AXES, None, None), P(AXES, None, None), P("inner", "tm"), P("inner", "tm"), P("inner"))
    return jax.shard_map(shards, mesh=mesh, in_specs=in_specs, out_specs=out_specs, check_vma=False)
```

time: 535 us -> 145 us (0.27); the launches traced: 525 us -> 145 us
  local copies, waits for them, and re-layouts: 230 us -> 9.62 us
  other arithmetic: 101 us -> 6 us
  waiting for transfers between devices: 107 us -> 43.6 us
  Pallas kernels: 0 us -> 58.4 us
  blocking collectives: 28.1 us -> 0 us
  between operations: 15.5 us -> 0.76 us
  matrix products: 13.3 us -> 0 us
    mul x36 -> x0, local copies, waits for them, and re-layouts: 98.1 us -> none  [the longest x18 49.6 us: attend_back(): query_grad = query_grad + score_w * key_h]
    reduce_scatter x2 -> x0, waiting for transfers between devices: 78.9 us -> none  [the longest x1 78.9 us: shards(): lax.psum_scatter(qkv_grad, 'inner', scatter_dimension=0, tiled=True)]
    pallas_call x0 -> x9, Pallas kernels: none -> 58.4 us  [the longest x6 30.7 us: call(): pl.pallas_call(kernel, out_shape=out_shape, in_specs=[pl.BlockSpec(memory...]
    reshape x22 -> x1, local copies, waits for them, and re-layouts: 53.5 us -> 1.27 us  [shards(): gain = norm_gain.reshape(1, width)]
    scatter-add x17 -> x0, other arithmetic: 47.1 us -> none  [the longest x8 23.4 us: attend_back(): key_grad = key_grad.at[offset:offset + held_frames].add(score_w * query_h)]
    unnamed x4 -> x0, other arithmetic: 24.3 us -> none
    dot_general x18 -> x0, local copies, waits for them, and re-layouts: 21.6 us -> none  [the longest x9 12.3 us: attend(): jnp.einsum('ftnd,ftnd->ftn', query_h, key_h, preferred_element_type=jnp.f...]
    unnamed x140 -> x16, local copies, waits for them, and re-layouts: 27 us -> 6.9 us
  transfers between devices with their start and end apart: 12 -> 10, of which waited for: 4 -> 7; matrix products, arithmetic and copies ran while one was open for 22% -> 6% of each run, Pallas kernels for 0% -> 21%
where the time goes in v1:
time: 145 us
  Pallas kernels  58.4 us (40%)
  waiting for transfers between devices  43.6 us (30%)
  starting transfers between devices  26.2 us (18%)
  local copies, waits for them, and re-layouts  9.62 us (7%)
  other arithmetic  6 us (4%)
    pallas_call x6, Pallas kernels, call(): pl.pallas_call(kernel, out_shape=out_shape, in_specs=[pl.BlockSpec(memory...  30.7 us
    ppermute x5, waiting for transfers between devices, reduce_weights(): got.append(lax.ppermute(out, AXES, perm))  19.7 us
    pallas_call x1, Pallas kernels, shards(): pl.pallas_call(forward_kernel, out_shape=(sds((width, tokens), BF), sds((...  12.2 us
    all_to_all x2, waiting for transfers between devices, to_tubes(): parts = lax.all_to_all(parts, AXES, split_axis=0, concat_axis=0, tiled=True)  12 us
    pallas_call x1, Pallas kernels, shards(): pl.pallas_call(backward_kernel, out_shape=(sds((tokens, 3 * width), BF),...  10.7 us
    all_to_all x2, starting transfers between devices, to_tubes(): parts = lax.all_to_all(parts, AXES, split_axis=0, concat_axis=0, tiled=True)  9.93 us
    all_to_all x1, waiting for transfers between devices, shards(): lax.all_to_all(shares.reshape(count, 1, -1), AXES, split_axis=0, concat_a...  7.07 us
    unnamed x16, local copies, waits for them, and re-layouts  6.9 us
  transfers between devices with their start and end apart: 10, of which 7 were waited for; matrix products, arithmetic and copies ran while one was open for 6% of the time, Pallas kernels for 21%

profile of v1, /device:TPU:0, one launch (start us, length us, event | category | flops | bytes accessed | tf_op | source)
XLA Modules:
  0.0 144.6 jit_solution(11538110252797392846)
XLA Ops:
  0.6 7.3 %all-to-all-start = ((bf16[32,1,8,768]{3,2,1,0:T(8,128)(2,1)}), bf16[32,1,8,768]{3,2,1,0:T(8,128)(2,1)S(1)}, u32[]{:S(2)}, u32[]{:S(2)}) async-start(bf16[32,1,8,768]{3,2,1,0:T(8,128)(2,1)} %bitcast.50), calls=%async_computation | async-start | bytes 786432 | tf_op jit(solution)/shard_map/all_to_all | solution.py:244
  8.0 1.3 reshape.810.gain_ref
  9.4 12.0 %all-to-all-done = bf16[32,1,8,768]{3,2,1,0:T(8,128)(2,1)S(1)} async-done(((bf16[32,1,8,768]{3,2,1,0:T(8,128)(2,1)}), bf16[32,1,8,768]{3,2,1,0:T(8,128)(2,1)S(1)}, u32[]{:S(2)}, u32[]{:S(2)}) %all-to-all-start) | async-done | bytes 393248 | tf_op jit(solution)/shard_map/all_to_all | solution.py:244
  21.4 2.6 %all-to-all-start.2 = ((bf16[32,1,8,768]{3,2,1,0:T(8,128)(2,1)}), bf16[32,1,8,768]{3,2,1,0:T(8,128)(2,1)S(1)}, u32[]{:S(2)}, u32[]{:S(2)}) async-start(bf16[32,1,8,768]{3,2,1,0:T(8,128)(2,1)} %bitcast.51), calls=%async_computation.2 | async-start | bytes 786432 | tf_op jit(solution)/shard_map/all_to_all | solution.py:244
  24.6 1.0 fusion.15.bias_ref
  25.6 12.2 %shard_map.92 = (bf16[768,256]{1,0:T(8,128)(2,1)}, bf16[256,768]{1,0:T(8,128)(2,1)}, bf16[768,256]{1,0:T(8,128)(2,1)}, bf16[256,768]{1,0:T(8,128)(2,1)}, f32[12,...) custom-call(bf16[256,768]{1,0:T(8,128)(2,1)} %bitcast.46, f32[1,768]{1,0:T(1,128)} %reshape.810.gain_ref, ...), custom_call_target="tpu_custom_call" | custom-call | tf_op jit(solution)/shard_map/pallas_call | solution.py:279
  37.8 0.8 copy-done.3
  38.6 10.7 %shard_map.93 = (bf16[256,2304]{1,0:T(8,128)(2,1)}, bf16[4,256,576]{2,1,0:T(8,128)(2,1)}, bf16[4,256,192]{2,1,0:T(8,128)(2,1)}) custom-call(bf16[256,768]{1,0:T(8,128)(2,1)} %bitcast.44, bf16[768,768]{1,0:T(8,128)(2,1)} %wout_ref.3, bf16[256,768]{1,0:T(8,128)(2,1)} %get-tuple-element.20.q_ref, bf16[768,256]{1,0:T(8,128)(2,1)} %get-tuple-element.21.kt_ref, ...), custom_call_target="tpu_custom_call" | custom-call | tf_op jit(solution)/shard_map/pallas_call | solution.py:294
  49.3 7.8 %shard_map.95 = bf16[16,48,1536]{2,1,0:T(8,128)(2,1)} custom-call(s32[16,2]{1,0:T(8,128)} %broadcast_select_fusion.table, bf16[8,96,256]{2,1,0:T(8,128)(2,1)} %bitcast.32, bf16[8,96,256]{2,1,0:T(8,128)(2,1)} %bitcast.38, bf16[4,256,576]{2,1,0:T(8,128)(2,1)} %get-tuple-element.28.db_ref, bf16[4,256,192]{2,1,0:T(8,128)(2,1)} %get-tuple-element.29.cb_ref), custom_call_target="tpu_custom_call" | custom-call | tf_op jit(solution)/shard_map/pallas_call | solution.py:213
  57.9 3.9 %collective-permute-done.rest_0_ = bf16[16,48,1536]{2,1,0:T(8,128)(2,1)S(1)} collective-permute-done((bf16[16,48,1536]{2,1,0:T(8,128)(2,1)}, bf16[16,48,1536]{2,1,0:T(8,128)(2,1)S(1)}, u32[]{:S(2)}, u32[]{:S(2)}) %collective-permute-start) | collective-permute-done | bytes 2359328 | tf_op jit(solution)/shard_map/ppermute | solution.py:233
  61.8 1.4 copy-done
  63.2 5.9 %shard_map.96 = bf16[8,48,1536]{2,1,0:T(8,128)(2,1)} custom-call(s32[8,3]{1,0:T(8,128)} %add_select_fusion.2.table, bf16[8,96,256]{2,1,0:T(8,128)(2,1)} %bitcast.33, bf16[8,96,256]{2,1,0:T(8,128)(2,1)} %bitcast.39, bf16[4,256,576]{2,1,0:T(8,128)(2,1)} %get-tuple-element.28.db_ref, bf16[4,256,192]{2,1,0:T(8,128)(2,1)} %get-tuple-element.29.cb_ref, ...), custom_call_target="tpu_custom_call" | custom-call | tf_op jit(solution)/shard_map/pallas_call | solution.py:213
  69.1 1.6 %collective-permute-start.1 = (bf16[8,48,1536]{2,1,0:T(8,128)(2,1)}, bf16[8,48,1536]{2,1,0:T(8,128)(2,1)S(1)}, u32[]{:S(2)}, u32[]{:S(2)}) collective-permute-start(bf16[8,48,1536]{2,1,0:T(8,128)(2,1)} %shard_map.96), channel_id=1, source_target_pairs={{0,8},{1,17},{2,10},{3,19},{4,12},{5,21},{6,14},{7,23},{8,0},{9,25... | collective-permute-start | bytes 3538952 | tf_op jit(solution)/shard_map/ppermute | solution.py:233
  70.8 4.8 %shard_map.94 = (bf16[256,768]{1,0:T(8,128)(2,1)}, f32[1,768]{1,0:T(1,128)}) custom-call(bf16[256,768]{1,0:T(8,128)(2,1)} %bitcast.47, bf16[256,768]{1,0:T(8,128)(2,1)} %bitcast.45, f32[1,768]{1,0:T(1,128)} %reshape.810.gain_ref, bf16[256,2304]{1,0:T(8,128)(2,1)} %get-tuple-element.24.dqkv_ref, bf16[768,2304]{1,0:T(8,128)(2,1)} %wqkv_ref.3), custom_call_target="tpu_custom_call" | custom-call | tf_op jit(solution)/shard_map/pallas_call | solution.py:304
  77.0 4.8 %all-to-all-start.4 = ((f32[32,1,96]{2,1,0:T(1,128)}), f32[32,1,96]{2,1,0:T(1,128)S(1)}, u32[]{:S(2)}, u32[]{:S(2)}) async-start(f32[32,1,96]{2,1,0:T(1,128)} %bitcast.29), calls=%async_computation.4 | async-start | bytes 32768 | tf_op jit(solution)/shard_map/all_to_all | solution.py:311
  81.8 7.1 %all-to-all-done.4 = f32[32,1,96]{2,1,0:T(1,128)S(1)} async-done(((f32[32,1,96]{2,1,0:T(1,128)}), f32[32,1,96]{2,1,0:T(1,128)S(1)}, u32[]{:S(2)}, u32[]{:S(2)}) %all-to-all-start.4) | async-done | bytes 12320 | tf_op jit(solution)/shard_map/all_to_all | solution.py:311
  88.8 2.8 %all-to-all-start.1 = ((bf16[32,1,8,768]{3,2,1,0:T(8,128)(2,1)}), bf16[32,1,8,768]{3,2,1,0:T(8,128)(2,1)S(1)}, u32[]{:S(2)}, u32[]{:S(2)}) async-start(bf16[32,1,8,768]{3,2,1,0:T(8,128)(2,1)} %bitcast.3), calls=%async_computation.1 | async-start | bytes 786432 | tf_op jit(solution)/shard_map/all_to_all | solution.py:251
  92.4 1.0 copy-done.1
  93.4 4.8 %shard_map.97 = bf16[4,48,1536]{2,1,0:T(8,128)(2,1)} custom-call(s32[4,4]{1,0:T(4,128)} %add_select_fusion.3.table, bf16[8,96,256]{2,1,0:T(8,128)(2,1)} %bitcast.34, bf16[8,96,256]{2,1,0:T(8,128)(2,1)} %bitcast.40, bf16[4,256,576]{2,1,0:T(8,128)(2,1)} %get-tuple-element.28.db_ref, bf16[4,256,192]{2,1,0:T(8,128)(2,1)} %get-tuple-element.29.cb_ref, ...), custom_call_target="tpu_custom_call" | custom-call | tf_op jit(solution)/shard_map/pallas_call | solution.py:213
  98.2 1.8 %collective-permute-start.2 = (bf16[4,48,1536]{2,1,0:T(8,128)(2,1)}, bf16[4,48,1536]{2,1,0:T(8,128)(2,1)S(1)}, u32[]{:S(2)}, u32[]{:S(2)}) collective-permute-start(bf16[4,48,1536]{2,1,0:T(8,128)(2,1)} %shard_map.97), channel_id=1, source_target_pairs={{0,16},{1,9},{2,18},{3,11},{4,20},{5,13},{6,22},{7,15},{8,24},{9,1... | collective-permute-start | bytes 1769480 | tf_op jit(solution)/shard_map/ppermute | solution.py:233
  100.1 4.9 %all-to-all-done.1 = bf16[32,1,8,768]{3,2,1,0:T(8,128)(2,1)S(1)} async-done(((bf16[32,1,8,768]{3,2,1,0:T(8,128)(2,1)}), bf16[32,1,8,768]{3,2,1,0:T(8,128)(2,1)S(1)}, u32[]{:S(2)}, u32[]{:S(2)}) %all-to-all-start.1) | async-done | bytes 393248 | tf_op jit(solution)/shard_map/all_to_all | solution.py:251
  105.1 2.6 %all-to-all-start.3 = ((bf16[32,1,8,768]{3,2,1,0:T(8,128)(2,1)}), bf16[32,1,8,768]{3,2,1,0:T(8,128)(2,1)S(1)}, u32[]{:S(2)}, u32[]{:S(2)}) async-start(bf16[32,1,8,768]{3,2,1,0:T(8,128)(2,1)} %bitcast.8), calls=%async_computation.3 | async-start | bytes 786432 | tf_op jit(solution)/shard_map/all_to_all | solution.py:251
  109.0 0.8 copy-done.2
  109.8 4.2 %shard_map.98 = bf16[2,48,1536]{2,1,0:T(8,128)(2,1)} custom-call(s32[2,5]{1,0:T(2,128)} %broadcast_select_fusion.2.table, bf16[8,96,256]{2,1,0:T(8,128)(2,1)} %bitcast.35, bf16[8,96,256]{2,1,0:T(8,128)(2,1)} %bitcast.41, bf16[4,256,576]{2,1,0:T(8,128)(2,1)} %get-tuple-element.28.db_ref, bf16[4,256,192]{2,1,0:T(8,128)(2,1)} %get-tuple-element.29.cb_ref, ...), custom_call_target="tpu_custom_call" | custom-call | tf_op jit(solution)/shard_map/pallas_call | solution.py:213
  114.0 1.6 %collective-permute-start.3 = (bf16[2,48,1536]{2,1,0:T(8,128)(2,1)}, bf16[2,48,1536]{2,1,0:T(8,128)(2,1)S(1)}, u32[]{:S(2)}, u32[]{:S(2)}) collective-permute-start(bf16[2,48,1536]{2,1,0:T(8,128)(2,1)} %shard_map.98), channel_id=1, source_target_pairs={{0,2},{1,3},{2,0},{3,1},{4,6},{5,7},{6,4},{7,5},{8,10},{9,11},{10,... | collective-permute-start | bytes 884744 | tf_op jit(solution)/shard_map/ppermute | solution.py:233
  117.0 7.6 %collective-permute-done.3.rest_3_ = bf16[2,48,1536]{2,1,0:T(8,128)(2,1)S(1)} collective-permute-done((bf16[2,48,1536]{2,1,0:T(8,128)(2,1)}, bf16[2,48,1536]{2,1,0:T(8,128)(2,1)S(1)}, u32[]{:S(2)}, u32[]{:S(2)}) %collective-permute-start.3) | collective-permute-done | bytes 294944 | tf_op jit(solution)/shard_map/ppermute | solution.py:233
  125.3 3.9 %shard_map.99 = bf16[1,48,1536]{2,1,0:T(8,128)(2,1)} custom-call(s32[1,6]{1,0:T(1,128)} %broadcast_select_fusion.1.table, bf16[8,96,256]{2,1,0:T(8,128)(2,1)} %bitcast.36, bf16[8,96,256]{2,1,0:T(8,128)(2,1)} %bitcast.42, bf16[4,256,576]{2,1,0:T(8,128)(2,1)} %get-tuple-element.28.db_ref, bf16[4,256,192]{2,1,0:T(8,128)(2,1)} %get-tuple-element.29.cb_ref, ...), custom_call_target="tpu_custom_call" | custom-call | tf_op jit(solution)/shard_map/pallas_call | solution.py:213
  129.2 1.0 collective-permute-start.4
  130.7 7.6 %collective-permute-done.4.rest_4_ = bf16[1,48,1536]{2,1,0:T(8,128)(2,1)S(1)} collective-permute-done((bf16[1,48,1536]{2,1,0:T(8,128)(2,1)}, bf16[1,48,1536]{2,1,0:T(8,128)(2,1)S(1)}, u32[]{:S(2)}, u32[]{:S(2)}) %collective-permute-start.4) | collective-permute-done | bytes 147488 | tf_op jit(solution)/shard_map/ppermute | solution.py:233
  139.0 4.1 %shard_map.100 = (f32[96,576]{1,0:T(8,128)}, f32[96,192]{1,0:T(8,128)}) custom-call(s32[1,7]{1,0:T(1,128)} %broadcast_select_fusion.3.table, bf16[8,96,256]{2,1,0:T(8,128)(2,1)} %bitcast.37, bf16[8,96,256]{2,1,0:T(8,128)(2,1)} %bitcast.43, bf16[4,256,576]{2,1,0:T(8,128)(2,1)} %get-tuple-element.28.db_ref, bf16[4,256,192]{2,1,0:T(8,128)(2,1)} %get-tuple-element.29.cb_ref, ...), custom_call_target="tpu_custom_call" | custom-call | tf_op jit(solution)/shard_map/pallas_call | solution.py:213
  143.1 0.7 copy.16
  143.9 0.7 copy.17
  (50 shorter events, 8.5 us)
Async XLA Ops:
  0.6 20.8 %all-to-all-start = ((bf16[32,1,8,768]{3,2,1,0:T(8,128)(2,1)}), bf16[32,1,8,768]{3,2,1,0:T(8,128)(2,1)S(1)}, u32[]{:S(2)}, u32[]{:S(2)}) async-start(bf16[32,1,8,768]{3,2,1,0:T(8,128)(2,1)} %bitcast.50), calls=%async_computation | async-start | bytes 786432 | tf_op jit(solution)/shard_map/all_to_all | solution.py:244
  21.4 4.2 %copy-start.4 = (bf16[32,1,8,768]{3,2,1,0:T(8,128)(2,1)}, bf16[32,1,8,768]{3,2,1,0:T(8,128)(2,1)S(1)}, u32[]{:S(2)}) copy-start(bf16[32,1,8,768]{3,2,1,0:T(8,128)(2,1)S(1)} %all-to-all-done) | copy-start | bytes 1179652
  21.4 16.4 %all-to-all-start.2 = ((bf16[32,1,8,768]{3,2,1,0:T(8,128)(2,1)}), bf16[32,1,8,768]{3,2,1,0:T(8,128)(2,1)S(1)}, u32[]{:S(2)}, u32[]{:S(2)}) async-start(bf16[32,1,8,768]{3,2,1,0:T(8,128)(2,1)} %bitcast.51), calls=%async_computation.2 | async-start | bytes 786432 | tf_op jit(solution)/shard_map/all_to_all | solution.py:244
  37.8 0.8 copy-start.3
  57.1 4.7 %collective-permute-start = (bf16[16,48,1536]{2,1,0:T(8,128)(2,1)}, bf16[16,48,1536]{2,1,0:T(8,128)(2,1)S(1)}, u32[]{:S(2)}, u32[]{:S(2)}) collective-permute-start(bf16[16,48,1536]{2,1,0:T(8,128)(2,1)} %shard_map.95), channel_id=1, source_target_pairs={{0,1},{1,0},{2,3},{3,2},{4,5},{5,4},{6,7},{7,6},{8,9},{9,8},{10,11... | collective-permute-start | bytes 7077896 | tf_op jit(solution)/shard_map/ppermute | solution.py:233
  61.8 1.4 copy-start
  69.1 23.2 %collective-permute-start.1 = (bf16[8,48,1536]{2,1,0:T(8,128)(2,1)}, bf16[8,48,1536]{2,1,0:T(8,128)(2,1)S(1)}, u32[]{:S(2)}, u32[]{:S(2)}) collective-permute-start(bf16[8,48,1536]{2,1,0:T(8,128)(2,1)} %shard_map.96), channel_id=1, source_target_pairs={{0,8},{1,17},{2,10},{3,19},{4,12},{5,21},{6,14},{7,23},{8,0},{9,25... | collective-permute-start | bytes 3538952 | tf_op jit(solution)/shard_map/ppermute | solution.py:233
  77.0 11.9 %all-to-all-start.4 = ((f32[32,1,96]{2,1,0:T(1,128)}), f32[32,1,96]{2,1,0:T(1,128)S(1)}, u32[]{:S(2)}, u32[]{:S(2)}) async-start(f32[32,1,96]{2,1,0:T(1,128)} %bitcast.29), calls=%async_computation.4 | async-start | bytes 32768 | tf_op jit(solution)/shard_map/all_to_all | solution.py:311
  88.8 16.2 %all-to-all-start.1 = ((bf16[32,1,8,768]{3,2,1,0:T(8,128)(2,1)}), bf16[32,1,8,768]{3,2,1,0:T(8,128)(2,1)S(1)}, u32[]{:S(2)}, u32[]{:S(2)}) async-start(bf16[32,1,8,768]{3,2,1,0:T(8,128)(2,1)} %bitcast.3), calls=%async_computation.1 | async-start | bytes 786432 | tf_op jit(solution)/shard_map/all_to_all | solution.py:251
  92.3 1.0 copy-start.1
  98.2 10.8 %collective-permute-start.2 = (bf16[4,48,1536]{2,1,0:T(8,128)(2,1)}, bf16[4,48,1536]{2,1,0:T(8,128)(2,1)S(1)}, u32[]{:S(2)}, u32[]{:S(2)}) collective-permute-start(bf16[4,48,1536]{2,1,0:T(8,128)(2,1)} %shard_map.97), channel_id=1, source_target_pairs={{0,16},{1,9},{2,18},{3,11},{4,20},{5,13},{6,22},{7,15},{8,24},{9,1... | collective-permute-start | bytes 1769480 | tf_op jit(solution)/shard_map/ppermute | solution.py:233
  105.1 25.7 %all-to-all-start.3 = ((bf16[32,1,8,768]{3,2,1,0:T(8,128)(2,1)}), bf16[32,1,8,768]{3,2,1,0:T(8,128)(2,1)S(1)}, u32[]{:S(2)}, u32[]{:S(2)}) async-start(bf16[32,1,8,768]{3,2,1,0:T(8,128)(2,1)} %bitcast.8), calls=%async_computation.3 | async-start | bytes 786432 | tf_op jit(solution)/shard_map/all_to_all | solution.py:251
  109.0 0.8 copy-start.2
  114.0 10.6 %collective-permute-start.3 = (bf16[2,48,1536]{2,1,0:T(8,128)(2,1)}, bf16[2,48,1536]{2,1,0:T(8,128)(2,1)S(1)}, u32[]{:S(2)}, u32[]{:S(2)}) collective-permute-start(bf16[2,48,1536]{2,1,0:T(8,128)(2,1)} %shard_map.98), channel_id=1, source_target_pairs={{0,2},{1,3},{2,0},{3,1},{4,6},{5,7},{6,4},{7,5},{8,10},{9,11},{10,... | collective-permute-start | bytes 884744 | tf_op jit(solution)/shard_map/ppermute | solution.py:233
  124.6 0.7 copy-start.5
  129.2 9.2 %collective-permute-start.4 = (bf16[1,48,1536]{2,1,0:T(8,128)(2,1)}, bf16[1,48,1536]{2,1,0:T(8,128)(2,1)S(1)}, u32[]{:S(2)}, u32[]{:S(2)}) collective-permute-start(bf16[1,48,1536]{2,1,0:T(8,128)(2,1)} %shard_map.99), channel_id=1, source_target_pairs={{0,4},{1,5},{2,6},{3,7},{4,0},{5,1},{6,2},{7,3},{8,12},{9,13},{10,... | collective-permute-start | bytes 442376 | tf_op jit(solution)/shard_map/ppermute | solution.py:233
  138.4 0.6 copy-start.6

commit v2 on v1

v2 whole, which is shorter than its diff:
```python
import functools
import math

import jax
import jax.numpy as jnp
from jax import lax
from jax.experimental import pallas as pl
from jax.experimental.pallas import tpu as pltpu
from jax.sharding import PartitionSpec as P

HEADS = 12
HEAD_DIM = 64
WINDOW = 4
CLIP_MAX = 256
EPSILON = 1e-06
SCALE = HEAD_DIM ** (-0.5)

BF = jnp.bfloat16
F32 = jnp.float32
AXES = ("tm", "inner")
LANES = 128
VMEM_LIMIT = 60 * 1024 * 1024


def mm(a, b):
    return lax.dot_general(a, b, (((1,), (0,)), ((), ())), preferred_element_type=F32)


def mm_t(a, b):
    return lax.dot_general(a, b, (((1,), (1,)), ((), ())), preferred_element_type=F32)


def call(kernel, out_shape, *args, scratch=(), flops=0):
    leaves = jax.tree.leaves(out_shape) + list(args)
    moved = sum(math.prod(a.shape) * a.dtype.itemsize for a in leaves)
    return pl.pallas_call(
        kernel,
        out_shape=out_shape,
        scratch_shapes=scratch,
        compiler_params=pltpu.CompilerParams(vmem_limit_bytes=VMEM_LIMIT),
        cost_estimate=pl.CostEstimate(flops=flops, bytes_accessed=moved, transcendentals=0),
    )(*args)


def row_stats(x):
    center = x - jnp.mean(x, axis=-1, keepdims=True)
    spread = lax.rsqrt(jnp.mean(center * center, axis=-1, keepdims=True) + EPSILON)
    return center * spread, spread


def key_spans(tokens, reach):
    spans = []
    for start in range(0, tokens, LANES):
        low = max(0, start - reach) // 16 * 16
        high = min(tokens, -(-(start + LANES + reach) // 16) * 16)
        spans.append((start, low, high))
    return spans


def split_rows(mine_ref, other_ref, slot, src_ref, core):
    count, rows = mine_ref.shape[1], mine_ref.shape[2]
    for z in range(count):
        mine = src_ref[pl.ds(pl.multiple_of((2 * z + core) * rows, 8), rows), :]
        other = src_ref[pl.ds(pl.multiple_of((2 * z + 1 - core) * rows, 8), rows), :]
        mine_ref[slot, z] = mine.astype(BF)
        other_ref[slot, z] = other.astype(BF)


def forward_kernel(reach, x_ref, gain_ref, wqkv_ref, bias_ref, mine_ref, other_ref, q_ref, kt_ref, v_ref, prob_ref, mixed_ref, n_ref, k_ref, t_ref):
    tokens, width = x_ref.shape
    core = lax.axis_index("inner") & 1
    unit, _ = row_stats(x_ref[...].astype(F32))
    normed = unit * gain_ref[...]
    n_ref[...] = normed.astype(BF)
    t_ref[...] = normed.T
    split_rows(mine_ref, other_ref, 0, t_ref, core)
    step = 256

    def project(i, carry):
        cols = pl.ds(pl.multiple_of(i * step, step), step)
        k_cols = pl.ds(pl.multiple_of(width + i * step, step), step)
        v_cols = pl.ds(pl.multiple_of(2 * width + i * step, step), step)
        q_ref[:, cols] = (mm(n_ref[...], wqkv_ref[:, cols]) * SCALE).astype(BF)
        k_ref[:, cols] = mm(n_ref[...], wqkv_ref[:, k_cols]).astype(BF)
        v_ref[:, cols] = mm(n_ref[...], wqkv_ref[:, v_cols]).astype(BF)
        return carry

    lax.fori_loop(0, width // step, project, 0)

    def pair(i, carry):
        cols = pl.ds(pl.multiple_of(i * 128, 128), 128)
        q2, k2, v2 = q_ref[:, cols], k_ref[:, cols], v_ref[:, cols]
        kt_ref[cols, :] = (k2.astype(F32).T * SCALE).astype(BF)
        v2t = v2.astype(F32).T.astype(BF)
        for half in range(2):
            span = slice(half * 64, half * 64 + 64)
            for b, (start, low, high) in enumerate(key_spans(tokens, reach)):
                block = slice(start, start + LANES)
                scores = mm_t(k2[low:high, span], q2[block, span]) + bias_ref[low:high, block]
                grown = jnp.exp(scores - jnp.max(scores, axis=0, keepdims=True))
                probs = grown * (1.0 / jnp.sum(grown, axis=0, keepdims=True))
                prob_ref[2 * i + half, b, : high - low] = probs
                rows = pl.ds(pl.multiple_of(i * 128 + half * 64, 64), 64)
                mixt = mm(v2t[span, low:high], probs.astype(BF))
                t_ref[rows, block] = mixt
        return carry

    lax.fori_loop(0, HEADS // 2, pair, 0)
    mixed_ref[...] = t_ref[...].T.astype(BF)
    split_rows(mine_ref, other_ref, 1, t_ref, core)


def out_kernel(frames_ref, mixed_ref, wout_ref, out_ref):
    out_ref[...] = (frames_ref[...].astype(F32) + mm(mixed_ref[...], wout_ref[...])).astype(BF)


def put_blocks(dst_ref, src):
    parts, _, wide = dst_ref.shape
    for j in range(parts):
        dst_ref[j] = src[:, j * wide : (j + 1) * wide]


def blocks_kernel(cot_ref, other_ref, out_ref, out_other_ref):
    put_blocks(out_ref, cot_ref[...])
    put_blocks(out_other_ref, other_ref[...])


def backward_kernel(reach, cot_ref, wout_ref, q_ref, kt_ref, v_ref, prob_ref, dqkv_ref, dblk_ref, gm_ref, dqt_ref):
    tokens, width = cot_ref.shape
    gm_ref[...] = mm_t(cot_ref[...], wout_ref[...]).astype(BF)
    spans = key_spans(tokens, reach)

    def widen(parts):
        cols = []
        for part, (_, low, high) in zip(parts, spans):
            rows = [jnp.zeros((low, LANES), BF)] if low else []
            rows += [part]
            rows += [jnp.zeros((tokens - high, LANES), BF)] if high < tokens else []
            cols.append(jnp.concatenate(rows, 0) if len(rows) > 1 else part)
        return jnp.concatenate(cols, 1) if len(cols) > 1 else cols[0]

    def pair(i, carry):
        cols = pl.ds(pl.multiple_of(i * 128, 128), 128)
        q2, g2, v2, kt2 = q_ref[:, cols], gm_ref[:, cols], v_ref[:, cols], kt_ref[cols, :]
        dks, dvs = [], []
        for half in range(2):
            span = slice(half * 64, half * 64 + 64)
            weights, grads = [], []
            for b, (start, low, high) in enumerate(spans):
                block = slice(start, start + LANES)
                probs = prob_ref[2 * i + half, b, : high - low]
                dots = mm_t(v2[low:high, span], g2[block, span])
                centre = jnp.sum(probs * dots, axis=0, keepdims=True)
                sgrad = (probs * (dots - centre)).astype(BF)
                rows = pl.ds(pl.multiple_of(i * 128 + half * 64, 64), 64)
                dqt_ref[rows, block] = mm(kt2[span, low:high], sgrad)
                weights.append(probs.astype(BF))
                grads.append(sgrad)
            dks.append(mm(widen(grads), q2[:, span]))
            dvs.append(mm(widen(weights), g2[:, span]))
        dqkv_ref[:, pl.ds(pl.multiple_of(width + i * 128, 128), 128)] = jnp.concatenate(dks, 1).astype(BF)
        dqkv_ref[:, pl.ds(pl.multiple_of(2 * width + i * 128, 128), 128)] = jnp.concatenate(dvs, 1).astype(BF)
        return carry

    lax.fori_loop(0, HEADS // 2, pair, 0)
    dqkv_ref[:, :width] = dqt_ref[...].T.astype(BF)
    put_blocks(dblk_ref, dqkv_ref[...])


def norm_kernel(x_ref, cot_ref, gain_ref, dqkv_ref, wqkv_ref, fgrad_ref, gpart_ref):
    unit, spread = row_stats(x_ref[...].astype(F32))
    ngrad = mm_t(dqkv_ref[...], wqkv_ref[...])
    gpart_ref[...] = jnp.sum(ngrad * unit, axis=0, keepdims=True)
    scaled = ngrad * gain_ref[...]
    mean_one = jnp.mean(scaled, axis=-1, keepdims=True)
    second = jnp.mean(scaled * unit, axis=-1, keepdims=True)
    fgrad_ref[...] = (cot_ref[...].astype(F32) + spread * (scaled - mean_one - unit * second)).astype(BF)


def squeeze_bits(value, bits):
    for b in sorted(bits, reverse=True):
        value = (value >> (b + 1) << b) | (value & ((1 << b) - 1))
    return value


def spread_bits(value, bits):
    for b in sorted(bits):
        value = (value >> b << (b + 1)) | (value & ((1 << b) - 1))
    return value


def bit_orders(runs):
    bits = list(range(runs.bit_length() - 1))
    return bits, bits[1:] + bits[:1]


def place_of(runs, stage, n, send):
    me = lax.axis_index("tm")
    found = []
    for order in bit_orders(runs):
        past, bit = order[:stage], order[stage]
        run = spread_bits(n, past + [bit])
        for b in past:
            run = run | (me & (1 << b))
        run = run | ((me ^ (1 << bit) if send else me) & (1 << bit))
        found.append((run, squeeze_bits(run, past)))
    first = lax.axis_index("inner") & 1 == 0
    return jnp.where(first, found[0][0], found[1][0]), jnp.where(first, found[0][1], found[1][1])


def exchange(value, runs, inner, stage):
    perm = []
    for t in range(runs):
        for i in range(inner):
            t2 = t ^ (1 << bit_orders(runs)[i & 1][stage])
            perm.append((t * inner + i, t2 * inner + i))
    return lax.ppermute(value, AXES, perm)


def to_partner(value, inner):
    return lax.ppermute(value, "inner", [(i, i ^ 1) for i in range(inner)])


def product_kernel(runs, slot, send, mine_ref, other_ref, d_ref, d_other_ref, out_ref):
    count, rows, tokens = mine_ref.shape[1:]
    half = rows // 2
    left = mine_ref[slot].reshape(count * rows, tokens)
    right = other_ref[slot].reshape(count * rows, tokens)
    for n in range(out_ref.shape[0]):
        run, _ = place_of(runs, 0, n, send)
        total = mm(left, d_ref[run]) + mm(right, d_other_ref[run])
        for z in range(count):
            block = total[z * rows : (z + 1) * rows]
            out_ref[n, z] = jnp.concatenate([block[:half], block[half:]], 1).astype(out_ref.dtype)


def stage_kernel(runs, stage, send, keep_ref, got_ref, out_ref):
    for n in range(out_ref.shape[0]):
        _, place = place_of(runs, stage, n, send)
        out_ref[n] = (keep_ref[place] + got_ref[place].astype(F32)).astype(out_ref.dtype)


def start_reduce(slot, mine, other, d, d_other, runs):
    count, rows, tokens = mine.shape[1:]
    folded = (runs // 2, count, rows // 2, 2 * d.shape[2])
    flops = 2 * count * rows * 2 * tokens * d.shape[2] * (runs // 2)
    send = call(functools.partial(product_kernel, runs, slot, True), jax.ShapeDtypeStruct(folded, BF), mine, other, d, d_other, flops=flops)
    keep = call(functools.partial(product_kernel, runs, slot, False), jax.ShapeDtypeStruct(folded, F32), mine, other, d, d_other, flops=flops)
    return send, keep


def reduce_runs(send, keep, runs, inner):
    got = exchange(send, runs, inner, 0)
    for stage in range(1, runs.bit_length() - 1):
        shape = (keep.shape[0] // 2,) + keep.shape[1:]
        send = call(functools.partial(stage_kernel, runs, stage, True), jax.ShapeDtypeStruct(shape, BF), keep, got)
        keep = call(functools.partial(stage_kernel, runs, stage, False), jax.ShapeDtypeStruct(shape, F32), keep, got)
        got = exchange(send, runs, inner, stage)
    return keep, got


def rows_kernel(keep_ref, got_ref, keep_o_ref, got_o_ref, own_ref, *send_refs):
    count = keep_ref.shape[1]
    me = lax.axis_index("inner") >> 1

    def total(z):
        left = keep_ref[0, z] + got_ref[0, z].astype(F32)
        right = keep_o_ref[0, z] + got_o_ref[0, z].astype(F32)
        return jnp.concatenate([left, right], 1)

    for k, ref in enumerate(send_refs):
        ref[...] = total(lax.rem(me + k + 1, count)).astype(BF)
    own_ref[...] = total(me)


def last_kernel(inv_root, own_ref, *rest):
    got, (q_ref, o_ref) = rest[:-2], rest[-2:]
    total = own_ref[...]
    for ref in got:
        total = total + ref[...].astype(F32)
    total = total * inv_root
    half = q_ref.shape[0] // 2
    wide, thin = q_ref.shape[1], o_ref.shape[1]
    q_ref[:half] = total[:, :wide]
    q_ref[half:] = total[:, wide : 2 * wide]
    o_ref[:half] = total[:, 2 * wide : 2 * wide + thin]
    o_ref[half:] = total[:, 2 * wide + thin :]


def reduce_rows(parts_q, parts_o, inner, inv_root):
    _, count, half, wide = parts_q[0].shape
    thin = parts_o[0].shape[3]
    block = (half, wide + thin)
    sds = jax.ShapeDtypeStruct
    own, *sends = call(rows_kernel, (sds(block, F32),) + (sds(block, BF),) * (count - 1), *parts_q, *parts_o)
    got = []
    for k, send in enumerate(sends):
        got.append(lax.ppermute(send, "inner", [(i, (i + 2 * (k + 1)) % inner) for i in range(inner)]))
    out = (sds((2 * half, wide // 2), F32), sds((2 * half, thin // 2), F32))
    return call(functools.partial(last_kernel, inv_root), out, own, *got)


def to_tubes(rows, count):
    held, patches, width = rows.shape
    parts = jnp.moveaxis(rows.reshape(held, count, patches // count, width), 1, 0)
    parts = lax.all_to_all(parts, AXES, split_axis=0, concat_axis=0, tiled=True)
    return parts.reshape(-1, width)


def to_frames(tubes, count, held, patches):
    width = tubes.shape[1]
    parts = tubes.reshape(count, held, patches // count, width)
    parts = lax.all_to_all(parts, AXES, split_axis=0, concat_axis=0, tiled=True)
    return jnp.moveaxis(parts, 0, 1).reshape(held, patches, width)


def window_bias(all_frames, patches, clip_len):
    tokens = all_frames * patches
    key = lax.broadcasted_iota(jnp.int32, (tokens, tokens), 0)
    query = lax.broadcasted_iota(jnp.int32, (tokens, tokens), 1)
    key_f, query_f = key // patches, query // patches
    inside = (key % patches == query % patches) & (abs(key_f - query_f) <= WINDOW)
    inside = inside & (key_f // clip_len == query_f // clip_len)
    return jnp.where(inside, 0.0, -1e30).astype(F32)


def shards(frames, norm_gain, w_qkv, w_out, cotangent):
    held, patches, width = frames.shape
    runs, inner = lax.axis_size("tm"), lax.axis_size("inner")
    count = runs * inner
    all_frames = held * count
    clip_len = min(CLIP_MAX, all_frames)
    inv_root = 1.0 / math.sqrt(all_frames * patches)
    tokens = all_frames * patches // count
    reach = WINDOW * (patches // count)
    gain = norm_gain.reshape(1, width)
    bias = window_bias(all_frames, patches // count, clip_len)
    spans = key_spans(tokens, reach)
    longest = max(high - low for _, low, high in spans)
    sds = jax.ShapeDtypeStruct
    vmem = pltpu.VMEM

    x = to_tubes(frames, count)
    cot = to_tubes(cotangent, count)
    halves = sds((2, inner // 2, width // inner, tokens), BF)
    mine, other, q, kt, v, prob, mixed = call(
        functools.partial(forward_kernel, reach),
        (
            halves,
            halves,
            sds((tokens, width), BF),
            sds((width, tokens), BF),
            sds((tokens, width), BF),
            sds((HEADS, len(spans), longest, LANES), F32),
            sds((tokens, width), BF),
        ),
        x,
        gain,
        w_qkv,
        bias,
        scratch=[vmem((tokens, width), BF), vmem((tokens, width), BF), vmem((width, tokens), F32)],
        flops=2 * tokens * width * 4 * width,
    )
    theirs = to_partner(other, inner)
    mixed_back = to_frames(mixed, count, held, patches)
    block_out = call(out_kernel, sds((held * patches, width), BF), frames.reshape(-1, width), mixed_back.reshape(-1, width), w_out, flops=2 * tokens * width * width)
    block_out = block_out.reshape(held, patches, width)

    cblk = sds((runs, tokens, width // runs), BF)
    cblk, cblk_other = call(blocks_kernel, (cblk, cblk), cot, to_partner(cot, inner))
    parts_o = reduce_runs(*start_reduce(1, mine, theirs, cblk, cblk_other, runs), runs, inner)

    dqkv, dblk = call(
        functools.partial(backward_kernel, reach),
        (sds((tokens, 3 * width), BF), sds((runs, tokens, 3 * width // runs), BF)),
        cot,
        w_out,
        q,
        kt,
        v,
        prob,
        scratch=[vmem((tokens, width), BF), vmem((width, tokens), F32)],
        flops=2 * tokens * width * 4 * width,
    )
    dblk_other = to_partner(dblk, inner)
    fgrad, gpart = call(
        norm_kernel,
        (sds((tokens, width), BF), sds((1, width), F32)),
        x,
        cot,
        gain,
        dqkv,
        w_qkv,
        flops=2 * tokens * width * 3 * width,
    )
    frames_grad = to_frames(fgrad, count, held, patches)
    parts_q = reduce_runs(*start_reduce(0, mine, theirs, dblk, dblk_other, runs), runs, inner)
    qkv_grad, out_grad = reduce_rows(parts_q, parts_o, inner, inv_root)
    shares = jnp.broadcast_to(gpart.reshape(1, inner, width // inner), (runs, inner, width // inner))
    shares = lax.all_to_all(shares.reshape(count, 1, -1), AXES, split_axis=0, concat_axis=0, tiled=True)
    gain_grad = jnp.sum(shares, axis=(0, 1)) * inv_root
    return block_out, frames_grad, qkv_grad, out_grad, gain_grad


def solution(mesh):
    in_specs = (P(AXES, None, None), P(), P(), P(), P(AXES, None, None))
    out_specs = (P(AXES, None, None), P(AXES, None, None), P("inner", "tm"), P("inner", "tm"), P("inner"))
    return jax.shard_map(shards, mesh=mesh, in_specs=in_specs, out_specs=out_specs, check_vma=False)
```

time: 145 us -> 147 us (1.014)
  blocking collectives: 0 us -> 32.6 us
  waiting for transfers between devices: 43.6 us -> 19.6 us
  starting transfers between devices: 26.2 us -> 19.3 us
  other arithmetic: 6 us -> 2.25 us
  local copies, waits for them, and re-layouts: 9.62 us -> 11.3 us
    all_to_all x0 -> x2, blocking collectives: none -> 32.6 us  [the longest x1 20.9 us: to_tubes(): parts = lax.all_to_all(parts, AXES, split_axis=0, concat_axis=0, tiled=True)]
    ppermute x5 -> x10, waiting for transfers between devices: 19.7 us -> 6.4 us  [the longest x3 3.85 us: reduce_rows(): lax.ppermute(send, 'inner', [(i, (i + 2 * (k + 1)) % inner) for i in rang...]
    all_to_all x2 -> x1, waiting for transfers between devices: 12 us -> 0.01 us  [to_tubes(): parts = lax.all_to_all(parts, AXES, split_axis=0, concat_axis=0, tiled=True)]
    all_to_all x2, waiting for transfers between devices: 4.93 us -> 13.2 us  [to_frames(): parts = lax.all_to_all(parts, AXES, split_axis=0, concat_axis=0, tiled=True)]
    all_to_all x2 -> x1, starting transfers between devices: 9.93 us -> 2.6 us  [to_tubes(): parts = lax.all_to_all(parts, AXES, split_axis=0, concat_axis=0, tiled=True)]
    all_to_all x1 -> x0, waiting for transfers between devices: 7.07 us -> none  [shards(): lax.all_to_all(shares.reshape(count, 1, -1), AXES, split_axis=0, concat_a...]
    ppermute x5 -> x10, starting transfers between devices: 6.13 us -> 11.5 us  [the longest x3 5.42 us: reduce_rows(): lax.ppermute(send, 'inner', [(i, (i + 2 * (k + 1)) % inner) for i in rang...]
    all_to_all x1 -> x0, starting transfers between devices: 4.76 us -> none  [shards(): lax.all_to_all(shares.reshape(count, 1, -1), AXES, split_axis=0, concat_a...]
  transfers between devices with their start and end apart: 10 -> 13, of which waited for: 7 -> 4; matrix products, arithmetic and copies ran while one was open for 6% -> 3% of each run, Pallas kernels for 21% -> 30%
where the time goes in v2:
time: 147 us; the launch traced here: 146 us
  Pallas kernels  59.8 us (41%)
  blocking collectives  32.6 us (22%)
  waiting for transfers between devices  19.6 us (13%)
  starting transfers between devices  19.3 us (13%)
  local copies, waits for them, and re-layouts  11.3 us (8%)
  other arithmetic  2.25 us (2%)
    pallas_call x15, Pallas kernels, call(): pl.pallas_call(kernel, out_shape=out_shape, scratch_shapes=scratch, compi...  59.8 us
    all_to_all x1, blocking collectives, to_tubes(): parts = lax.all_to_all(parts, AXES, split_axis=0, concat_axis=0, tiled=True)  20.9 us
    all_to_all x2, waiting for transfers between devices, to_frames(): parts = lax.all_to_all(parts, AXES, split_axis=0, concat_axis=0, tiled=True)  13.2 us
    all_to_all x1, blocking collectives, shards(): lax.all_to_all(shares.reshape(count, 1, -1), AXES, split_axis=0, concat_a...  11.7 us
    unnamed x29, local copies, waits for them, and re-layouts  7.57 us
    ppermute x3, starting transfers between devices, reduce_rows(): lax.ppermute(send, 'inner', [(i, (i + 2 * (k + 1)) % inner) for i in rang...  5.42 us
    ppermute x4, starting transfers between devices, exchange(): return lax.ppermute(value, AXES, perm)  5.29 us
    all_to_all x2, starting transfers between devices, to_frames(): parts = lax.all_to_all(parts, AXES, split_axis=0, concat_axis=0, tiled=True)  5.19 us
  transfers between devices with their start and end apart: 13, of which 4 were waited for; matrix products, arithmetic and copies ran while one was open for 3% of the time, Pallas kernels for 30%

profile of v2, /device:TPU:0, one launch (start us, length us, event | category | flops | bytes accessed | tf_op | source)
XLA Modules:
  0.0 145.6 jit_solution(14436741536249251547)
XLA Ops:
  0.6 20.9 %all_to_all.25 = bf16[32,1,8,768]{3,2,1,0:T(8,128)(2,1)} all-to-all(bf16[32,1,8,768]{3,2,1,0:T(8,128)(2,1)} %bitcast.19), channel_id=1, replica_groups=mesh['tm'=4,'inner'=8] {'tm','inner'}, dimensions={0} | all-to-all | bytes 786432 | tf_op jit(solution)/shard_map/all_to_all | solution.py:306
  21.5 2.6 %all-to-all-start.2 = ((bf16[32,1,8,768]{3,2,1,0:T(8,128)(2,1)}), bf16[32,1,8,768]{3,2,1,0:T(8,128)(2,1)S(1)}, u32[]{:S(2)}, u32[]{:S(2)}) async-start(bf16[32,1,8,768]{3,2,1,0:T(8,128)(2,1)} %bitcast.26), calls=%async_computation.2 | async-start | bytes 786432 | tf_op jit(solution)/shard_map/all_to_all | solution.py:306
  24.7 1.0 fusion.15.bias_ref
  25.7 13.0 %shard_map.92 = (bf16[2,4,96,256]{3,2,1,0:T(8,128)(2,1)}, bf16[2,4,96,256]{3,2,1,0:T(8,128)(2,1)}, bf16[256,768]{1,0:T(8,128)(2,1)}, bf16[768,256]{1,0:T(8,128)(...) custom-call(bf16[256,768]{1,0:T(8,128)(2,1)} %bitcast.23, ...), custom_call_target="tpu_custom_call" | custom-call | flops 1207959552 | bytes 8522752 | tf_op jit(solution)/shard_map/pallas_call | solution.py:36
  39.5 10.5 %shard_map.94 = (bf16[256,2304]{1,0:T(8,128)(2,1)}, bf16[4,256,576]{2,1,0:T(8,128)(2,1)}) custom-call(bf16[256,768]{1,0:T(8,128)(2,1)} %bitcast.15, bf16[768,768]{1,0:T(8,128)(2,1)} %wout_ref.3, bf16[256,768]{1,0:T(8,128)(2,1)} %get-tuple-element.25.q_ref, bf16[768,256]{1,0:T(8,128)(2,1)} %get-tuple-element.26.kt_ref, ...), custom_call_target="tpu_custom_call" | custom-call | flops 1207959552 | bytes 7077888 | tf_op jit(solution)/shard_map/pallas_call | solution.py:36
  50.0 1.6 %copy.12 = bf16[4,256,576]{1,2,0:T(8,128)(2,1)S(1)} copy(bf16[4,256,576]{2,1,0:T(8,128)(2,1)} %get-tuple-element.33.d_ref) | data formatting | bytes 2359296 | tf_op jit(solution)/shard_map/pallas_call | solution.py:36
  52.2 2.3 %collective-permute-done.1 = bf16[4,256,576]{1,2,0:T(8,128)(2,1)S(1)} collective-permute-done((bf16[4,256,576]{1,2,0:T(8,128)(2,1)S(1)}, bf16[4,256,576]{1,2,0:T(8,128)(2,1)S(1)}, u32[]{:S(2)}, u32[]{:S(2)}) %collective-permute-start.1) | collective-permute-done | bytes 1179680 | tf_op jit(solution)/shard_map/ppermute | solution.py:221
  54.5 1.4 copy.13.d_other_ref
  56.7 3.8 %shard_map.97 = bf16[2,4,48,1152]{3,2,1,0:T(8,128)(2,1)} custom-call(bf16[2,4,96,256]{3,2,1,0:T(8,128)(2,1)} %get-tuple-element.31.mine_ref, bf16[2,4,96,256]{3,2,1,0:T(8,128)(2,1)} %copy-done, bf16[4,256,576]{2,1,0:T(8,128)(2,1)} %get-tuple-element.33.d_ref, bf16[4,256,576]{2,1,0:T(8,128)(2,1)} %copy.13.d_other_ref), custom_call_target="tpu_custom_call" | custom-call | flops 452984832 | bytes 4030464 | tf_op jit(solution)/shard_map/pallas_call | solution.py:36
  60.5 1.6 %collective-permute-start.2 = (bf16[2,4,48,1152]{3,2,1,0:T(8,128)(2,1)}, bf16[2,4,48,1152]{3,2,1,0:T(8,128)(2,1)S(1)}, u32[]{:S(2)}, u32[]{:S(2)}) collective-permute-start(bf16[2,4,48,1152]{3,2,1,0:T(8,128)(2,1)} %shard_map.97), channel_id=1, source_target_pairs={{0,8},{1,17},{2,10},{3,19},{4,12},{5,21},{6,14},{7,23},{8,0},{9,25... | collective-permute-start | bytes 2654216 | tf_op jit(solution)/shard_map/ppermute | solution.py:217
  62.1 4.8 %shard_map.95 = (bf16[256,768]{1,0:T(8,128)(2,1)}, f32[1,768]{1,0:T(1,128)}) custom-call(bf16[256,768]{1,0:T(8,128)(2,1)} %bitcast.24, bf16[256,768]{1,0:T(8,128)(2,1)} %bitcast.16, f32[1,768]{1,0:T(1,128)} %reshape.38.gain_ref, bf16[256,2304]{1,0:T(8,128)(2,1)} %get-tuple-element.29.dqkv_ref, bf16[768,2304]{1,0:T(8,128)(2,1)} %wqkv_ref.3), custom_call_target="tpu_custom_call" | custom-call | flops 905969664 | bytes 5904384 | tf_op jit(solution)/shard_map/pallas_call | solution.py:36
  67.7 11.7 %all_to_all.26 = f32[32,1,96]{2,1,0:T(1,128)S(1)} all-to-all(f32[32,1,96]{2,1,0:T(1,128)S(1)} %bitcast.28), channel_id=1, replica_groups=mesh['tm'=4,'inner'=8] {'tm','inner'}, dimensions={0} | all-to-all | bytes 24576 | tf_op jit(solution)/shard_map/all_to_all | solution.py:400
  79.4 2.6 %all-to-all-start.3 = ((bf16[32,1,8,768]{3,2,1,0:T(8,128)(2,1)}), bf16[32,1,8,768]{3,2,1,0:T(8,128)(2,1)S(1)}, u32[]{:S(2)}, u32[]{:S(2)}) async-start(bf16[32,1,8,768]{3,2,1,0:T(8,128)(2,1)} %bitcast.27), calls=%async_computation.3 | async-start | bytes 786432 | tf_op jit(solution)/shard_map/all_to_all | solution.py:313
  82.2 13.2 %all-to-all-done.3 = bf16[32,1,8,768]{3,2,1,0:T(8,128)(2,1)S(1)} async-done(((bf16[32,1,8,768]{3,2,1,0:T(8,128)(2,1)}), bf16[32,1,8,768]{3,2,1,0:T(8,128)(2,1)S(1)}, u32[]{:S(2)}, u32[]{:S(2)}) %all-to-all-start.3) | async-done | bytes 393248 | tf_op jit(solution)/shard_map/all_to_all | solution.py:313
  95.5 2.6 %all-to-all-start.1 = ((bf16[32,1,8,768]{3,2,1,0:T(8,128)(2,1)}), bf16[32,1,8,768]{3,2,1,0:T(8,128)(2,1)S(1)}, u32[]{:S(2)}, u32[]{:S(2)}) async-start(bf16[32,1,8,768]{3,2,1,0:T(8,128)(2,1)} %bitcast.4), calls=%async_computation.1 | async-start | bytes 786432 | tf_op jit(solution)/shard_map/all_to_all | solution.py:313
  98.8 2.3 %shard_map.100 = (bf16[4,256,192]{2,1,0:T(8,128)(2,1)}, bf16[4,256,192]{2,1,0:T(8,128)(2,1)}) custom-call(bf16[256,768]{1,0:T(8,128)(2,1)} %bitcast.17, bf16[256,768]{1,0:T(8,128)(2,1)} %copy-done.7), custom_call_target="tpu_custom_call" | custom-call | bytes 1572864 | tf_op jit(solution)/shard_map/pallas_call | solution.py:36
  101.1 2.6 %shard_map.102 = bf16[2,4,48,384]{3,2,1,0:T(8,128)(2,1)} custom-call(bf16[2,4,96,256]{3,2,1,0:T(8,128)(2,1)} %get-tuple-element.31.mine_ref, bf16[2,4,96,256]{3,2,1,0:T(8,128)(2,1)} %copy-done, bf16[4,256,192]{2,1,0:T(8,128)(2,1)} %get-tuple-element.34.d_ref, bf16[4,256,192]{2,1,0:T(8,128)(2,1)} %get-tuple-element.35.d_other_ref), custom_call_target="tpu_custom_call" | custom-call | flops 150994944 | bytes 1867776 | tf_op jit(solution)/shard_map/pallas_call | solution.py:36
  103.7 1.6 %collective-permute-start.5 = (bf16[2,4,48,384]{3,2,1,0:T(8,128)(2,1)}, bf16[2,4,48,384]{3,2,1,0:T(8,128)(2,1)S(1)}, u32[]{:S(2)}, u32[]{:S(2)}) collective-permute-start(bf16[2,4,48,384]{3,2,1,0:T(8,128)(2,1)} %shard_map.102), channel_id=1, source_target_pairs={{0,8},{1,17},{2,10},{3,19},{4,12},{5,21},{6,14},{7,23},{8,0},{9,25... | collective-permute-start | bytes 884744 | tf_op jit(solution)/shard_map/ppermute | solution.py:217
  105.3 4.1 %shard_map.96.keep_ref = f32[2,4,48,1152]{3,2,1,0:T(8,128)} custom-call(bf16[2,4,96,256]{3,2,1,0:T(8,128)(2,1)} %get-tuple-element.31.mine_ref, bf16[2,4,96,256]{3,2,1,0:T(8,128)(2,1)} %copy-done, bf16[4,256,576]{2,1,0:T(8,128)(2,1)} %get-tuple-element.33.d_ref, bf16[4,256,576]{2,1,0:T(8,128)(2,1)} %copy.13.d_other_ref), custom_call_target="tpu_custom_call" | custom-call | flops 452984832 | bytes 4915200 | tf_op jit(solution)/shard_map/pallas_call | solution.py:36
  110.4 2.6 %shard_map.99 = bf16[1,4,48,1152]{3,2,1,0:T(8,128)(2,1)} custom-call(f32[2,4,48,1152]{3,2,1,0:T(8,128)} %shard_map.96.keep_ref, bf16[2,4,48,1152]{3,2,1,0:T(8,128)(2,1)} %copy-done.3), custom_call_target="tpu_custom_call" | custom-call | bytes 3096576 | tf_op jit(solution)/shard_map/pallas_call | solution.py:36
  113.0 1.5 %collective-permute-start.3 = (bf16[1,4,48,1152]{3,2,1,0:T(8,128)(2,1)}, bf16[1,4,48,1152]{3,2,1,0:T(8,128)(2,1)S(1)}, u32[]{:S(2)}, u32[]{:S(2)}) collective-permute-start(bf16[1,4,48,1152]{3,2,1,0:T(8,128)(2,1)} %shard_map.99), channel_id=1, source_target_pairs={{0,16},{1,9},{2,18},{3,11},{4,20},{5,13},{6,22},{7,15},{8,24},{9,1... | collective-permute-start | bytes 1327112 | tf_op jit(solution)/shard_map/ppermute | solution.py:217
  114.5 2.7 %shard_map.101.keep_ref = f32[2,4,48,384]{3,2,1,0:T(8,128)} custom-call(bf16[2,4,96,256]{3,2,1,0:T(8,128)(2,1)} %get-tuple-element.31.mine_ref, bf16[2,4,96,256]{3,2,1,0:T(8,128)(2,1)} %copy-done, bf16[4,256,192]{2,1,0:T(8,128)(2,1)} %get-tuple-element.34.d_ref, bf16[4,256,192]{2,1,0:T(8,128)(2,1)} %get-tuple-element.35.d_other_ref), custom_call_target="tpu_custom_call" | custom-call | flops 150994944 | bytes 2162688 | tf_op jit(solution)/shard_map/pallas_call | solution.py:36
  117.9 1.8 %shard_map.104 = bf16[1,4,48,384]{3,2,1,0:T(8,128)(2,1)} custom-call(f32[2,4,48,384]{3,2,1,0:T(8,128)} %shard_map.101.keep_ref, bf16[2,4,48,384]{3,2,1,0:T(8,128)(2,1)} %copy-done.5), custom_call_target="tpu_custom_call" | custom-call | bytes 1032192 | tf_op jit(solution)/shard_map/pallas_call | solution.py:36
  120.3 1.9 %shard_map.103.keep_o_ref = f32[1,4,48,384]{3,2,1,0:T(8,128)} custom-call(f32[2,4,48,384]{3,2,1,0:T(8,128)} %shard_map.101.keep_ref, bf16[2,4,48,384]{3,2,1,0:T(8,128)(2,1)} %copy-done.5), custom_call_target="tpu_custom_call" | custom-call | bytes 1179648 | tf_op jit(solution)/shard_map/pallas_call | solution.py:36
  122.2 2.7 %shard_map.98.keep_ref = f32[1,4,48,1152]{3,2,1,0:T(8,128)} custom-call(f32[2,4,48,1152]{3,2,1,0:T(8,128)} %shard_map.96.keep_ref, bf16[2,4,48,1152]{3,2,1,0:T(8,128)(2,1)} %copy-done.3), custom_call_target="tpu_custom_call" | custom-call | bytes 3538944 | tf_op jit(solution)/shard_map/pallas_call | solution.py:36
  126.5 2.4 %shard_map.105 = (f32[48,1536]{1,0:T(8,128)}, bf16[48,1536]{1,0:T(8,128)(2,1)}, bf16[48,1536]{1,0:T(8,128)(2,1)}, bf16[48,1536]{1,0:T(8,128)(2,1)}) custom-call(f32[1,4,48,1152]{3,2,1,0:T(8,128)} %shard_map.98.keep_ref, bf16[1,4,48,1152]{3,2,1,0:T(8,128)(2,1)} %copy-done.6, f32[1,4,48,384]{3,2,1,0:T(8,128)} %shard_map.103.keep_o_ref, ...), custom_call_target="tpu_custom_call" | custom-call | bytes 2506752 | tf_op jit(solution)/shard_map/pallas_call | solution.py:36
  128.9 1.5 %collective-permute-start.7 = (bf16[48,1536]{1,0:T(8,128)(2,1)}, bf16[48,1536]{1,0:T(8,128)(2,1)S(1)}, u32[]{:S(2)}, u32[]{:S(2)}) collective-permute-start(bf16[48,1536]{1,0:T(8,128)(2,1)} %get-tuple-element.37), channel_id=1, source_target_pairs={{0,2},{1,3},{2,4},{3,5},{4,6},{5,7},{6,0},{7,1},{8,10},{9,11},{10,... | collective-permute-start | bytes 442376 | tf_op jit(solution)/shard_map/ppermute | solution.py:298
  130.4 2.5 %collective-permute-start.8 = (bf16[48,1536]{1,0:T(8,128)(2,1)}, bf16[48,1536]{1,0:T(8,128)(2,1)S(1)}, u32[]{:S(2)}, u32[]{:S(2)}) collective-permute-start(bf16[48,1536]{1,0:T(8,128)(2,1)} %get-tuple-element.38), channel_id=1, source_target_pairs={{0,4},{1,5},{2,6},{3,7},{4,0},{5,1},{6,2},{7,3},{8,12},{9,13},{10,... | collective-permute-start | bytes 442376 | tf_op jit(solution)/shard_map/ppermute | solution.py:298
  132.9 1.4 collective-permute-start.9
  135.6 2.7 %shard_map.93 = bf16[256,768]{1,0:T(8,128)(2,1)} custom-call(bf16[256,768]{1,0:T(8,128)(2,1)} %bitcast.20, bf16[256,768]{1,0:T(8,128)(2,1)} %bitcast.22, bf16[768,768]{1,0:T(8,128)(2,1)} %wout_ref.3), custom_call_target="tpu_custom_call" | custom-call | flops 301989888 | bytes 2359296 | tf_op jit(solution)/shard_map/pallas_call | solution.py:36
  138.3 3.8 %collective-permute-done.8.rest_1_ = bf16[48,1536]{1,0:T(8,128)(2,1)S(1)} collective-permute-done((bf16[48,1536]{1,0:T(8,128)(2,1)}, bf16[48,1536]{1,0:T(8,128)(2,1)S(1)}, u32[]{:S(2)}, u32[]{:S(2)}) %collective-permute-start.8) | collective-permute-done | bytes 147488 | tf_op jit(solution)/shard_map/ppermute | solution.py:298
  142.9 2.0 %shard_map.106 = (f32[96,576]{1,0:T(8,128)}, f32[96,192]{1,0:T(8,128)}) custom-call(f32[48,1536]{1,0:T(8,128)} %get-tuple-element.36.own_ref, bf16[48,1536]{1,0:T(8,128)(2,1)} %copy-done.9, bf16[48,1536]{1,0:T(8,128)(2,1)} %copy-done.10, bf16[48,1536]{1,0:T(8,128)(2,1)} %copy-done.11), custom_call_target="tpu_custom_call" | custom-call | bytes 1032192 | tf_op jit(solution)/shard_map/pallas_call | solution.py:36
  (52 shorter events, 11.0 us)
Async XLA Ops:
  0.6 23.5 %copy-start.12 = (f32[768]{0:T(1024)S(1)}, f32[768]{0:T(1024)}, u32[]{:S(2)}) copy-start(f32[768]{0:T(1024)} %param.6) | copy-start | bytes 9220
  21.5 17.2 %all-to-all-start.2 = ((bf16[32,1,8,768]{3,2,1,0:T(8,128)(2,1)}), bf16[32,1,8,768]{3,2,1,0:T(8,128)(2,1)S(1)}, u32[]{:S(2)}, u32[]{:S(2)}) async-start(bf16[32,1,8,768]{3,2,1,0:T(8,128)(2,1)} %bitcast.26), calls=%async_computation.2 | async-start | bytes 786432 | tf_op jit(solution)/shard_map/all_to_all | solution.py:306
  38.7 0.8 copy-start.1
  50.0 1.8 %copy-start.13 = (bf16[2,4,96,256]{3,2,1,0:T(8,128)(2,1)S(1)}, bf16[2,4,96,256]{3,2,1,0:T(8,128)(2,1)}, u32[]{:S(2)}) copy-start(bf16[2,4,96,256]{3,2,1,0:T(8,128)(2,1)} %get-tuple-element.32) | copy-start | bytes 1179652
  51.6 2.9 %collective-permute-start.1 = (bf16[4,256,576]{1,2,0:T(8,128)(2,1)S(1)}, bf16[4,256,576]{1,2,0:T(8,128)(2,1)S(1)}, u32[]{:S(2)}, u32[]{:S(2)}) collective-permute-start(bf16[4,256,576]{1,2,0:T(8,128)(2,1)S(1)} %copy.12), channel_id=1, source_target_pairs={{0,1},{1,0},{2,3},{3,2},{4,5},{5,4},{6,7},{7,6},{8,9},{9,8},{10,11... | collective-permute-start | bytes 3538952 | tf_op jit(solution)/shard_map/ppermute | solution.py:221
  51.8 4.2 %collective-permute-start = (bf16[2,4,96,256]{3,2,1,0:T(8,128)(2,1)S(1)}, bf16[2,4,96,256]{3,2,1,0:T(8,128)(2,1)S(1)}, u32[]{:S(2)}, u32[]{:S(2)}) collective-permute-start(bf16[2,4,96,256]{3,2,1,0:T(8,128)(2,1)S(1)} %copy-done.13), channel_id=1, source_target_pairs={{0,1},{1,0},{2,3},{3,2},{4,5},{5,4},{6,7},{7,6},{8,9},{9,8},{10,11... | collective-permute-start | bytes 1179656 | tf_op jit(solution)/shard_map/ppermute | solution.py:221
  56.0 0.8 copy-start
  60.5 48.9 %collective-permute-start.2 = (bf16[2,4,48,1152]{3,2,1,0:T(8,128)(2,1)}, bf16[2,4,48,1152]{3,2,1,0:T(8,128)(2,1)S(1)}, u32[]{:S(2)}, u32[]{:S(2)}) collective-permute-start(bf16[2,4,48,1152]{3,2,1,0:T(8,128)(2,1)} %shard_map.97), channel_id=1, source_target_pairs={{0,8},{1,17},{2,10},{3,19},{4,12},{5,21},{6,14},{7,23},{8,0},{9,25... | collective-permute-start | bytes 2654216 | tf_op jit(solution)/shard_map/ppermute | solution.py:217
  62.1 19.9 %copy-start.2 = (bf16[32,1,8,768]{3,2,1,0:T(8,128)(2,1)S(1)}, bf16[32,1,8,768]{3,2,1,0:T(8,128)(2,1)}, u32[]{:S(2)}) copy-start(bf16[32,1,8,768]{3,2,1,0:T(8,128)(2,1)} %copy-done.1) | copy-start | bytes 1179652
  79.4 16.0 %all-to-all-start.3 = ((bf16[32,1,8,768]{3,2,1,0:T(8,128)(2,1)}), bf16[32,1,8,768]{3,2,1,0:T(8,128)(2,1)S(1)}, u32[]{:S(2)}, u32[]{:S(2)}) async-start(bf16[32,1,8,768]{3,2,1,0:T(8,128)(2,1)} %bitcast.27), calls=%async_computation.3 | async-start | bytes 786432 | tf_op jit(solution)/shard_map/all_to_all | solution.py:313
  82.0 16.0 %collective-permute-start.4 = (bf16[256,768]{1,0:T(8,128)(2,1)S(1)}, bf16[256,768]{1,0:T(8,128)(2,1)S(1)}, u32[]{:S(2)}, u32[]{:S(2)}) collective-permute-start(bf16[256,768]{1,0:T(8,128)(2,1)S(1)} %bitcast.18), channel_id=1, source_target_pairs={{0,1},{1,0},{2,3},{3,2},{4,5},{5,4},{6,7},{7,6},{8,9},{9,8},{10,11... | collective-permute-start | bytes 1179656 | tf_op jit(solution)/shard_map/ppermute | solution.py:221
  95.5 39.4 %all-to-all-start.1 = ((bf16[32,1,8,768]{3,2,1,0:T(8,128)(2,1)}), bf16[32,1,8,768]{3,2,1,0:T(8,128)(2,1)S(1)}, u32[]{:S(2)}, u32[]{:S(2)}) async-start(bf16[32,1,8,768]{3,2,1,0:T(8,128)(2,1)} %bitcast.4), calls=%async_computation.1 | async-start | bytes 786432 | tf_op jit(solution)/shard_map/all_to_all | solution.py:313
  98.1 0.7 copy-start.7
  103.7 13.5 %collective-permute-start.5 = (bf16[2,4,48,384]{3,2,1,0:T(8,128)(2,1)}, bf16[2,4,48,384]{3,2,1,0:T(8,128)(2,1)S(1)}, u32[]{:S(2)}, u32[]{:S(2)}) collective-permute-start(bf16[2,4,48,384]{3,2,1,0:T(8,128)(2,1)} %shard_map.102), channel_id=1, source_target_pairs={{0,8},{1,17},{2,10},{3,19},{4,12},{5,21},{6,14},{7,23},{8,0},{9,25... | collective-permute-start | bytes 884744 | tf_op jit(solution)/shard_map/ppermute | solution.py:217
  109.4 1.0 copy-start.3
  113.0 12.1 %collective-permute-start.3 = (bf16[1,4,48,1152]{3,2,1,0:T(8,128)(2,1)}, bf16[1,4,48,1152]{3,2,1,0:T(8,128)(2,1)S(1)}, u32[]{:S(2)}, u32[]{:S(2)}) collective-permute-start(bf16[1,4,48,1152]{3,2,1,0:T(8,128)(2,1)} %shard_map.99), channel_id=1, source_target_pairs={{0,16},{1,9},{2,18},{3,11},{4,20},{5,13},{6,22},{7,15},{8,24},{9,1... | collective-permute-start | bytes 1327112 | tf_op jit(solution)/shard_map/ppermute | solution.py:217
  117.2 0.7 copy-start.5
  119.7 5.4 %collective-permute-start.6 = (bf16[1,4,48,384]{3,2,1,0:T(8,128)(2,1)}, bf16[1,4,48,384]{3,2,1,0:T(8,128)(2,1)S(1)}, u32[]{:S(2)}, u32[]{:S(2)}) collective-permute-start(bf16[1,4,48,384]{3,2,1,0:T(8,128)(2,1)} %shard_map.104), channel_id=1, source_target_pairs={{0,16},{1,9},{2,18},{3,11},{4,20},{5,13},{6,22},{7,15},{8,24},{9,1... | collective-permute-start | bytes 442376 | tf_op jit(solution)/shard_map/ppermute | solution.py:217
  125.1 0.7 copy-start.8
  125.8 0.8 copy-start.6
  128.9 9.4 %collective-permute-start.7 = (bf16[48,1536]{1,0:T(8,128)(2,1)}, bf16[48,1536]{1,0:T(8,128)(2,1)S(1)}, u32[]{:S(2)}, u32[]{:S(2)}) collective-permute-start(bf16[48,1536]{1,0:T(8,128)(2,1)} %get-tuple-element.37), channel_id=1, source_target_pairs={{0,2},{1,3},{2,4},{3,5},{4,6},{5,7},{6,0},{7,1},{8,10},{9,11},{10,... | collective-permute-start | bytes 442376 | tf_op jit(solution)/shard_map/ppermute | solution.py:298
  130.4 11.7 %collective-permute-start.8 = (bf16[48,1536]{1,0:T(8,128)(2,1)}, bf16[48,1536]{1,0:T(8,128)(2,1)S(1)}, u32[]{:S(2)}, u32[]{:S(2)}) collective-permute-start(bf16[48,1536]{1,0:T(8,128)(2,1)} %get-tuple-element.38), channel_id=1, source_target_pairs={{0,4},{1,5},{2,6},{3,7},{4,0},{5,1},{6,2},{7,3},{8,12},{9,13},{10,... | collective-permute-start | bytes 442376 | tf_op jit(solution)/shard_map/ppermute | solution.py:298
  132.9 9.3 %collective-permute-start.9 = (bf16[48,1536]{1,0:T(8,128)(2,1)}, bf16[48,1536]{1,0:T(8,128)(2,1)S(1)}, u32[]{:S(2)}, u32[]{:S(2)}) collective-permute-start(bf16[48,1536]{1,0:T(8,128)(2,1)} %get-tuple-element.39), channel_id=1, source_target_pairs={{0,6},{1,7},{2,0},{3,1},{4,2},{5,3},{6,4},{7,5},{8,14},{9,15},{10,... | collective-permute-start | bytes 442376 | tf_op jit(solution)/shard_map/ppermute | solution.py:298
  134.8 0.7 copy-start.4
  138.3 3.9 %copy-start.9 = (bf16[48,1536]{1,0:T(8,128)(2,1)}, bf16[48,1536]{1,0:T(8,128)(2,1)S(1)}, u32[]{:S(2)}) copy-start(bf16[48,1536]{1,0:T(8,128)(2,1)S(1)} %collective-permute-done.7.rest_0_) | copy-start | bytes 442372
  142.2 0.7 copy-start.10
  142.2 0.7 copy-start.11

commit v3 on v2

--- a/solution.py
+++ b/solution.py
@@ -8,6 +8,7 @@
 from jax.experimental.pallas import tpu as pltpu
 from jax.sharding import PartitionSpec as P
 
+
 HEADS = 12
 HEAD_DIM = 64
 WINDOW = 4
@@ -19,7 +20,7 @@
 F32 = jnp.float32
 AXES = ("tm", "inner")
 LANES = 128
-VMEM_LIMIT = 60 * 1024 * 1024
+VMEM_SPARE = 8 * 1024 * 1024
 
 
 def mm(a, b):
@@ -31,13 +32,15 @@
 
 
 def call(kernel, out_shape, *args, scratch=(), flops=0):
-    leaves = jax.tree.leaves(out_shape) + list(args)
-    moved = sum(math.prod(a.shape) * a.dtype.itemsize for a in leaves)
+    def size(arrays):
+        return sum(math.prod(a.shape) * jnp.dtype(a.dtype).itemsize for a in arrays)
+
+    moved = size(jax.tree.leaves(out_shape) + list(args))
     return pl.pallas_call(
         kernel,
         out_shape=out_shape,
         scratch_shapes=scratch,
-        compiler_params=pltpu.CompilerParams(vmem_limit_bytes=VMEM_LIMIT),
+        compiler_params=pltpu.CompilerParams(vmem_limit_bytes=moved + size(scratch) + VMEM_SPARE),
         cost_estimate=pl.CostEstimate(flops=flops, bytes_accessed=moved, transcendentals=0),
     )(*args)
 
@@ -114,18 +117,7 @@
     out_ref[...] = (frames_ref[...].astype(F32) + mm(mixed_ref[...], wout_ref[...])).astype(BF)
 
 
-def put_blocks(dst_ref, src):
-    parts, _, wide = dst_ref.shape
-    for j in range(parts):
-        dst_ref[j] = src[:, j * wide : (j + 1) * wide]
-
-
-def blocks_kernel(cot_ref, other_ref, out_ref, out_other_ref):
-    put_blocks(out_ref, cot_ref[...])
-    put_blocks(out_other_ref, other_ref[...])
-
-
-def backward_kernel(reach, cot_ref, wout_ref, q_ref, kt_ref, v_ref, prob_ref, dqkv_ref, dblk_ref, gm_ref, dqt_ref):
+def backward_kernel(reach, cot_ref, wout_ref, q_ref, kt_ref, v_ref, prob_ref, dqkv_ref, gm_ref, dqt_ref):
     tokens, width = cot_ref.shape
     gm_ref[...] = mm_t(cot_ref[...], wout_ref[...]).astype(BF)
     spans = key_spans(tokens, reach)
@@ -164,7 +156,6 @@
 
     lax.fori_loop(0, HEADS // 2, pair, 0)
     dqkv_ref[:, :width] = dqt_ref[...].T.astype(BF)
-    put_blocks(dblk_ref, dqkv_ref[...])
 
 
 def norm_kernel(x_ref, cot_ref, gain_ref, dqkv_ref, wqkv_ref, fgrad_ref, gpart_ref):
@@ -221,17 +212,26 @@
     return lax.ppermute(value, "inner", [(i, i ^ 1) for i in range(inner)])
 
 
-def product_kernel(runs, slot, send, mine_ref, other_ref, d_ref, d_other_ref, out_ref):
+def product_kernel(runs, send, mine_ref, other_ref, d_ref, d_other_ref, c_ref, c_other_ref, out_ref, dblk_ref, cblk_ref):
     count, rows, tokens = mine_ref.shape[1:]
     half = rows // 2
-    left = mine_ref[slot].reshape(count * rows, tokens)
-    right = other_ref[slot].reshape(count * rows, tokens)
+    for p, (d, c) in enumerate(((d_ref, c_ref), (d_other_ref, c_other_ref))):
+        for dst, src in ((dblk_ref, d), (cblk_ref, c)):
+            wide = dst.shape[3]
+            for j in range(runs):
+                dst[p, j] = src[:, j * wide : (j + 1) * wide]
     for n in range(out_ref.shape[0]):
         run, _ = place_of(runs, 0, n, send)
-        total = mm(left, d_ref[run]) + mm(right, d_other_ref[run])
-        for z in range(count):
-            block = total[z * rows : (z + 1) * rows]
-            out_ref[n, z] = jnp.concatenate([block[:half], block[half:]], 1).astype(out_ref.dtype)
+        first = 0
+        for slot, blocks in ((0, dblk_ref), (1, cblk_ref)):
+            left = mine_ref[slot].reshape(count * rows, tokens)
+            right = other_ref[slot].reshape(count * rows, tokens)
+            total = mm(left, blocks[0, run]) + mm(right, blocks[1, run])
+            wide = 2 * total.shape[1]
+            for z in range(count):
+                block = total[z * rows : (z + 1) * rows]
+                out_ref[n, z, :, first : first + wide] = jnp.concatenate([block[:half], block[half:]], 1).astype(out_ref.dtype)
+            first += wide
 
 
 def stage_kernel(runs, stage, send, keep_ref, got_ref, out_ref):
@@ -240,33 +240,31 @@
         out_ref[n] = (keep_ref[place] + got_ref[place].astype(F32)).astype(out_ref.dtype)
 
 
-def start_reduce(slot, mine, other, d, d_other, runs):
+def reduce_runs(mine, other, d, d_other, c, c_other, runs, inner):
     count, rows, tokens = mine.shape[1:]
-    folded = (runs // 2, count, rows // 2, 2 * d.shape[2])
-    flops = 2 * count * rows * 2 * tokens * d.shape[2] * (runs // 2)
-    send = call(functools.partial(product_kernel, runs, slot, True), jax.ShapeDtypeStruct(folded, BF), mine, other, d, d_other, flops=flops)
-    keep = call(functools.partial(product_kernel, runs, slot, False), jax.ShapeDtypeStruct(folded, F32), mine, other, d, d_other, flops=flops)
-    return send, keep
-
-
-def reduce_runs(send, keep, runs, inner):
+    wide, thin = d.shape[1] // runs, c.shape[1] // runs
+    shape = (runs // 2, count, rows // 2, 2 * (wide + thin))
+    flops = 2 * count * rows * 2 * tokens * (wide + thin) * (runs // 2)
+    scratch = [pltpu.VMEM((2, runs, tokens, wide), BF), pltpu.VMEM((2, runs, tokens, thin), BF)]
+    args = (mine, other, d, d_other, c, c_other)
+    send = call(functools.partial(product_kernel, runs, True), jax.ShapeDtypeStruct(shape, BF), *args, scratch=scratch, flops=flops)
     got = exchange(send, runs, inner, 0)
+    keep = call(functools.partial(product_kernel, runs, False), jax.ShapeDtypeStruct(shape, F32), *args, scratch=scratch, flops=flops)
     for stage in range(1, runs.bit_length() - 1):
-        shape = (keep.shape[0] // 2,) + keep.shape[1:]
+        shape = (shape[0] // 2,) + shape[1:]
         send = call(functools.partial(stage_kernel, runs, stage, True), jax.ShapeDtypeStruct(shape, BF), keep, got)
+        later = exchange(send, runs, inner, stage)
         keep = call(functools.partial(stage_kernel, runs, stage, False), jax.ShapeDtypeStruct(shape, F32), keep, got)
-        got = exchange(send, runs, inner, stage)
+        got = later
     return keep, got
 
 
-def rows_kernel(keep_ref, got_ref, keep_o_ref, got_o_ref, own_ref, *send_refs):
+def rows_kernel(keep_ref, got_ref, own_ref, *send_refs):
     count = keep_ref.shape[1]
     me = lax.axis_index("inner") >> 1
 
     def total(z):
-        left = keep_ref[0, z] + got_ref[0, z].astype(F32)
-        right = keep_o_ref[0, z] + got_o_ref[0, z].astype(F32)
-        return jnp.concatenate([left, right], 1)
+        return keep_ref[0, z] + got_ref[0, z].astype(F32)
 
     for k, ref in enumerate(send_refs):
         ref[...] = total(lax.rem(me + k + 1, count)).astype(BF)
@@ -287,16 +285,15 @@
     o_ref[half:] = total[:, 2 * wide + thin :]
 
 
-def reduce_rows(parts_q, parts_o, inner, inv_root):
-    _, count, half, wide = parts_q[0].shape
-    thin = parts_o[0].shape[3]
-    block = (half, wide + thin)
+def reduce_rows(keep, got, wide, thin, inner, inv_root):
+    _, count, half, lanes = keep.shape
+    block = (half, lanes)
     sds = jax.ShapeDtypeStruct
-    own, *sends = call(rows_kernel, (sds(block, F32),) + (sds(block, BF),) * (count - 1), *parts_q, *parts_o)
+    own, *sends = call(rows_kernel, (sds(block, F32),) + (sds(block, BF),) * (count - 1), keep, got)
     got = []
     for k, send in enumerate(sends):
         got.append(lax.ppermute(send, "inner", [(i, (i + 2 * (k + 1)) % inner) for i in range(inner)]))
-    out = (sds((2 * half, wide // 2), F32), sds((2 * half, thin // 2), F32))
+    out = (sds((2 * half, wide), F32), sds((2 * half, thin), F32))
     return call(functools.partial(last_kernel, inv_root), out, own, *got)
 
 
@@ -365,14 +362,10 @@
     mixed_back = to_frames(mixed, count, held, patches)
     block_out = call(out_kernel, sds((held * patches, width), BF), frames.reshape(-1, width), mixed_back.reshape(-1, width), w_out, flops=2 * tokens * width * width)
     block_out = block_out.reshape(held, patches, width)
-
-    cblk = sds((runs, tokens, width // runs), BF)
-    cblk, cblk_other = call(blocks_kernel, (cblk, cblk), cot, to_partner(cot, inner))
-    parts_o = reduce_runs(*start_reduce(1, mine, theirs, cblk, cblk_other, runs), runs, inner)
-
-    dqkv, dblk = call(
+    cot_other = to_partner(cot, inner)
+    dqkv = call(
         functools.partial(backward_kernel, reach),
-        (sds((tokens, 3 * width), BF), sds((runs, tokens, 3 * width // runs), BF)),
+        sds((tokens, 3 * width), BF),
         cot,
         w_out,
         q,
@@ -382,7 +375,7 @@
         scratch=[vmem((tokens, width), BF), vmem((width, tokens), F32)],
         flops=2 * tokens * width * 4 * width,
     )
-    dblk_other = to_partner(dblk, inner)
+    dqkv_other = to_partner(dqkv, inner)
     fgrad, gpart = call(
         norm_kernel,
         (sds((tokens, width), BF), sds((1, width), F32)),
@@ -394,8 +387,8 @@
         flops=2 * tokens * width * 3 * width,
     )
     frames_grad = to_frames(fgrad, count, held, patches)
-    parts_q = reduce_runs(*start_reduce(0, mine, theirs, dblk, dblk_other, runs), runs, inner)
-    qkv_grad, out_grad = reduce_rows(parts_q, parts_o, inner, inv_root)
+    keep, got = reduce_runs(mine, theirs, dqkv, dqkv_other, cot, cot_other, runs, inner)
+    qkv_grad, out_grad = reduce_rows(keep, got, 3 * width // runs, width // runs, inner, inv_root)
     shares = jnp.broadcast_to(gpart.reshape(1, inner, width // inner), (runs, inner, width // inner))
     shares = lax.all_to_all(shares.reshape(count, 1, -1), AXES, split_axis=0, concat_axis=0, tiled=True)
     gain_grad = jnp.sum(shares, axis=(0, 1)) * inv_root

time: 147 us -> 123 us (0.84)
  Pallas kernels: 59.8 us -> 27.7 us
  local copies, waits for them, and re-layouts: 11.3 us -> 19 us
  blocking collectives: 32.6 us -> 34.6 us
    pallas_call x15 -> x10, Pallas kernels: 59.8 us -> 27.7 us  [call(): pl.pallas_call(kernel, out_shape=out_shape, scratch_shapes=scratch, compi...]
    unnamed x29 -> x55, local copies, waits for them, and re-layouts: 7.57 us -> 18.9 us
    all_to_all x2, starting transfers between devices: 5.19 us -> 7.53 us  [to_frames(): parts = lax.all_to_all(parts, AXES, split_axis=0, concat_axis=0, tiled=True)]
    ppermute x3, waiting for transfers between devices: 3.85 us -> 1.53 us  [reduce_rows(): lax.ppermute(send, 'inner', [(i, (i + 2 * (k + 1)) % inner) for i in rang...]
    ppermute x4 -> x2, waiting for transfers between devices: 0.21 us -> 2.51 us  [exchange(): return lax.ppermute(value, AXES, perm)]
    all_to_all x1, blocking collectives: 11.7 us -> 13.8 us  [shards(): lax.all_to_all(shares.reshape(count, 1, -1), AXES, split_axis=0, concat_a...]
    ppermute x4 -> x2, starting transfers between devices: 5.29 us -> 3.4 us  [exchange(): return lax.ppermute(value, AXES, perm)]
    pallas_call x1 -> x0, local copies, waits for them, and re-layouts: 1.64 us -> none  [call(): pl.pallas_call(kernel, out_shape=out_shape, scratch_shapes=scratch, compi...]
  transfers between devices with their start and end apart: 13 -> 11, of which waited for: 4 -> 6; matrix products, arithmetic and copies ran while one was open for 3% -> 1% of each run, Pallas kernels for 30% -> 15%
where the time goes in v3:
time: 123 us; the launch traced here: 122 us
  blocking collectives  34.6 us (28%)
  Pallas kernels  27.7 us (23%)
  waiting for transfers between devices  19.5 us (16%)
  starting transfers between devices  19.2 us (16%)
  local copies, waits for them, and re-layouts  19 us (15%)
    pallas_call x10, Pallas kernels, call(): pl.pallas_call(kernel, out_shape=out_shape, scratch_shapes=scratch, compi...  27.7 us
    all_to_all x1, blocking collectives, to_tubes(): parts = lax.all_to_all(parts, AXES, split_axis=0, concat_axis=0, tiled=True)  20.8 us
    unnamed x55, local copies, waits for them, and re-layouts  18.9 us
    all_to_all x1, blocking collectives, shards(): lax.all_to_all(shares.reshape(count, 1, -1), AXES, split_axis=0, concat_a...  13.8 us
    all_to_all x2, waiting for transfers between devices, to_frames(): parts = lax.all_to_all(parts, AXES, split_axis=0, concat_axis=0, tiled=True)  12.1 us
    all_to_all x2, starting transfers between devices, to_frames(): parts = lax.all_to_all(parts, AXES, split_axis=0, concat_axis=0, tiled=True)  7.53 us
    ppermute x3, starting transfers between devices, reduce_rows(): lax.ppermute(send, 'inner', [(i, (i + 2 * (k + 1)) % inner) for i in rang...  4.94 us
    ppermute x2, starting transfers between devices, exchange(): return lax.ppermute(value, AXES, perm)  3.4 us
  transfers between devices with their start and end apart: 11, of which 6 were waited for; matrix products, arithmetic and copies ran while one was open for 1% of the time, Pallas kernels for 15%

profile of v3, /device:TPU:0, one launch (start us, length us, event | category | flops | bytes accessed | tf_op | source)
XLA Modules:
  0.0 121.7 jit_solution(2779625741575352886)
XLA Ops:
  0.6 20.8 %all_to_all.25 = bf16[32,1,8,768]{3,2,1,0:T(8,128)(2,1)S(1)} all-to-all(bf16[32,1,8,768]{3,2,1,0:T(8,128)(2,1)} %bitcast.20), channel_id=1, replica_groups=mesh['tm'=4,'inner'=8] {'tm','inner'}, dimensions={0} | all-to-all | bytes 786432 | tf_op jit(solution)/shard_map/all_to_all | solution.py:303
  21.4 2.6 %all-to-all-start.2 = ((bf16[32,1,8,768]{3,2,1,0:T(8,128)(2,1)}), bf16[32,1,8,768]{3,2,1,0:T(8,128)(2,1)S(1)}, u32[]{:S(2)}, u32[]{:S(2)}) async-start(bf16[32,1,8,768]{3,2,1,0:T(8,128)(2,1)} %bitcast.27), calls=%async_computation.2 | async-start | bytes 786432 | tf_op jit(solution)/shard_map/all_to_all | solution.py:303
  24.4 2.0 %copy-done.6 = bf16[768,2304]{1,0:T(8,128)(2,1)S(1)} copy-done((bf16[768,2304]{1,0:T(8,128)(2,1)S(1)}, bf16[768,2304]{1,0:T(8,128)(2,1)}, u32[]{:S(2)}) %copy-start.6) | copy-done | bytes 3538968
  26.4 8.9 %shard_map.92 = (bf16[2,4,96,256]{3,2,1,0:T(8,128)(2,1)S(1)}, bf16[2,4,96,256]{3,2,1,0:T(8,128)(2,1)S(1)}, bf16[256,768]{1,0:T(8,128)(2,1)S(1)}, bf16[768,256]{1...) custom-call(bf16[256,768]{1,0:T(8,128)(2,1)S(1)} %bitcast.22, ...), custom_call_target="tpu_custom_call" | custom-call | flops 1207959552 | bytes 8522752 | tf_op jit(solution)/shard_map/pallas_call | solution.py:39
  35.2 1.3 %copy-done.8 = f32[12,2,160,128]{3,2,1,0:T(8,128)} copy-done((f32[12,2,160,128]{3,2,1,0:T(8,128)}, f32[12,2,160,128]{3,2,1,0:T(8,128)S(1)}, u32[]{:S(2)}) %copy-start.8) | copy-done | bytes 1966104
  40.3 1.8 %copy-done.9 = f32[12,2,160,128]{3,2,1,0:T(8,128)S(1)} copy-done((f32[12,2,160,128]{3,2,1,0:T(8,128)S(1)}, f32[12,2,160,128]{3,2,1,0:T(8,128)}, u32[]{:S(2)}) %copy-start.9) | copy-done | bytes 1966104
  42.1 1.0 copy-done.18
  43.1 1.0 copy-done.20
  44.1 1.0 copy-done.22
  45.1 6.6 %shard_map.94.dqkv_ref.d_ref = bf16[256,2304]{1,0:T(8,128)(2,1)S(1)} custom-call(bf16[256,768]{1,0:T(8,128)(2,1)S(1)} %bitcast.15, bf16[768,768]{1,0:T(8,128)(2,1)S(1)} %copy-done.4, bf16[256,768]{1,0:T(8,128)(2,1)S(1)} %copy-done.18, bf16[768,256]{1,0:T(8,128)(2,1)S(1)} %copy-done.20, bf16[256,768]{1,0:T(8,128)(2,1)S(1)} %copy-done.22, ...), custom_call_target="tpu_custom_call" | custom-call | flops 1207959552 | bytes 5898240 | tf_op jit(solution)/shard_map/pallas_call | solution.py:39
  52.4 2.8 %collective-permute-done.2.c_other_ref = bf16[256,768]{1,0:T(8,128)(2,1)S(1)} collective-permute-done((bf16[256,768]{1,0:T(8,128)(2,1)S(1)}, bf16[256,768]{1,0:T(8,128)(2,1)S(1)}, u32[]{:S(2)}, u32[]{:S(2)}) %collective-permute-start.2) | collective-permute-done | bytes 393248 | tf_op jit(solution)/shard_map/ppermute | solution.py:212
  55.8 2.4 %shard_map.97 = bf16[2,4,48,1536]{3,2,1,0:T(8,128)(2,1)} custom-call(bf16[2,4,96,256]{3,2,1,0:T(8,128)(2,1)S(1)} %get-tuple-element.26.mine_ref, bf16[2,4,96,256]{3,2,1,0:T(8,128)(2,1)S(1)} %collective-permute-done.other_ref, bf16[256,2304]{1,0:T(8,128)(2,1)S(1)} %shard_map.94.dqkv_ref.d_ref, bf16[256,2304]{1,0:T(8,128)(2,1)S(1)} %collective-permute-done.1.d_other_ref, ...), custom_call_target="tpu_custom_call" | custom-call | flops 603979776 | bytes 5111808 | tf_op jit(solution)/shard_map/pallas_call | solution.py:39
  58.2 1.7 %collective-permute-start.3 = (bf16[2,4,48,1536]{3,2,1,0:T(8,128)(2,1)}, bf16[2,4,48,1536]{3,2,1,0:T(8,128)(2,1)}, u32[]{:S(2)}, u32[]{:S(2)}) collective-permute-start(bf16[2,4,48,1536]{3,2,1,0:T(8,128)(2,1)} %shard_map.97), channel_id=1, source_target_pairs={{0,8},{1,17},{2,10},{3,19},{4,12},{5,21},{6,14},{7,23},{8,0},{9,25... | collective-permute-start | bytes 3538952 | tf_op jit(solution)/shard_map/ppermute | solution.py:208
  59.9 2.1 %shard_map.95 = (bf16[256,768]{1,0:T(8,128)(2,1)}, f32[1,768]{1,0:T(1,128)S(1)}) custom-call(bf16[256,768]{1,0:T(8,128)(2,1)S(1)} %bitcast.23, bf16[256,768]{1,0:T(8,128)(2,1)S(1)} %bitcast.18, f32[1,768]{1,0:T(1,128)S(1)} %reshape.38.gain_ref, bf16[256,2304]{1,0:T(8,128)(2,1)S(1)} %shard_map.94.dqkv_ref.d_ref, bf16[768,2304]{1,0:T(8,128)(2,1)S(1)} %copy-done.7), custom_call_target="tpu_custom_call" | custom-call | flops 905969664 | bytes 5904384 | tf_op jit(solution)/shard_map/pallas_call | solution.py:39
  62.1 13.8 %all_to_all.26 = f32[32,1,96]{2,1,0:T(1,128)S(1)} all-to-all(f32[32,1,96]{2,1,0:T(1,128)S(1)} %bitcast.28), channel_id=1, replica_groups=mesh['tm'=4,'inner'=8] {'tm','inner'}, dimensions={0} | all-to-all | bytes 24576 | tf_op jit(solution)/shard_map/all_to_all | solution.py:393
  75.9 4.9 %all-to-all-start.3 = ((bf16[32,1,8,768]{3,2,1,0:T(8,128)(2,1)}), bf16[32,1,8,768]{3,2,1,0:T(8,128)(2,1)}, u32[]{:S(2)}, u32[]{:S(2)}) async-start(bf16[32,1,8,768]{3,2,1,0:T(8,128)(2,1)} %bitcast.10), calls=%async_computation.3 | async-start | bytes 786432 | tf_op jit(solution)/shard_map/all_to_all | solution.py:310
  81.9 1.3 %copy-done.3 = bf16[256,2304]{1,0:T(8,128)(2,1)S(1)} copy-done((bf16[256,2304]{1,0:T(8,128)(2,1)S(1)}, bf16[256,2304]{1,0:T(8,128)(2,1)}, u32[]{:S(2)}) %copy-start.3) | copy-done | bytes 1179672
  83.1 1.0 copy-done.11
  84.1 1.0 copy-done.13
  86.1 1.3 %shard_map.96.keep_ref = f32[2,4,48,1536]{3,2,1,0:T(8,128)S(1)} custom-call(bf16[2,4,96,256]{3,2,1,0:T(8,128)(2,1)S(1)} %copy-done.11, bf16[2,4,96,256]{3,2,1,0:T(8,128)(2,1)S(1)} %copy-done.15, bf16[256,2304]{1,0:T(8,128)(2,1)S(1)} %shard_map.94.dqkv_ref.d_ref, bf16[256,2304]{1,0:T(8,128)(2,1)S(1)} %copy-done.3, bf16[256,768]{1,0:T(8,128)(2,1)S(1)} %bitcast.19, ...), custom_call_target="tpu_custom_call" | custom-call | flops 603979776 | bytes 6291456 | tf_op jit(solution)/shard_map/pallas_call | solution.py:39
  87.5 2.2 %shard_map.99 = bf16[1,4,48,1536]{3,2,1,0:T(8,128)(2,1)} custom-call(f32[2,4,48,1536]{3,2,1,0:T(8,128)S(1)} %shard_map.96.keep_ref, bf16[2,4,48,1536]{3,2,1,0:T(8,128)(2,1)} %collective-permute-done.3.got_ref), custom_call_target="tpu_custom_call" | custom-call | bytes 4128768 | tf_op jit(solution)/shard_map/pallas_call | solution.py:39
  89.7 1.7 %collective-permute-start.4 = (bf16[1,4,48,1536]{3,2,1,0:T(8,128)(2,1)}, bf16[1,4,48,1536]{3,2,1,0:T(8,128)(2,1)S(1)}, u32[]{:S(2)}, u32[]{:S(2)}) collective-permute-start(bf16[1,4,48,1536]{3,2,1,0:T(8,128)(2,1)} %shard_map.99), channel_id=1, source_target_pairs={{0,16},{1,9},{2,18},{3,11},{4,20},{5,13},{6,22},{7,15},{8,24},{9,1... | collective-permute-start | bytes 1769480 | tf_op jit(solution)/shard_map/ppermute | solution.py:208
  91.4 2.9 %all-to-all-done.3 = bf16[32,1,8,768]{3,2,1,0:T(8,128)(2,1)} async-done(((bf16[32,1,8,768]{3,2,1,0:T(8,128)(2,1)}), bf16[32,1,8,768]{3,2,1,0:T(8,128)(2,1)}, u32[]{:S(2)}, u32[]{:S(2)}) %all-to-all-start.3) | async-done | bytes 393248 | tf_op jit(solution)/shard_map/all_to_all | solution.py:310
  94.3 2.6 %all-to-all-start.1 = ((bf16[32,1,8,768]{3,2,1,0:T(8,128)(2,1)}), bf16[32,1,8,768]{3,2,1,0:T(8,128)(2,1)S(1)}, u32[]{:S(2)}, u32[]{:S(2)}) async-start(bf16[32,1,8,768]{3,2,1,0:T(8,128)(2,1)} %bitcast.25), calls=%async_computation.1 | async-start | bytes 786432 | tf_op jit(solution)/shard_map/all_to_all | solution.py:310
  97.0 1.4 %shard_map.98.keep_ref = f32[1,4,48,1536]{3,2,1,0:T(8,128)S(1)} custom-call(f32[2,4,48,1536]{3,2,1,0:T(8,128)S(1)} %shard_map.96.keep_ref, bf16[2,4,48,1536]{3,2,1,0:T(8,128)(2,1)} %collective-permute-done.3.got_ref), custom_call_target="tpu_custom_call" | custom-call | bytes 4718592 | tf_op jit(solution)/shard_map/pallas_call | solution.py:39
  98.3 2.5 %collective-permute-done.4.got_ref = bf16[1,4,48,1536]{3,2,1,0:T(8,128)(2,1)S(1)} collective-permute-done((bf16[1,4,48,1536]{3,2,1,0:T(8,128)(2,1)}, bf16[1,4,48,1536]{3,2,1,0:T(8,128)(2,1)S(1)}, u32[]{:S(2)}, u32[]{:S(2)}) %collective-permute-start.4) | collective-permute-done | bytes 589856 | tf_op jit(solution)/shard_map/ppermute | solution.py:208
  101.6 1.7 %collective-permute-start.5 = (bf16[48,1536]{1,0:T(8,128)(2,1)}, bf16[48,1536]{1,0:T(8,128)(2,1)S(1)}, u32[]{:S(2)}, u32[]{:S(2)}) collective-permute-start(bf16[48,1536]{1,0:T(8,128)(2,1)} %get-tuple-element.29), channel_id=1, source_target_pairs={{0,2},{1,3},{2,4},{3,5},{4,6},{5,7},{6,0},{7,1},{8,10},{9,11},{10,... | collective-permute-start | bytes 442376 | tf_op jit(solution)/shard_map/ppermute | solution.py:295
  103.4 3.0 %collective-permute-start.6 = (bf16[48,1536]{1,0:T(8,128)(2,1)}, bf16[48,1536]{1,0:T(8,128)(2,1)S(1)}, u32[]{:S(2)}, u32[]{:S(2)}) collective-permute-start(bf16[48,1536]{1,0:T(8,128)(2,1)} %get-tuple-element.30), channel_id=1, source_target_pairs={{0,4},{1,5},{2,6},{3,7},{4,0},{5,1},{6,2},{7,3},{8,12},{9,13},{10,... | collective-permute-start | bytes 442376 | tf_op jit(solution)/shard_map/ppermute | solution.py:295
  107.1 9.2 %all-to-all-done.1 = bf16[32,1,8,768]{3,2,1,0:T(8,128)(2,1)S(1)} async-done(((bf16[32,1,8,768]{3,2,1,0:T(8,128)(2,1)}), bf16[32,1,8,768]{3,2,1,0:T(8,128)(2,1)S(1)}, u32[]{:S(2)}, u32[]{:S(2)}) %all-to-all-start.1) | async-done | bytes 393248 | tf_op jit(solution)/shard_map/all_to_all | solution.py:310
  116.3 1.2 %shard_map.93 = bf16[256,768]{1,0:T(8,128)(2,1)} custom-call(bf16[256,768]{1,0:T(8,128)(2,1)S(1)} %bitcast.21, bf16[256,768]{1,0:T(8,128)(2,1)S(1)} %bitcast.24, bf16[768,768]{1,0:T(8,128)(2,1)S(1)} %copy-done.5), custom_call_target="tpu_custom_call" | custom-call | flops 301989888 | bytes 2359296 | tf_op jit(solution)/shard_map/pallas_call | solution.py:39
  117.6 1.5 %collective-permute-done.6.rest_1_ = bf16[48,1536]{1,0:T(8,128)(2,1)S(1)} collective-permute-done((bf16[48,1536]{1,0:T(8,128)(2,1)}, bf16[48,1536]{1,0:T(8,128)(2,1)S(1)}, u32[]{:S(2)}, u32[]{:S(2)}) %collective-permute-start.6) | collective-permute-done | bytes 147488 | tf_op jit(solution)/shard_map/ppermute | solution.py:295
  119.9 1.8 %copy.13 = bf16[1,256,768]{2,1,0:T(8,128)(2,1)} copy(bf16[1,256,768]{2,1,0:T(8,128)(2,1)} %bitcast.11) | data formatting | bytes 786432
  (67 shorter events, 9.8 us)
Async XLA Ops:
  0.6 23.4 %copy-start.26 = (f32[768]{0:T(1024)S(1)}, f32[768]{0:T(1024)}, u32[]{:S(2)}) copy-start(f32[768]{0:T(1024)} %param.6) | copy-start | bytes 9220
  21.4 18.9 %all-to-all-start.2 = ((bf16[32,1,8,768]{3,2,1,0:T(8,128)(2,1)}), bf16[32,1,8,768]{3,2,1,0:T(8,128)(2,1)S(1)}, u32[]{:S(2)}, u32[]{:S(2)}) async-start(bf16[32,1,8,768]{3,2,1,0:T(8,128)(2,1)} %bitcast.27), calls=%async_computation.2 | async-start | bytes 786432 | tf_op jit(solution)/shard_map/all_to_all | solution.py:303
  24.4 2.0 %copy-start.6 = (bf16[768,2304]{1,0:T(8,128)(2,1)S(1)}, bf16[768,2304]{1,0:T(8,128)(2,1)}, u32[]{:S(2)}) copy-start(bf16[768,2304]{1,0:T(8,128)(2,1)} %wqkv_ref.3) | copy-start | bytes 10616836
  26.4 13.9 %copy-start.4 = (bf16[768,768]{1,0:T(8,128)(2,1)S(1)}, bf16[768,768]{1,0:T(8,128)(2,1)}, u32[]{:S(2)}) copy-start(bf16[768,768]{1,0:T(8,128)(2,1)} %wout_ref.3) | copy-start | bytes 3538948
  35.2 1.3 %copy-start.8 = (f32[12,2,160,128]{3,2,1,0:T(8,128)}, f32[12,2,160,128]{3,2,1,0:T(8,128)S(1)}, u32[]{:S(2)}) copy-start(f32[12,2,160,128]{3,2,1,0:T(8,128)S(1)} %get-tuple-element.24.prob_ref) | copy-start | bytes 5898244
  40.3 15.5 %copy-start.10 = (bf16[2,4,96,256]{3,2,1,0:T(8,128)(2,1)}, bf16[2,4,96,256]{3,2,1,0:T(8,128)(2,1)S(1)}, u32[]{:S(2)}) copy-start(bf16[2,4,96,256]{3,2,1,0:T(8,128)(2,1)S(1)} %get-tuple-element.26.mine_ref) | copy-start | bytes 1179652
  40.3 19.6 %copy-start = (bf16[32,1,8,768]{3,2,1,0:T(8,128)(2,1)}, bf16[32,1,8,768]{3,2,1,0:T(8,128)(2,1)S(1)}, u32[]{:S(2)}) copy-start(bf16[32,1,8,768]{3,2,1,0:T(8,128)(2,1)S(1)} %all-to-all-done.2) | copy-start | bytes 1179652
  40.3 1.8 %copy-start.9 = (f32[12,2,160,128]{3,2,1,0:T(8,128)S(1)}, f32[12,2,160,128]{3,2,1,0:T(8,128)}, u32[]{:S(2)}) copy-start(f32[12,2,160,128]{3,2,1,0:T(8,128)} %copy-done.8) | copy-start | bytes 5898244
  42.1 1.0 copy-start.18
  43.1 1.0 copy-start.20
  44.1 1.0 copy-start.22
  45.1 7.2 %copy-start.25 = (bf16[2,4,96,256]{3,2,1,0:T(8,128)(2,1)S(1)}, bf16[2,4,96,256]{3,2,1,0:T(8,128)(2,1)}, u32[]{:S(2)}) copy-start(bf16[2,4,96,256]{3,2,1,0:T(8,128)(2,1)} %copy-done.24) | copy-start | bytes 1179652
  51.7 4.0 %collective-permute-start.1 = (bf16[256,2304]{1,0:T(8,128)(2,1)S(1)}, bf16[256,2304]{1,0:T(8,128)(2,1)S(1)}, u32[]{:S(2)}, u32[]{:S(2)}) collective-permute-start(bf16[256,2304]{1,0:T(8,128)(2,1)S(1)} %shard_map.94.dqkv_ref.d_ref), channel_id=1, source_target_pairs={{0,1},{1,0},{2,3},{3,2},{4,5},{5,4},{6,7},{7,6},{8,9},{9,8},{10,11... | collective-permute-start | bytes 3538952 | tf_op jit(solution)/shard_map/ppermute | solution.py:212
  51.9 3.3 %collective-permute-start.2 = (bf16[256,768]{1,0:T(8,128)(2,1)S(1)}, bf16[256,768]{1,0:T(8,128)(2,1)S(1)}, u32[]{:S(2)}, u32[]{:S(2)}) collective-permute-start(bf16[256,768]{1,0:T(8,128)(2,1)S(1)} %bitcast.16), channel_id=1, source_target_pairs={{0,1},{1,0},{2,3},{3,2},{4,5},{5,4},{6,7},{7,6},{8,9},{9,8},{10,11... | collective-permute-start | bytes 1179656 | tf_op jit(solution)/shard_map/ppermute | solution.py:212
  52.3 3.5 %collective-permute-start = (bf16[2,4,96,256]{3,2,1,0:T(8,128)(2,1)S(1)}, bf16[2,4,96,256]{3,2,1,0:T(8,128)(2,1)S(1)}, u32[]{:S(2)}, u32[]{:S(2)}) collective-permute-start(bf16[2,4,96,256]{3,2,1,0:T(8,128)(2,1)S(1)} %copy-done.25), channel_id=1, source_target_pairs={{0,1},{1,0},{2,3},{3,2},{4,5},{5,4},{6,7},{7,6},{8,9},{9,8},{10,11... | collective-permute-start | bytes 1179656 | tf_op jit(solution)/shard_map/ppermute | solution.py:212
  55.2 3.0 %copy-start.12 = (bf16[256,768]{1,0:T(8,128)(2,1)}, bf16[256,768]{1,0:T(8,128)(2,1)S(1)}, u32[]{:S(2)}) copy-start(bf16[256,768]{1,0:T(8,128)(2,1)S(1)} %collective-permute-done.2.c_other_ref) | copy-start | bytes 1179652
  55.8 2.4 %copy-start.14 = (bf16[2,4,96,256]{3,2,1,0:T(8,128)(2,1)}, bf16[2,4,96,256]{3,2,1,0:T(8,128)(2,1)S(1)}, u32[]{:S(2)}) copy-start(bf16[2,4,96,256]{3,2,1,0:T(8,128)(2,1)S(1)} %collective-permute-done.other_ref) | copy-start | bytes 1179652
  55.8 2.4 %copy-start.2 = (bf16[256,2304]{1,0:T(8,128)(2,1)}, bf16[256,2304]{1,0:T(8,128)(2,1)S(1)}, u32[]{:S(2)}) copy-start(bf16[256,2304]{1,0:T(8,128)(2,1)S(1)} %collective-permute-done.1.d_other_ref) | copy-start | bytes 3538948
  55.8 4.1 %copy-start.7 = (bf16[768,2304]{1,0:T(8,128)(2,1)S(1)}, bf16[768,2304]{1,0:T(8,128)(2,1)}, u32[]{:S(2)}) copy-start(bf16[768,2304]{1,0:T(8,128)(2,1)} %wqkv_ref.3) | copy-start | bytes 10616836
  58.2 29.3 %collective-permute-start.3 = (bf16[2,4,48,1536]{3,2,1,0:T(8,128)(2,1)}, bf16[2,4,48,1536]{3,2,1,0:T(8,128)(2,1)}, u32[]{:S(2)}, u32[]{:S(2)}) collective-permute-start(bf16[2,4,48,1536]{3,2,1,0:T(8,128)(2,1)} %shard_map.97), channel_id=1, source_target_pairs={{0,8},{1,17},{2,10},{3,19},{4,12},{5,21},{6,14},{7,23},{8,0},{9,25... | collective-permute-start | bytes 3538952 | tf_op jit(solution)/shard_map/ppermute | solution.py:208
  75.9 18.4 %all-to-all-start.3 = ((bf16[32,1,8,768]{3,2,1,0:T(8,128)(2,1)}), bf16[32,1,8,768]{3,2,1,0:T(8,128)(2,1)}, u32[]{:S(2)}, u32[]{:S(2)}) async-start(bf16[32,1,8,768]{3,2,1,0:T(8,128)(2,1)} %bitcast.10), calls=%async_computation.3 | async-start | bytes 786432 | tf_op jit(solution)/shard_map/all_to_all | solution.py:310
  80.9 1.0 copy-start.1
  81.9 1.3 %copy-start.3 = (bf16[256,2304]{1,0:T(8,128)(2,1)S(1)}, bf16[256,2304]{1,0:T(8,128)(2,1)}, u32[]{:S(2)}) copy-start(bf16[256,2304]{1,0:T(8,128)(2,1)} %copy-done.2) | copy-start | bytes 3538948
  83.1 1.0 copy-start.11
  84.1 1.0 copy-start.13
  89.7 11.2 %collective-permute-start.4 = (bf16[1,4,48,1536]{3,2,1,0:T(8,128)(2,1)}, bf16[1,4,48,1536]{3,2,1,0:T(8,128)(2,1)S(1)}, u32[]{:S(2)}, u32[]{:S(2)}) collective-permute-start(bf16[1,4,48,1536]{3,2,1,0:T(8,128)(2,1)} %shard_map.99), channel_id=1, source_target_pairs={{0,16},{1,9},{2,18},{3,11},{4,20},{5,13},{6,22},{7,15},{8,24},{9,1... | collective-permute-start | bytes 1769480 | tf_op jit(solution)/shard_map/ppermute | solution.py:208
  94.3 22.0 %all-to-all-start.1 = ((bf16[32,1,8,768]{3,2,1,0:T(8,128)(2,1)}), bf16[32,1,8,768]{3,2,1,0:T(8,128)(2,1)S(1)}, u32[]{:S(2)}, u32[]{:S(2)}) async-start(bf16[32,1,8,768]{3,2,1,0:T(8,128)(2,1)} %bitcast.25), calls=%async_computation.1 | async-start | bytes 786432 | tf_op jit(solution)/shard_map/all_to_all | solution.py:310
  98.3 18.0 %copy-start.5 = (bf16[768,768]{1,0:T(8,128)(2,1)S(1)}, bf16[768,768]{1,0:T(8,128)(2,1)}, u32[]{:S(2)}) copy-start(bf16[768,768]{1,0:T(8,128)(2,1)} %wout_ref.3) | copy-start | bytes 3538948
  98.3 18.0 %copy-start.16 = (bf16[1,256,768]{2,1,0:T(8,128)(2,1)S(1)}, bf16[1,256,768]{2,1,0:T(8,128)(2,1)}, u32[]{:S(2)}) copy-start(bf16[1,256,768]{2,1,0:T(8,128)(2,1)} %param.5) | copy-start | bytes 1179652
  101.6 15.9 %collective-permute-start.5 = (bf16[48,1536]{1,0:T(8,128)(2,1)}, bf16[48,1536]{1,0:T(8,128)(2,1)S(1)}, u32[]{:S(2)}, u32[]{:S(2)}) collective-permute-start(bf16[48,1536]{1,0:T(8,128)(2,1)} %get-tuple-element.29), channel_id=1, source_target_pairs={{0,2},{1,3},{2,4},{3,5},{4,6},{5,7},{6,0},{7,1},{8,10},{9,11},{10,... | collective-permute-start | bytes 442376 | tf_op jit(solution)/shard_map/ppermute | solution.py:295
  103.4 15.7 %collective-permute-start.6 = (bf16[48,1536]{1,0:T(8,128)(2,1)}, bf16[48,1536]{1,0:T(8,128)(2,1)S(1)}, u32[]{:S(2)}, u32[]{:S(2)}) collective-permute-start(bf16[48,1536]{1,0:T(8,128)(2,1)} %get-tuple-element.30), channel_id=1, source_target_pairs={{0,4},{1,5},{2,6},{3,7},{4,0},{5,1},{6,2},{7,3},{8,12},{9,13},{10,... | collective-permute-start | bytes 442376 | tf_op jit(solution)/shard_map/ppermute | solution.py:295
  106.3 12.8 %collective-permute-start.7 = (bf16[48,1536]{1,0:T(8,128)(2,1)S(1)}, bf16[48,1536]{1,0:T(8,128)(2,1)S(1)}, u32[]{:S(2)}, u32[]{:S(2)}) collective-permute-start(bf16[48,1536]{1,0:T(8,128)(2,1)S(1)} %get-tuple-element.31), channel_id=1, source_target_pairs={{0,6},{1,7},{2,0},{3,1},{4,2},{5,3},{6,4},{7,5},{8,14},{9,15},{10,... | collective-permute-start | bytes 442376 | tf_op jit(solution)/shard_map/ppermute | solution.py:295
  (6 other events, 4.8 us)

commit v4 on v3

v4 whole, which is shorter than its diff:
```python
import functools
import math

import jax
import jax.numpy as jnp
from jax import lax
from jax.experimental import pallas as pl
from jax.experimental.pallas import tpu as pltpu
from jax.sharding import PartitionSpec as P


HEADS = 12
HEAD_DIM = 64
WINDOW = 4
CLIP_MAX = 256
EPSILON = 1e-06
SCALE = HEAD_DIM ** (-0.5)

BF = jnp.bfloat16
F32 = jnp.float32
AXES = ("tm", "inner")
LANES = 128
VMEM_SPARE = 8 * 1024 * 1024
PIECES = 2


def mm(a, b):
    return lax.dot_general(a, b, (((1,), (0,)), ((), ())), preferred_element_type=F32)


def mm_t(a, b):
    return lax.dot_general(a, b, (((1,), (1,)), ((), ())), preferred_element_type=F32)


def call(kernel, out_shape, *args, scratch=(), flops=0, raw_in=(), raw_out=(), copies=0):
    outs = jax.tree.leaves(out_shape)

    def size(arrays):
        return sum(math.prod(a.shape) * jnp.dtype(a.dtype).itemsize for a in arrays)

    def spec(raw):
        return pl.BlockSpec(memory_space=pltpu.HBM if raw else pltpu.VMEM)

    moved = size(outs) + size(args)
    out_specs = [spec(i in raw_out) for i in range(len(outs))]
    taken = size(a for i, a in enumerate(args) if i not in raw_in) + size(a for i, a in enumerate(outs) if i not in raw_out)
    semaphores = [pltpu.SemaphoreType.DMA((copies,))] if copies else []
    placed = [pltpu.HBM(a.shape, a.dtype) for a in outs]
    args = [pltpu.with_memory_space_constraint(a, pltpu.HBM) if i in raw_in else a for i, a in enumerate(args)]
    return pl.pallas_call(
        kernel,
        out_shape=placed if isinstance(out_shape, (tuple, list)) else placed[0],
        in_specs=[spec(i in raw_in) for i in range(len(args))],
        out_specs=out_specs if isinstance(out_shape, (tuple, list)) else out_specs[0],
        scratch_shapes=list(scratch) + semaphores,
        compiler_params=pltpu.CompilerParams(vmem_limit_bytes=taken + size(scratch) + VMEM_SPARE),
        cost_estimate=pl.CostEstimate(flops=flops, bytes_accessed=moved, transcendentals=0),
    )(*args)


def row_stats(x):
    center = x - jnp.mean(x, axis=-1, keepdims=True)
    spread = lax.rsqrt(jnp.mean(center * center, axis=-1, keepdims=True) + EPSILON)
    return center * spread, spread


def key_spans(tokens, reach):
    spans = []
    for start in range(0, tokens, LANES):
        low = max(0, start - reach) // 16 * 16
        high = min(tokens, -(-(start + LANES + reach) // 16) * 16)
        spans.append((start, low, high))
    return spans


def split_rows(mine_ref, other_ref, slot, src_ref, core):
    pieces, count, rows = mine_ref.shape[1:4]
    for z in range(count):
        for dst, which in ((mine_ref, core), (other_ref, 1 - core)):
            start = pl.multiple_of((2 * z + which) * pieces * rows, 8)
            block = src_ref[pl.ds(start, pieces * rows), :].astype(BF)
            for p in range(pieces):
                dst[slot, p, z] = block[p * rows : (p + 1) * rows]


def forward_kernel(reach, x_ref, gain_ref, bias_ref, wqkv_hbm, *rest):
    outs, (wqkv_ref, mine_ref, other_ref, q_ref, kt_ref, v_ref, prob_ref, mixed_ref, n_ref, k_ref, t_ref, sem) = rest[:7], rest[7:]
    tokens, width = x_ref.shape
    core = lax.axis_index("inner") & 1
    loads = []
    for part in range(3):
        cols = pl.ds(part * width, width)
        loads.append(pltpu.make_async_copy(wqkv_hbm.at[:, cols], wqkv_ref.at[part], sem.at[part]))
        loads[-1].start()
    sources = (mine_ref, other_ref, q_ref, kt_ref, v_ref, prob_ref, mixed_ref)
    stores = {i: pltpu.make_async_copy(sources[i], outs[i], sem.at[3 + i]) for i in (0, 1, 2, 3, 4, 6)}
    unit, _ = row_stats(x_ref[...].astype(F32))
    normed = unit * gain_ref[...]
    n_ref[...] = normed.astype(BF)
    t_ref[...] = normed.T
    split_rows(mine_ref, other_ref, 0, t_ref, core)
    step = 256
    for part, (dst, factor) in enumerate(((q_ref, SCALE), (k_ref, 1.0), (v_ref, 1.0))):
        loads[part].wait()
        for i in range(width // step):
            cols = slice(i * step, (i + 1) * step)
            dst[:, cols] = (mm(n_ref[...], wqkv_ref[part, :, cols]) * factor).astype(BF)
        if part != 1:
            stores[2 + part].start()

    def prob_store(i):
        heads = pl.ds(2 * i, 2)
        return pltpu.make_async_copy(prob_ref.at[heads], outs[5].at[heads], sem.at[10 + i])

    def pair(i, carry):
        cols = pl.ds(pl.multiple_of(i * 128, 128), 128)
        q2, k2, v2 = q_ref[:, cols], k_ref[:, cols], v_ref[:, cols]
        kt_ref[cols, :] = (k2.astype(F32).T * SCALE).astype(BF)
        v2t = v2.astype(F32).T.astype(BF)
        for half in range(2):
            span = slice(half * 64, half * 64 + 64)
            for b, (start, low, high) in enumerate(key_spans(tokens, reach)):
                block = slice(start, start + LANES)
                scores = mm_t(k2[low:high, span], q2[block, span]) + bias_ref[low:high, block]
                grown = jnp.exp(scores - jnp.max(scores, axis=0, keepdims=True))
                probs = grown * (1.0 / jnp.sum(grown, axis=0, keepdims=True))
                prob_ref[2 * i + half, b, : high - low] = probs
                rows = pl.ds(pl.multiple_of(i * 128 + half * 64, 64), 64)
                mixt = mm(v2t[span, low:high], probs.astype(BF))
                t_ref[rows, block] = mixt
        prob_store(i).start()
        return carry

    lax.fori_loop(0, HEADS // 2, pair, 0)
    stores[3].start()
    mixed_ref[...] = t_ref[...].T.astype(BF)
    stores[6].start()
    split_rows(mine_ref, other_ref, 1, t_ref, core)
    stores[0].start()
    stores[1].start()

    def finish(i, carry):
        prob_store(i).wait()
        return carry

    lax.fori_loop(0, HEADS // 2, finish, 0)
    for store in stores.values():
        store.wait()


def out_kernel(frames_ref, mixed_ref, wout_ref, out_ref):
    out_ref[...] = (frames_ref[...].astype(F32) + mm(mixed_ref[...], wout_ref[...])).astype(BF)


def copy_kernel(src_ref, dst_ref):
    dst_ref[...] = src_ref[...]


def backward_kernel(reach, cot_ref, *rest):
    sources, (dqkv_hbm, blocks_hbm), rest = rest[:5], rest[5:7], rest[7:]
    wout_ref, q_ref, kt_ref, v_ref, prob_ref, dqkv_ref, blocks_ref, gm_ref, dqt_ref, sem = rest
    tokens, width = cot_ref.shape
    targets = (wout_ref, q_ref, kt_ref, v_ref, prob_ref)
    loads = [pltpu.make_async_copy(src, dst, sem.at[i]) for i, (src, dst) in enumerate(zip(sources, targets))]
    for load in loads:
        load.start()
    loads[0].wait()
    gm_ref[...] = mm_t(cot_ref[...], wout_ref[...]).astype(BF)
    for load in loads[1:]:
        load.wait()
    spans = key_spans(tokens, reach)

    def widen(parts):
        cols = []
        for part, (_, low, high) in zip(parts, spans):
            rows = [jnp.zeros((low, LANES), BF)] if low else []
            rows += [part]
            rows += [jnp.zeros((tokens - high, LANES), BF)] if high < tokens else []
            cols.append(jnp.concatenate(rows, 0) if len(rows) > 1 else part)
        return jnp.concatenate(cols, 1) if len(cols) > 1 else cols[0]

    def pair(i, carry):
        cols = pl.ds(pl.multiple_of(i * 128, 128), 128)
        q2, g2, v2, kt2 = q_ref[:, cols], gm_ref[:, cols], v_ref[:, cols], kt_ref[cols, :]
        dks, dvs = [], []
        for half in range(2):
            span = slice(half * 64, half * 64 + 64)
            weights, grads = [], []
            for b, (start, low, high) in enumerate(spans):
                block = slice(start, start + LANES)
                probs = prob_ref[2 * i + half, b, : high - low]
                dots = mm_t(v2[low:high, span], g2[block, span])
                centre = jnp.sum(probs * dots, axis=0, keepdims=True)
                sgrad = (probs * (dots - centre)).astype(BF)
                rows = pl.ds(pl.multiple_of(i * 128 + half * 64, 64), 64)
                dqt_ref[rows, block] = mm(kt2[span, low:high], sgrad)
                weights.append(probs.astype(BF))
                grads.append(sgrad)
            dks.append(mm(widen(grads), q2[:, span]))
            dvs.append(mm(widen(weights), g2[:, span]))
        dqkv_ref[:, pl.ds(pl.multiple_of(width + i * 128, 128), 128)] = jnp.concatenate(dks, 1).astype(BF)
        dqkv_ref[:, pl.ds(pl.multiple_of(2 * width + i * 128, 128), 128)] = jnp.concatenate(dvs, 1).astype(BF)
        return carry

    lax.fori_loop(0, HEADS // 2, pair, 0)
    dqkv_ref[:, :width] = dqt_ref[...].T.astype(BF)
    whole = pltpu.make_async_copy(dqkv_ref, dqkv_hbm, sem.at[5])
    runs = blocks_ref.shape[0]
    wide, thin = 3 * width // runs, width // runs
    stores = []
    for j in range(runs):
        blocks_ref[j, :, :wide] = dqkv_ref[:, j * wide : (j + 1) * wide]
        blocks_ref[j, :, wide:] = cot_ref[:, j * thin : (j + 1) * thin]
        stores.append(pltpu.make_async_copy(blocks_ref.at[j], blocks_hbm.at[j], sem.at[6 + j]))
        stores[-1].start()
    whole.start()
    for store in stores + [whole]:
        store.wait()


def norm_kernel(x_ref, cot_ref, gain_ref, dqkv_ref, wqkv_ref, fgrad_ref, gpart_ref):
    unit, spread = row_stats(x_ref[...].astype(F32))
    ngrad = mm_t(dqkv_ref[...], wqkv_ref[...])
    gpart_ref[...] = jnp.sum(ngrad * unit, axis=0, keepdims=True)
    scaled = ngrad * gain_ref[...]
    mean_one = jnp.mean(scaled, axis=-1, keepdims=True)
    second = jnp.mean(scaled * unit, axis=-1, keepdims=True)
    fgrad_ref[...] = (cot_ref[...].astype(F32) + spread * (scaled - mean_one - unit * second)).astype(BF)


def squeeze_bits(value, bits):
    for b in sorted(bits, reverse=True):
        value = (value >> (b + 1) << b) | (value & ((1 << b) - 1))
    return value


def spread_bits(value, bits):
    for b in sorted(bits):
        value = (value >> b << (b + 1)) | (value & ((1 << b) - 1))
    return value


def bit_orders(runs):
    bits = list(range(runs.bit_length() - 1))
    return bits, bits[1:] + bits[:1]


def by_core(values):
    return jnp.where(lax.axis_index("inner") & 1 == 0, *values)


def run_of(runs, stage, n, send):
    me = lax.axis_index("tm")
    found = []
    for order in bit_orders(runs):
        past, bit = order[:stage], order[stage]
        run = spread_bits(n, past + [bit])
        for b in past:
            run = run | (me & (1 << b))
        found.append(run | ((me ^ (1 << bit) if send else me) & (1 << bit)))
    return by_core(found)


def place_of(runs, stage, run):
    return by_core([squeeze_bits(run, order[: stage + 1]) for order in bit_orders(runs)])


def exchange(value, runs, inner, stage):
    perm = []
    for t in range(runs):
        for i in range(inner):
            t2 = t ^ (1 << bit_orders(runs)[i & 1][stage])
            perm.append((t * inner + i, t2 * inner + i))
    return lax.ppermute(value, AXES, perm)


def to_partner(value, inner):
    return lax.ppermute(value, "inner", [(i, i ^ 1) for i in range(inner)])


def product_kernel(runs, pieces, send, mine_ref, other_ref, d_ref, d_other_ref, *out_refs):
    _, _, count, rows, tokens = mine_ref.shape
    for piece, out_ref in zip(pieces, out_refs):
        wide = out_ref.shape[3] * 3 // 4
        for n in range(out_ref.shape[0]):
            run = run_of(runs, 0, n, send)
            totals = []
            for slot, cols in ((0, slice(0, wide)), (1, slice(wide, None))):
                left = mine_ref[slot, piece].reshape(count * rows, tokens)
                right = other_ref[slot, piece].reshape(count * rows, tokens)
                totals.append(mm(left, d_ref[run][:, cols]) + mm(right, d_other_ref[run][:, cols]))
            total = jnp.concatenate(totals, 1).astype(out_ref.dtype)
            for z in range(count):
                out_ref[n, z] = total[z * rows : (z + 1) * rows]


def partial_sum(runs, run, keep_ref, got_refs, z):
    total = keep_ref[place_of(runs, 0, run), z]
    for stage, ref in enumerate(got_refs):
        total = total + ref[place_of(runs, stage, run), z].astype(F32)
    return total


def stage_kernel(runs, stage, keep_ref, *rest):
    got_refs, out_ref = rest[:-1], rest[-1]
    for n in range(out_ref.shape[0]):
        run = run_of(runs, stage, n, True)
        for z in range(out_ref.shape[1]):
            out_ref[n, z] = partial_sum(runs, run, keep_ref, got_refs, z).astype(BF)


def rows_kernel(runs, keep_ref, *rest):
    stages = runs.bit_length() - 1
    got_refs, own_ref, send_refs = rest[:stages], rest[stages], rest[stages + 1 :]
    count = keep_ref.shape[1]
    me, run = lax.axis_index("inner") >> 1, lax.axis_index("tm")
    for k, ref in enumerate(send_refs):
        ref[...] = partial_sum(runs, run, keep_ref, got_refs, lax.rem(me + k + 1, count)).astype(BF)
    own_ref[...] = partial_sum(runs, run, keep_ref, got_refs, me)


def last_kernel(inv_root, pieces, *rest):
    got, (q_ref, o_ref) = rest[:-2], rest[-2:]
    rows, wide = q_ref.shape[0] // pieces, q_ref.shape[1]
    each = len(got) // pieces
    for p in range(pieces):
        own_ref, *others = got[p * each : (p + 1) * each]
        total = own_ref[...]
        for ref in others:
            total = total + ref[...].astype(F32)
        total = total * inv_root
        q_ref[p * rows : (p + 1) * rows] = total[:, :wide]
        o_ref[p * rows : (p + 1) * rows] = total[:, wide:]


def reduce_weights(mine, other, d, d_other, runs, inner, inv_root):
    sds = jax.ShapeDtypeStruct
    _, pieces, count, rows, tokens = mine.shape
    lanes = d.shape[2]
    stages = runs.bit_length() - 1
    shape = (runs // 2, count, rows, lanes)
    flops = 4 * count * rows * tokens * lanes * (runs // 2)
    args = (mine, other, d, d_other)
    got = [[] for _ in range(pieces)]
    for p in range(pieces):
        send = call(functools.partial(product_kernel, runs, (p,), True), (sds(shape, BF),), *args, flops=flops)[0]
        got[p].append(exchange(send, runs, inner, 0))
    keep = call(functools.partial(product_kernel, runs, tuple(range(pieces)), False), (sds(shape, F32),) * pieces, *args, flops=pieces * flops)
    for stage in range(1, stages):
        shape = (shape[0] // 2,) + shape[1:]
        for p in range(pieces):
            send = call(functools.partial(stage_kernel, runs, stage), sds(shape, BF), keep[p], *got[p])
            got[p].append(exchange(send, runs, inner, stage))
    last = []
    block = (rows, lanes)
    for p in range(pieces):
        own, *sends = call(functools.partial(rows_kernel, runs), (sds(block, F32),) + (sds(block, BF),) * (count - 1), keep[p], *got[p])
        last.append(own)
        for k, send in enumerate(sends):
            last.append(lax.ppermute(send, "inner", [(i, (i + 2 * (k + 1)) % inner) for i in range(inner)]))
    out = (sds((pieces * rows, lanes * 3 // 4), F32), sds((pieces * rows, lanes // 4), F32))
    return call(functools.partial(last_kernel, inv_root, pieces), out, *last)


def to_tubes(rows, count):
    held, patches, width = rows.shape
    parts = jnp.moveaxis(rows.reshape(held, count, patches // count, width), 1, 0)
    parts = lax.all_to_all(parts, AXES, split_axis=0, concat_axis=0, tiled=True)
    return parts.reshape(-1, width)


def to_frames(tubes, count, held, patches):
    width = tubes.shape[1]
    parts = tubes.reshape(count, held, patches // count, width)
    parts = lax.all_to_all(parts, AXES, split_axis=0, concat_axis=0, tiled=True)
    return jnp.moveaxis(parts, 0, 1).reshape(held, patches, width)


def window_bias(all_frames, patches, clip_len):
    tokens = all_frames * patches
    key = lax.broadcasted_iota(jnp.int32, (tokens, tokens), 0)
    query = lax.broadcasted_iota(jnp.int32, (tokens, tokens), 1)
    key_f, query_f = key // patches, query // patches
    inside = (key % patches == query % patches) & (abs(key_f - query_f) <= WINDOW)
    inside = inside & (key_f // clip_len == query_f // clip_len)
    return jnp.where(inside, 0.0, -1e30).astype(F32)


def shards(frames, norm_gain, w_qkv, w_out, cotangent):
    held, patches, width = frames.shape
    runs, inner = lax.axis_size("tm"), lax.axis_size("inner")
    count = runs * inner
    all_frames = held * count
    clip_len = min(CLIP_MAX, all_frames)
    inv_root = 1.0 / math.sqrt(all_frames * patches)
    tokens = all_frames * patches // count
    reach = WINDOW * (patches // count)
    gain = norm_gain.reshape(1, width)
    bias = window_bias(all_frames, patches // count, clip_len)
    spans = key_spans(tokens, reach)
    longest = max(high - low for _, low, high in spans)
    sds = jax.ShapeDtypeStruct
    vmem = pltpu.VMEM

    x = to_tubes(frames, count)
    cot = to_tubes(cotangent, count)
    halves = ((2, PIECES, inner // 2, width // inner // PIECES, tokens), BF)
    flat, turned = ((tokens, width), BF), ((width, tokens), BF)
    probs = ((HEADS, len(spans), longest, LANES), F32)
    made = (halves, halves, flat, turned, flat, probs, flat)
    mine, other, q, kt, v, prob, mixed = call(
        functools.partial(forward_kernel, reach),
        tuple(sds(*each) for each in made),
        x,
        gain,
        bias,
        w_qkv,
        scratch=[vmem((3, width, width), BF), *(vmem(*each) for each in made), vmem(*flat), vmem(*flat), vmem((width, tokens), F32)],
        flops=2 * tokens * width * 4 * width,
        raw_in=(3,),
        raw_out=range(7),
        copies=10 + HEADS // 2,
    )
    theirs = to_partner(other, inner)
    mixed_back = to_frames(mixed, count, held, patches)
    block_out = call(out_kernel, sds((held * patches, width), BF), frames.reshape(-1, width), mixed_back.reshape(-1, width), w_out, flops=2 * tokens * width * width)
    block_out = block_out.reshape(held, patches, width)
    made = (((tokens, 3 * width), BF), ((runs, tokens, 4 * width // runs), BF))
    dqkv, blocks = call(
        functools.partial(backward_kernel, reach),
        tuple(sds(*each) for each in made),
        cot,
        w_out,
        q,
        kt,
        v,
        prob,
        scratch=[*(vmem(*each) for each in (((width, width), BF), flat, turned, flat, probs) + made), vmem(*flat), vmem((width, tokens), F32)],
        flops=2 * tokens * width * 4 * width,
        raw_in=range(1, 6),
        raw_out=range(2),
        copies=6 + runs,
    )
    blocks_other = to_partner(blocks, inner)
    fgrad, gpart = call(
        norm_kernel,
        (sds((tokens, width), BF), sds((1, width), F32)),
        x,
        cot,
        gain,
        dqkv,
        w_qkv,
        flops=2 * tokens * width * 3 * width,
    )
    frames_grad = to_frames(fgrad, count, held, patches)
    frames_grad = call(copy_kernel, sds((held * patches, width), BF), frames_grad.reshape(-1, width)).reshape(held, patches, width)
    qkv_grad, out_grad = reduce_weights(mine, theirs, blocks, blocks_other, runs, inner, inv_root)
    shares = jnp.broadcast_to(gpart.reshape(1, inner, width // inner), (runs, inner, width // inner))
    shares = lax.all_to_all(shares.reshape(count, 1, -1), AXES, split_axis=0, concat_axis=0, tiled=True)
    gain_grad = jnp.sum(shares, axis=(0, 1)) * inv_root
    return block_out, frames_grad, qkv_grad, out_grad, gain_grad


def solution(mesh):
    in_specs = (P(AXES, None, None), P(), P(), P(), P(AXES, None, None))
    out_specs = (P(AXES, None, None), P(AXES, None, None), P("inner", "tm"), P("inner", "tm"), P("inner"))
    return jax.shard_map(shards, mesh=mesh, in_specs=in_specs, out_specs=out_specs, check_vma=False)
```

time: 123 us -> 117 us (0.951)
  Pallas kernels: 27.7 us -> 43.8 us
  local copies, waits for them, and re-layouts: 19 us -> 3.75 us
  waiting for transfers between devices: 19.5 us -> 11.4 us
  starting transfers between devices: 19.2 us -> 22.9 us
  blocking collectives: 34.6 us -> 31.4 us
    pallas_call x10 -> x13, Pallas kernels: 27.7 us -> 43.8 us  [call(): pl.pallas_call(kernel, out_shape=placed if isinstance(out_shape, (tuple,...]
    unnamed x55 -> x30, local copies, waits for them, and re-layouts: 18.9 us -> 3.67 us
    all_to_all x2, waiting for transfers between devices: 12.1 us -> 5.48 us  [to_frames(): parts = lax.all_to_all(parts, AXES, split_axis=0, concat_axis=0, tiled=True)]
    ppermute x3 -> x6, starting transfers between devices: 4.94 us -> 9.02 us  [reduce_weights(): lax.ppermute(send, 'inner', [(i, (i + 2 * (k + 1)) % inner) for i in rang...]
    ppermute x3 -> x2, waiting for transfers between devices: 3.34 us -> 0.01 us  [to_partner(): return lax.ppermute(value, 'inner', [(i, i ^ 1) for i in range(inner)])]
    all_to_all x1, blocking collectives: 13.8 us -> 10.7 us  [shards(): lax.all_to_all(shares.reshape(count, 1, -1), AXES, split_axis=0, concat_a...]
    all_to_all x1, waiting for transfers between devices: 0.01 us -> 2.17 us  [to_tubes(): parts = lax.all_to_all(parts, AXES, split_axis=0, concat_axis=0, tiled=True)]
    ppermute x3 -> x6, waiting for transfers between devices: 1.53 us -> 0.15 us  [reduce_weights(): lax.ppermute(send, 'inner', [(i, (i + 2 * (k + 1)) % inner) for i in rang...]
  transfers between devices with their start and end apart: 11 -> 15, of which waited for: 6 -> 4; matrix products, arithmetic and copies ran while one was open for 1% -> 1% of each run, Pallas kernels for 15% -> 28%
where the time goes in v4:
time: 117 us; the launch traced here: 116 us
  Pallas kernels  43.8 us (37%)
  blocking collectives  31.4 us (27%)
  starting transfers between devices  22.9 us (20%)
  waiting for transfers between devices  11.4 us (10%)
  local copies, waits for them, and re-layouts  3.75 us (3%)
  other arithmetic  1.55 us (1%)
    pallas_call x13, Pallas kernels, call(): pl.pallas_call(kernel, out_shape=placed if isinstance(out_shape, (tuple,...  43.8 us
    all_to_all x1, blocking collectives, to_tubes(): parts = lax.all_to_all(parts, AXES, split_axis=0, concat_axis=0, tiled=True)  20.8 us
    all_to_all x1, blocking collectives, shards(): lax.all_to_all(shares.reshape(count, 1, -1), AXES, split_axis=0, concat_a...  10.7 us
    ppermute x6, starting transfers between devices, reduce_weights(): lax.ppermute(send, 'inner', [(i, (i + 2 * (k + 1)) % inner) for i in rang...  9.02 us
    all_to_all x2, starting transfers between devices, to_frames(): parts = lax.all_to_all(parts, AXES, split_axis=0, concat_axis=0, tiled=True)  6.61 us
    all_to_all x2, waiting for transfers between devices, to_frames(): parts = lax.all_to_all(parts, AXES, split_axis=0, concat_axis=0, tiled=True)  5.48 us
    ppermute x4, starting transfers between devices, exchange(): return lax.ppermute(value, AXES, perm)  4.05 us
    unnamed x30, local copies, waits for them, and re-layouts  3.67 us
  transfers between devices with their start and end apart: 15, of which 4 were waited for; matrix products, arithmetic and copies ran while one was open for 1% of the time, Pallas kernels for 28%

profile of v4, /device:TPU:0, one launch (start us, length us, event | category | flops | bytes accessed | tf_op | source)
XLA Modules:
  0.0 115.6 jit_solution(4282236028806262095)
XLA Ops:
  0.6 20.8 %all_to_all.25 = bf16[32,1,8,768]{3,2,1,0:T(8,128)(2,1)S(1)} all-to-all(bf16[32,1,8,768]{3,2,1,0:T(8,128)(2,1)} %bitcast.18), channel_id=1, replica_groups=mesh['tm'=4,'inner'=8] {'tm','inner'}, dimensions={0} | all-to-all | bytes 786432 | tf_op jit(solution)/shard_map/all_to_all | solution.py:368
  21.4 2.6 %all-to-all-start.2 = ((bf16[32,1,8,768]{3,2,1,0:T(8,128)(2,1)}), bf16[32,1,8,768]{3,2,1,0:T(8,128)(2,1)S(1)}, u32[]{:S(2)}, u32[]{:S(2)}) async-start(bf16[32,1,8,768]{3,2,1,0:T(8,128)(2,1)} %bitcast.23), calls=%async_computation.2 | async-start | bytes 786432 | tf_op jit(solution)/shard_map/all_to_all | solution.py:368
  24.4 10.9 %shard_map.92 = (bf16[2,2,4,48,256]{4,3,2,1,0:T(8,128)(2,1)}, bf16[2,2,4,48,256]{4,3,2,1,0:T(8,128)(2,1)}, bf16[256,768]{1,0:T(8,128)(2,1)}, bf16[768,256]{1,0:T...) custom-call(bf16[256,768]{1,0:T(8,128)(2,1)S(1)} %bitcast.20, ...), custom_call_target="tpu_custom_call" | custom-call | flops 1207959552 | bytes 8522752 | tf_op jit(solution)/shard_map/pallas_call | solution.py:50
  35.3 2.2 %all-to-all-done.2 = bf16[32,1,8,768]{3,2,1,0:T(8,128)(2,1)S(1)} async-done(((bf16[32,1,8,768]{3,2,1,0:T(8,128)(2,1)}), bf16[32,1,8,768]{3,2,1,0:T(8,128)(2,1)S(1)}, u32[]{:S(2)}, u32[]{:S(2)}) %all-to-all-start.2) | async-done | bytes 393248 | tf_op jit(solution)/shard_map/all_to_all | solution.py:368
  37.4 10.2 %shard_map.94 = (bf16[256,2304]{1,0:T(8,128)(2,1)}, bf16[4,256,768]{2,1,0:T(8,128)(2,1)}) custom-call(bf16[256,768]{1,0:T(8,128)(2,1)S(1)} %bitcast.16, bf16[768,768]{1,0:T(8,128)(2,1)} %rest_0_.1, bf16[256,768]{1,0:T(8,128)(2,1)} %get-tuple-element.29.rest_1_, bf16[768,256]{1,0:T(8,128)(2,1)} %get-tuple-element.30.rest_2_, ...), custom_call_target="tpu_custom_call" | custom-call | flops 1207959552 | bytes 7471104 | tf_op jit(solution)/shard_map/pallas_call | solution.py:50
  48.2 1.3 %copy-done.11 = bf16[256,2304]{1,0:T(8,128)(2,1)S(1)} copy-done((bf16[256,2304]{1,0:T(8,128)(2,1)S(1)}, bf16[256,2304]{1,0:T(8,128)(2,1)}, u32[]{:S(2)}) %copy-start.11) | copy-done | bytes 1179672
  49.5 2.2 %shard_map.95 = (bf16[256,768]{1,0:T(8,128)(2,1)}, f32[1,768]{1,0:T(1,128)}) custom-call(bf16[256,768]{1,0:T(8,128)(2,1)S(1)} %bitcast.21, bf16[256,768]{1,0:T(8,128)(2,1)S(1)} %bitcast.17, f32[1,768]{1,0:T(1,128)S(1)} %reshape.41.gain_ref, bf16[256,2304]{1,0:T(8,128)(2,1)S(1)} %copy-done.11, bf16[768,2304]{1,0:T(8,128)(2,1)S(1)} %copy-done.5), custom_call_target="tpu_custom_call" | custom-call | flops 905969664 | bytes 5904384 | tf_op jit(solution)/shard_map/pallas_call | solution.py:50
  52.5 10.7 %all_to_all.26 = f32[32,1,96]{2,1,0:T(1,128)S(1)} all-to-all(f32[32,1,96]{2,1,0:T(1,128)S(1)} %bitcast.27), channel_id=1, replica_groups=mesh['tm'=4,'inner'=8] {'tm','inner'}, dimensions={0} | all-to-all | bytes 24576 | tf_op jit(solution)/shard_map/all_to_all | solution.py:459
  63.1 3.3 %all-to-all-start.3 = ((bf16[32,1,8,768]{3,2,1,0:T(8,128)(2,1)}), bf16[32,1,8,768]{3,2,1,0:T(8,128)(2,1)}, u32[]{:S(2)}, u32[]{:S(2)}) async-start(bf16[32,1,8,768]{3,2,1,0:T(8,128)(2,1)} %bitcast.26), calls=%async_computation.3 | async-start | bytes 786432 | tf_op jit(solution)/shard_map/all_to_all | solution.py:375
  66.5 1.0 copy-done.6
  67.5 2.4 %shard_map.98 = bf16[2,4,48,768]{3,2,1,0:T(8,128)(2,1)} custom-call(bf16[2,2,4,48,256]{4,3,2,1,0:T(8,128)(2,1)S(1)} %copy-done.6, bf16[2,2,4,48,256]{4,3,2,1,0:T(8,128)(2,1)} %collective-permute-done.other_ref, bf16[4,256,768]{2,1,0:T(8,128)(2,1)S(1)} %copy-done, bf16[4,256,768]{2,1,0:T(8,128)(2,1)S(1)} %collective-permute-done.1.d_other_ref), custom_call_target="tpu_custom_call" | custom-call | flops 301989888 | bytes 4521984 | tf_op jit(solution)/shard_map/pallas_call | solution.py:50
  69.9 1.6 %collective-permute-start.2 = (bf16[2,4,48,768]{3,2,1,0:T(8,128)(2,1)}, bf16[2,4,48,768]{3,2,1,0:T(8,128)(2,1)}, u32[]{:S(2)}, u32[]{:S(2)}) collective-permute-start(bf16[2,4,48,768]{3,2,1,0:T(8,128)(2,1)} %shard_map.98), channel_id=1, source_target_pairs={{0,8},{1,17},{2,10},{3,19},{4,12},{5,21},{6,14},{7,23},{8,0},{9,25... | collective-permute-start | bytes 1769480 | tf_op jit(solution)/shard_map/ppermute | solution.py:274
  71.5 2.5 %shard_map.101 = bf16[2,4,48,768]{3,2,1,0:T(8,128)(2,1)} custom-call(bf16[2,2,4,48,256]{4,3,2,1,0:T(8,128)(2,1)S(1)} %copy-done.6, bf16[2,2,4,48,256]{4,3,2,1,0:T(8,128)(2,1)} %collective-permute-done.other_ref, bf16[4,256,768]{2,1,0:T(8,128)(2,1)S(1)} %copy-done, bf16[4,256,768]{2,1,0:T(8,128)(2,1)S(1)} %collective-permute-done.1.d_other_ref), custom_call_target="tpu_custom_call" | custom-call | flops 301989888 | bytes 4521984 | tf_op jit(solution)/shard_map/pallas_call | solution.py:50
  74.4 5.5 %all-to-all-done.3 = bf16[32,1,8,768]{3,2,1,0:T(8,128)(2,1)} async-done(((bf16[32,1,8,768]{3,2,1,0:T(8,128)(2,1)}), bf16[32,1,8,768]{3,2,1,0:T(8,128)(2,1)}, u32[]{:S(2)}, u32[]{:S(2)}) %all-to-all-start.3) | async-done | bytes 393248 | tf_op jit(solution)/shard_map/all_to_all | solution.py:375
  79.9 3.3 %all-to-all-start.1 = ((bf16[32,1,8,768]{3,2,1,0:T(8,128)(2,1)}), bf16[32,1,8,768]{3,2,1,0:T(8,128)(2,1)}, u32[]{:S(2)}, u32[]{:S(2)}) async-start(bf16[32,1,8,768]{3,2,1,0:T(8,128)(2,1)} %bitcast.24), calls=%async_computation.1 | async-start | bytes 786432 | tf_op jit(solution)/shard_map/all_to_all | solution.py:375
  83.2 3.3 %shard_map.97 = (f32[2,4,48,768]{3,2,1,0:T(8,128)}, f32[2,4,48,768]{3,2,1,0:T(8,128)}) custom-call(bf16[2,2,4,48,256]{4,3,2,1,0:T(8,128)(2,1)S(1)} %copy-done.7, bf16[2,2,4,48,256]{4,3,2,1,0:T(8,128)(2,1)} %collective-permute-done.other_ref, bf16[4,256,768]{2,1,0:T(8,128)(2,1)S(1)} %copy-done, bf16[4,256,768]{2,1,0:T(8,128)(2,1)S(1)} %collective-permute-done.1.d_other_ref), custom_call_target="tpu_custom_call" | custom-call | flops 603979776 | bytes 6291456 | tf_op jit(solution)/shard_map/pallas_call | solution.py:50
  86.5 1.4 %copy-done.3 = f32[2,4,48,768]{3,2,1,0:T(8,128)S(1)} copy-done((f32[2,4,48,768]{3,2,1,0:T(8,128)S(1)}, f32[2,4,48,768]{3,2,1,0:T(8,128)}, u32[]{:S(2)}) %copy-start.3) | copy-done | bytes 1179672
  87.8 1.9 %shard_map.99 = bf16[1,4,48,768]{3,2,1,0:T(8,128)(2,1)} custom-call(f32[2,4,48,768]{3,2,1,0:T(8,128)S(1)} %copy-done.3, bf16[2,4,48,768]{3,2,1,0:T(8,128)(2,1)} %collective-permute-done.2.rest_0_), custom_call_target="tpu_custom_call" | custom-call | bytes 2064384 | tf_op jit(solution)/shard_map/pallas_call | solution.py:50
  89.8 1.6 %collective-permute-start.3 = (bf16[1,4,48,768]{3,2,1,0:T(8,128)(2,1)}, bf16[1,4,48,768]{3,2,1,0:T(8,128)(2,1)S(1)}, u32[]{:S(2)}, u32[]{:S(2)}) collective-permute-start(bf16[1,4,48,768]{3,2,1,0:T(8,128)(2,1)} %shard_map.99), channel_id=1, source_target_pairs={{0,16},{1,9},{2,18},{3,11},{4,20},{5,13},{6,22},{7,15},{8,24},{9,1... | collective-permute-start | bytes 884744 | tf_op jit(solution)/shard_map/ppermute | solution.py:274
  91.4 1.8 %shard_map.102 = bf16[1,4,48,768]{3,2,1,0:T(8,128)(2,1)} custom-call(f32[2,4,48,768]{3,2,1,0:T(8,128)S(1)} %copy-done.2, bf16[2,4,48,768]{3,2,1,0:T(8,128)(2,1)} %collective-permute-done.7.rest_0_), custom_call_target="tpu_custom_call" | custom-call | bytes 2064384 | tf_op jit(solution)/shard_map/pallas_call | solution.py:50
  93.7 3.6 %collective-permute-done.3.rest_1_ = bf16[1,4,48,768]{3,2,1,0:T(8,128)(2,1)S(1)} collective-permute-done((bf16[1,4,48,768]{3,2,1,0:T(8,128)(2,1)}, bf16[1,4,48,768]{3,2,1,0:T(8,128)(2,1)S(1)}, u32[]{:S(2)}, u32[]{:S(2)}) %collective-permute-start.3) | collective-permute-done | bytes 294944 | tf_op jit(solution)/shard_map/ppermute | solution.py:274
  97.3 1.9 %shard_map.100 = (f32[48,768]{1,0:T(8,128)}, bf16[48,768]{1,0:T(8,128)(2,1)}, bf16[48,768]{1,0:T(8,128)(2,1)}, bf16[48,768]{1,0:T(8,128)(2,1)}) custom-call(f32[2,4,48,768]{3,2,1,0:T(8,128)S(1)} %copy-done.4, bf16[2,4,48,768]{3,2,1,0:T(8,128)(2,1)} %collective-permute-done.2.rest_0_, bf16[1,4,48,768]{3,2,1,0:T(8,128)(2,1)S(1)} %collective-permute-done.3.rest_1_), custom_call_target="tpu_custom_call" | custom-call | bytes 2433024 | tf_op jit(solution)/shard_map/pallas_call | solution.py:50
  99.1 1.6 %collective-permute-start.4 = (bf16[48,768]{1,0:T(8,128)(2,1)}, bf16[48,768]{1,0:T(8,128)(2,1)S(1)}, u32[]{:S(2)}, u32[]{:S(2)}) collective-permute-start(bf16[48,768]{1,0:T(8,128)(2,1)} %get-tuple-element.40), channel_id=1, source_target_pairs={{0,2},{1,3},{2,4},{3,5},{4,6},{5,7},{6,0},{7,1},{8,10},{9,11},{10,... | collective-permute-start | bytes 221192 | tf_op jit(solution)/shard_map/ppermute | solution.py:360
  100.8 2.3 %collective-permute-start.5 = (bf16[48,768]{1,0:T(8,128)(2,1)}, bf16[48,768]{1,0:T(8,128)(2,1)S(1)}, u32[]{:S(2)}, u32[]{:S(2)}) collective-permute-start(bf16[48,768]{1,0:T(8,128)(2,1)} %get-tuple-element.41), channel_id=1, source_target_pairs={{0,4},{1,5},{2,6},{3,7},{4,0},{5,1},{6,2},{7,3},{8,12},{9,13},{10,... | collective-permute-start | bytes 221192 | tf_op jit(solution)/shard_map/ppermute | solution.py:360
  103.1 1.3 %collective-permute-start.6 = (bf16[48,768]{1,0:T(8,128)(2,1)}, bf16[48,768]{1,0:T(8,128)(2,1)S(1)}, u32[]{:S(2)}, u32[]{:S(2)}) collective-permute-start(bf16[48,768]{1,0:T(8,128)(2,1)} %get-tuple-element.42), channel_id=1, source_target_pairs={{0,6},{1,7},{2,0},{3,1},{4,2},{5,3},{6,4},{7,5},{8,14},{9,15},{10,... | collective-permute-start | bytes 221192 | tf_op jit(solution)/shard_map/ppermute | solution.py:360
  104.4 1.8 %shard_map.103 = (f32[48,768]{1,0:T(8,128)}, bf16[48,768]{1,0:T(8,128)(2,1)}, bf16[48,768]{1,0:T(8,128)(2,1)}, bf16[48,768]{1,0:T(8,128)(2,1)}) custom-call(f32[2,4,48,768]{3,2,1,0:T(8,128)S(1)} %copy-done.2, bf16[2,4,48,768]{3,2,1,0:T(8,128)(2,1)} %collective-permute-done.7.rest_0_, bf16[1,4,48,768]{3,2,1,0:T(8,128)(2,1)S(1)} %collective-permute-done.8.rest_1_), custom_call_target="tpu_custom_call" | custom-call | bytes 2433024 | tf_op jit(solution)/shard_map/pallas_call | solution.py:50
  106.2 0.7 collective-permute-start.9
  106.9 0.7 collective-permute-start.10
  107.6 2.4 %collective-permute-start.11 = (bf16[48,768]{1,0:T(8,128)(2,1)}, bf16[48,768]{1,0:T(8,128)(2,1)S(1)}, u32[]{:S(2)}, u32[]{:S(2)}) collective-permute-start(bf16[48,768]{1,0:T(8,128)(2,1)} %get-tuple-element.47), channel_id=1, source_target_pairs={{0,6},{1,7},{2,0},{3,1},{4,2},{5,3},{6,4},{7,5},{8,14},{9,15},{10,... | collective-permute-start | bytes 221192 | tf_op jit(solution)/shard_map/ppermute | solution.py:360
  110.6 1.8 %shard_map.96 = bf16[256,768]{1,0:T(8,128)(2,1)} custom-call(bf16[256,768]{1,0:T(8,128)(2,1)} %bitcast.11.src_ref), custom_call_target="tpu_custom_call" | custom-call | bytes 786432 | tf_op jit(solution)/shard_map/pallas_call | solution.py:50
  112.4 2.2 %shard_map.93 = bf16[256,768]{1,0:T(8,128)(2,1)} custom-call(bf16[256,768]{1,0:T(8,128)(2,1)S(1)} %bitcast.19, bf16[256,768]{1,0:T(8,128)(2,1)} %bitcast.5.mixed_ref, bf16[768,768]{1,0:T(8,128)(2,1)S(1)} %copy-done.1), custom_call_target="tpu_custom_call" | custom-call | flops 301989888 | bytes 2359296 | tf_op jit(solution)/shard_map/pallas_call | solution.py:50
  114.8 0.8 shard_map.104
  (53 shorter events, 3.3 us)
Async XLA Ops:
  0.6 23.4 %copy-start.14 = (f32[768]{0:T(1024)S(1)}, f32[768]{0:T(1024)}, u32[]{:S(2)}) copy-start(f32[768]{0:T(1024)} %param.6) | copy-start | bytes 9220
  21.4 13.9 %copy-start.9 = (bf16[32,1,8,768]{3,2,1,0:T(8,128)(2,1)}, bf16[32,1,8,768]{3,2,1,0:T(8,128)(2,1)S(1)}, u32[]{:S(2)}) copy-start(bf16[32,1,8,768]{3,2,1,0:T(8,128)(2,1)S(1)} %all_to_all.25) | copy-start | bytes 1179652
  21.4 16.0 %all-to-all-start.2 = ((bf16[32,1,8,768]{3,2,1,0:T(8,128)(2,1)}), bf16[32,1,8,768]{3,2,1,0:T(8,128)(2,1)S(1)}, u32[]{:S(2)}, u32[]{:S(2)}) async-start(bf16[32,1,8,768]{3,2,1,0:T(8,128)(2,1)} %bitcast.23), calls=%async_computation.2 | async-start | bytes 786432 | tf_op jit(solution)/shard_map/all_to_all | solution.py:368
  37.4 10.8 %copy-start.5 = (bf16[768,2304]{1,0:T(8,128)(2,1)S(1)}, bf16[768,2304]{1,0:T(8,128)(2,1)}, u32[]{:S(2)}) copy-start(bf16[768,2304]{1,0:T(8,128)(2,1)} %wqkv_ref.1) | copy-start | bytes 10616836
  37.4 10.8 %copy-start.10 = (bf16[32,1,8,768]{3,2,1,0:T(8,128)(2,1)S(1)}, bf16[32,1,8,768]{3,2,1,0:T(8,128)(2,1)}, u32[]{:S(2)}) copy-start(bf16[32,1,8,768]{3,2,1,0:T(8,128)(2,1)} %copy-done.9) | copy-start | bytes 1179652
  47.7 18.8 %collective-permute-start.1 = (bf16[4,256,768]{2,1,0:T(8,128)(2,1)}, bf16[4,256,768]{2,1,0:T(8,128)(2,1)S(1)}, u32[]{:S(2)}, u32[]{:S(2)}) collective-permute-start(bf16[4,256,768]{2,1,0:T(8,128)(2,1)} %get-tuple-element.37.d_ref), channel_id=1, source_target_pairs={{0,1},{1,0},{2,3},{3,2},{4,5},{5,4},{6,7},{7,6},{8,9},{9,8},{10,11... | collective-permute-start | bytes 4718600 | tf_op jit(solution)/shard_map/ppermute | solution.py:278
  47.8 18.6 %collective-permute-start = (bf16[2,2,4,48,256]{4,3,2,1,0:T(8,128)(2,1)}, bf16[2,2,4,48,256]{4,3,2,1,0:T(8,128)(2,1)}, u32[]{:S(2)}, u32[]{:S(2)}) collective-permute-start(bf16[2,2,4,48,256]{4,3,2,1,0:T(8,128)(2,1)} %get-tuple-element.36), channel_id=1, source_target_pairs={{0,1},{1,0},{2,3},{3,2},{4,5},{5,4},{6,7},{7,6},{8,9},{9,8},{10,11... | collective-permute-start | bytes 1179656 | tf_op jit(solution)/shard_map/ppermute | solution.py:278
  48.2 1.3 %copy-start.11 = (bf16[256,2304]{1,0:T(8,128)(2,1)S(1)}, bf16[256,2304]{1,0:T(8,128)(2,1)}, u32[]{:S(2)}) copy-start(bf16[256,2304]{1,0:T(8,128)(2,1)} %get-tuple-element.33.dqkv_ref) | copy-start | bytes 3538948
  49.5 17.0 %copy-start = (bf16[4,256,768]{2,1,0:T(8,128)(2,1)S(1)}, bf16[4,256,768]{2,1,0:T(8,128)(2,1)}, u32[]{:S(2)}) copy-start(bf16[4,256,768]{2,1,0:T(8,128)(2,1)} %get-tuple-element.37.d_ref) | copy-start | bytes 4718596
  63.1 16.7 %all-to-all-start.3 = ((bf16[32,1,8,768]{3,2,1,0:T(8,128)(2,1)}), bf16[32,1,8,768]{3,2,1,0:T(8,128)(2,1)}, u32[]{:S(2)}, u32[]{:S(2)}) async-start(bf16[32,1,8,768]{3,2,1,0:T(8,128)(2,1)} %bitcast.26), calls=%async_computation.3 | async-start | bytes 786432 | tf_op jit(solution)/shard_map/all_to_all | solution.py:375
  66.5 1.0 copy-start.6
  69.9 13.3 %copy-start.7 = (bf16[2,2,4,48,256]{4,3,2,1,0:T(8,128)(2,1)S(1)}, bf16[2,2,4,48,256]{4,3,2,1,0:T(8,128)(2,1)}, u32[]{:S(2)}) copy-start(bf16[2,2,4,48,256]{4,3,2,1,0:T(8,128)(2,1)} %get-tuple-element.35.mine_ref) | copy-start | bytes 1179652
  69.9 16.5 %collective-permute-start.2 = (bf16[2,4,48,768]{3,2,1,0:T(8,128)(2,1)}, bf16[2,4,48,768]{3,2,1,0:T(8,128)(2,1)}, u32[]{:S(2)}, u32[]{:S(2)}) collective-permute-start(bf16[2,4,48,768]{3,2,1,0:T(8,128)(2,1)} %shard_map.98), channel_id=1, source_target_pairs={{0,8},{1,17},{2,10},{3,19},{4,12},{5,21},{6,14},{7,23},{8,0},{9,25... | collective-permute-start | bytes 1769480 | tf_op jit(solution)/shard_map/ppermute | solution.py:274
  73.9 17.4 %collective-permute-start.7 = (bf16[2,4,48,768]{3,2,1,0:T(8,128)(2,1)}, bf16[2,4,48,768]{3,2,1,0:T(8,128)(2,1)}, u32[]{:S(2)}, u32[]{:S(2)}) collective-permute-start(bf16[2,4,48,768]{3,2,1,0:T(8,128)(2,1)} %shard_map.101), channel_id=1, source_target_pairs={{0,8},{1,17},{2,10},{3,19},{4,12},{5,21},{6,14},{7,23},{8,0},{9,25... | collective-permute-start | bytes 1769480 | tf_op jit(solution)/shard_map/ppermute | solution.py:274
  79.9 32.5 %all-to-all-start.1 = ((bf16[32,1,8,768]{3,2,1,0:T(8,128)(2,1)}), bf16[32,1,8,768]{3,2,1,0:T(8,128)(2,1)}, u32[]{:S(2)}, u32[]{:S(2)}) async-start(bf16[32,1,8,768]{3,2,1,0:T(8,128)(2,1)} %bitcast.24), calls=%async_computation.1 | async-start | bytes 786432 | tf_op jit(solution)/shard_map/all_to_all | solution.py:375
  86.5 4.9 %copy-start.2 = (f32[2,4,48,768]{3,2,1,0:T(8,128)S(1)}, f32[2,4,48,768]{3,2,1,0:T(8,128)}, u32[]{:S(2)}) copy-start(f32[2,4,48,768]{3,2,1,0:T(8,128)} %get-tuple-element.43.keep_ref) | copy-start | bytes 3538948
  86.5 1.4 %copy-start.3 = (f32[2,4,48,768]{3,2,1,0:T(8,128)S(1)}, f32[2,4,48,768]{3,2,1,0:T(8,128)}, u32[]{:S(2)}) copy-start(f32[2,4,48,768]{3,2,1,0:T(8,128)} %get-tuple-element.38.keep_ref) | copy-start | bytes 3538948
  87.8 9.4 %copy-start.4 = (f32[2,4,48,768]{3,2,1,0:T(8,128)S(1)}, f32[2,4,48,768]{3,2,1,0:T(8,128)}, u32[]{:S(2)}) copy-start(f32[2,4,48,768]{3,2,1,0:T(8,128)} %get-tuple-element.38.keep_ref) | copy-start | bytes 3538948
  89.8 7.5 %collective-permute-start.3 = (bf16[1,4,48,768]{3,2,1,0:T(8,128)(2,1)}, bf16[1,4,48,768]{3,2,1,0:T(8,128)(2,1)S(1)}, u32[]{:S(2)}, u32[]{:S(2)}) collective-permute-start(bf16[1,4,48,768]{3,2,1,0:T(8,128)(2,1)} %shard_map.99), channel_id=1, source_target_pairs={{0,16},{1,9},{2,18},{3,11},{4,20},{5,13},{6,22},{7,15},{8,24},{9,1... | collective-permute-start | bytes 884744 | tf_op jit(solution)/shard_map/ppermute | solution.py:274
  93.2 11.2 %collective-permute-start.8 = (bf16[1,4,48,768]{3,2,1,0:T(8,128)(2,1)}, bf16[1,4,48,768]{3,2,1,0:T(8,128)(2,1)S(1)}, u32[]{:S(2)}, u32[]{:S(2)}) collective-permute-start(bf16[1,4,48,768]{3,2,1,0:T(8,128)(2,1)} %shard_map.102), channel_id=1, source_target_pairs={{0,16},{1,9},{2,18},{3,11},{4,20},{5,13},{6,22},{7,15},{8,24},{9,1... | collective-permute-start | bytes 884744 | tf_op jit(solution)/shard_map/ppermute | solution.py:274
  99.1 13.3 %copy-start.1 = (bf16[768,768]{1,0:T(8,128)(2,1)S(1)}, bf16[768,768]{1,0:T(8,128)(2,1)}, u32[]{:S(2)}) copy-start(bf16[768,768]{1,0:T(8,128)(2,1)} %rest_0_.1) | copy-start | bytes 3538948
  99.1 13.3 %copy-start.8 = (bf16[1,256,768]{2,1,0:T(8,128)(2,1)S(1)}, bf16[1,256,768]{2,1,0:T(8,128)(2,1)}, u32[]{:S(2)}) copy-start(bf16[1,256,768]{2,1,0:T(8,128)(2,1)} %param.5) | copy-start | bytes 1179652
  99.1 8.5 %collective-permute-start.4 = (bf16[48,768]{1,0:T(8,128)(2,1)}, bf16[48,768]{1,0:T(8,128)(2,1)S(1)}, u32[]{:S(2)}, u32[]{:S(2)}) collective-permute-start(bf16[48,768]{1,0:T(8,128)(2,1)} %get-tuple-element.40), channel_id=1, source_target_pairs={{0,2},{1,3},{2,4},{3,5},{4,6},{5,7},{6,0},{7,1},{8,10},{9,11},{10,... | collective-permute-start | bytes 221192 | tf_op jit(solution)/shard_map/ppermute | solution.py:360
  100.8 13.8 %collective-permute-start.5 = (bf16[48,768]{1,0:T(8,128)(2,1)}, bf16[48,768]{1,0:T(8,128)(2,1)S(1)}, u32[]{:S(2)}, u32[]{:S(2)}) collective-permute-start(bf16[48,768]{1,0:T(8,128)(2,1)} %get-tuple-element.41), channel_id=1, source_target_pairs={{0,4},{1,5},{2,6},{3,7},{4,0},{5,1},{6,2},{7,3},{8,12},{9,13},{10,... | collective-permute-start | bytes 221192 | tf_op jit(solution)/shard_map/ppermute | solution.py:360
  103.1 11.6 %collective-permute-start.6 = (bf16[48,768]{1,0:T(8,128)(2,1)}, bf16[48,768]{1,0:T(8,128)(2,1)S(1)}, u32[]{:S(2)}, u32[]{:S(2)}) collective-permute-start(bf16[48,768]{1,0:T(8,128)(2,1)} %get-tuple-element.42), channel_id=1, source_target_pairs={{0,6},{1,7},{2,0},{3,1},{4,2},{5,3},{6,4},{7,5},{8,14},{9,15},{10,... | collective-permute-start | bytes 221192 | tf_op jit(solution)/shard_map/ppermute | solution.py:360
  106.2 8.4 %collective-permute-start.9 = (bf16[48,768]{1,0:T(8,128)(2,1)}, bf16[48,768]{1,0:T(8,128)(2,1)S(1)}, u32[]{:S(2)}, u32[]{:S(2)}) collective-permute-start(bf16[48,768]{1,0:T(8,128)(2,1)} %get-tuple-element.45), channel_id=1, source_target_pairs={{0,2},{1,3},{2,4},{3,5},{4,6},{5,7},{6,0},{7,1},{8,10},{9,11},{10,... | collective-permute-start | bytes 221192 | tf_op jit(solution)/shard_map/ppermute | solution.py:360
  106.9 7.8 %collective-permute-start.10 = (bf16[48,768]{1,0:T(8,128)(2,1)}, bf16[48,768]{1,0:T(8,128)(2,1)S(1)}, u32[]{:S(2)}, u32[]{:S(2)}) collective-permute-start(bf16[48,768]{1,0:T(8,128)(2,1)} %get-tuple-element.46), channel_id=1, source_target_pairs={{0,4},{1,5},{2,6},{3,7},{4,0},{5,1},{6,2},{7,3},{8,12},{9,13},{10,... | collective-permute-start | bytes 221192 | tf_op jit(solution)/shard_map/ppermute | solution.py:360
  107.6 7.1 %collective-permute-start.11 = (bf16[48,768]{1,0:T(8,128)(2,1)}, bf16[48,768]{1,0:T(8,128)(2,1)S(1)}, u32[]{:S(2)}, u32[]{:S(2)}) collective-permute-start(bf16[48,768]{1,0:T(8,128)(2,1)} %get-tuple-element.47), channel_id=1, source_target_pairs={{0,6},{1,7},{2,0},{3,1},{4,2},{5,3},{6,4},{7,5},{8,14},{9,15},{10,... | collective-permute-start | bytes 221192 | tf_op jit(solution)/shard_map/ppermute | solution.py:360
  110.6 4.2 %copy-start.12 = (f32[48,768]{1,0:T(8,128)S(1)}, f32[48,768]{1,0:T(8,128)}, u32[]{:S(2)}) copy-start(f32[48,768]{1,0:T(8,128)} %get-tuple-element.39.rest_0_) | copy-start | bytes 442372
  110.6 4.2 %copy-start.13 = (f32[48,768]{1,0:T(8,128)S(1)}, f32[48,768]{1,0:T(8,128)}, u32[]{:S(2)}) copy-start(f32[48,768]{1,0:T(8,128)} %get-tuple-element.44.rest_4_) | copy-start | bytes 442372

commit v5 on v4

--- a/solution.py
+++ b/solution.py
@@ -22,6 +22,8 @@
 LANES = 128
 VMEM_SPARE = 8 * 1024 * 1024
 PIECES = 2
+FRONT_UNROLL = 1
+BACK_UNROLL = 2
 
 
 def mm(a, b):
@@ -45,7 +47,7 @@
     out_specs = [spec(i in raw_out) for i in range(len(outs))]
     taken = size(a for i, a in enumerate(args) if i not in raw_in) + size(a for i, a in enumerate(outs) if i not in raw_out)
     semaphores = [pltpu.SemaphoreType.DMA((copies,))] if copies else []
-    placed = [pltpu.HBM(a.shape, a.dtype) for a in outs]
+    placed = [pltpu.HBM(a.shape, a.dtype) if i in raw_out else a for i, a in enumerate(outs)]
     args = [pltpu.with_memory_space_constraint(a, pltpu.HBM) if i in raw_in else a for i, a in enumerate(args)]
     return pl.pallas_call(
         kernel,
@@ -131,7 +133,7 @@
         prob_store(i).start()
         return carry
 
-    lax.fori_loop(0, HEADS // 2, pair, 0)
+    lax.fori_loop(0, HEADS // 2, pair, 0, unroll=FRONT_UNROLL)
     stores[3].start()
     mixed_ref[...] = t_ref[...].T.astype(BF)
     stores[6].start()
@@ -148,17 +150,9 @@
         store.wait()
 
 
-def out_kernel(frames_ref, mixed_ref, wout_ref, out_ref):
-    out_ref[...] = (frames_ref[...].astype(F32) + mm(mixed_ref[...], wout_ref[...])).astype(BF)
-
-
-def copy_kernel(src_ref, dst_ref):
-    dst_ref[...] = src_ref[...]
-
-
 def backward_kernel(reach, cot_ref, *rest):
-    sources, (dqkv_hbm, blocks_hbm), rest = rest[:5], rest[5:7], rest[7:]
-    wout_ref, q_ref, kt_ref, v_ref, prob_ref, dqkv_ref, blocks_ref, gm_ref, dqt_ref, sem = rest
+    sources, blocks_ref, rest = rest[:5], rest[5], rest[6:]
+    wout_ref, q_ref, kt_ref, v_ref, prob_ref, dqkv_ref, gm_ref, dqt_ref, sem = rest
     tokens, width = cot_ref.shape
     targets = (wout_ref, q_ref, kt_ref, v_ref, prob_ref)
     loads = [pltpu.make_async_copy(src, dst, sem.at[i]) for i, (src, dst) in enumerate(zip(sources, targets))]
@@ -202,30 +196,49 @@
         dqkv_ref[:, pl.ds(pl.multiple_of(2 * width + i * 128, 128), 128)] = jnp.concatenate(dvs, 1).astype(BF)
         return carry
 
-    lax.fori_loop(0, HEADS // 2, pair, 0)
+    lax.fori_loop(0, HEADS // 2, pair, 0, unroll=BACK_UNROLL)
     dqkv_ref[:, :width] = dqt_ref[...].T.astype(BF)
-    whole = pltpu.make_async_copy(dqkv_ref, dqkv_hbm, sem.at[5])
     runs = blocks_ref.shape[0]
     wide, thin = 3 * width // runs, width // runs
-    stores = []
     for j in range(runs):
         blocks_ref[j, :, :wide] = dqkv_ref[:, j * wide : (j + 1) * wide]
         blocks_ref[j, :, wide:] = cot_ref[:, j * thin : (j + 1) * thin]
-        stores.append(pltpu.make_async_copy(blocks_ref.at[j], blocks_hbm.at[j], sem.at[6 + j]))
-        stores[-1].start()
-    whole.start()
-    for store in stores + [whole]:
-        store.wait()
-
-
-def norm_kernel(x_ref, cot_ref, gain_ref, dqkv_ref, wqkv_ref, fgrad_ref, gpart_ref):
+
+
+def norm_kernel(inner, x_ref, cot_ref, gain_ref, blocks_ref, wqkv_ref, mixed_ref, back_ref, dqkv_ref, extra_ref):
+    tokens, width = x_ref.shape
+    runs = blocks_ref.shape[0]
+    wide = 3 * width // runs
+    for j in range(runs):
+        dqkv_ref[:, j * wide : (j + 1) * wide] = blocks_ref[j, :, :wide]
     unit, spread = row_stats(x_ref[...].astype(F32))
     ngrad = mm_t(dqkv_ref[...], wqkv_ref[...])
-    gpart_ref[...] = jnp.sum(ngrad * unit, axis=0, keepdims=True)
+    part = jnp.sum(ngrad * unit, axis=0, keepdims=True)
     scaled = ngrad * gain_ref[...]
     mean_one = jnp.mean(scaled, axis=-1, keepdims=True)
     second = jnp.mean(scaled * unit, axis=-1, keepdims=True)
-    fgrad_ref[...] = (cot_ref[...].astype(F32) + spread * (scaled - mean_one - unit * second)).astype(BF)
+    back_ref[:, :width] = mixed_ref[...]
+    back_ref[:, width : 2 * width] = (cot_ref[...].astype(F32) + spread * (scaled - mean_one - unit * second)).astype(BF)
+    high = part.astype(BF).astype(F32)
+    extra_ref[...] = jnp.zeros_like(extra_ref)
+    share, each = width // inner, tokens // (runs * inner)
+    for k, value in enumerate((high, part - high)):
+        row, lane = k % each, k // each * LANES
+        for i in range(inner):
+            piece = value[:, i * share : (i + 1) * share]
+            for t in range(runs):
+                start = (t * inner + i) * each + row
+                extra_ref[start : start + 1, lane : lane + share] = piece
+    back_ref[:, 2 * width :] = extra_ref[...].astype(BF)
+
+
+def finish_kernel(inv_root, frames_ref, wout_ref, back_ref, block_ref, fgrad_ref, gain_ref):
+    width, share = fgrad_ref.shape[1], gain_ref.shape[1]
+    block_ref[...] = (frames_ref[...].astype(F32) + mm(back_ref[:, :width], wout_ref[...])).astype(BF)
+    fgrad_ref[...] = back_ref[:, width : 2 * width]
+    total = jnp.sum(back_ref[:, 2 * width :].astype(F32), axis=0, keepdims=True)
+    parts = [total[:, k : k + share] for k in range(0, total.shape[1], LANES)]
+    gain_ref[...] = sum(parts) * inv_root
 
 
 def squeeze_bits(value, bits):
@@ -288,7 +301,7 @@
             for slot, cols in ((0, slice(0, wide)), (1, slice(wide, None))):
                 left = mine_ref[slot, piece].reshape(count * rows, tokens)
                 right = other_ref[slot, piece].reshape(count * rows, tokens)
-                totals.append(mm(left, d_ref[run][:, cols]) + mm(right, d_other_ref[run][:, cols]))
+                totals.append(mm(left, d_ref[run, :, cols]) + mm(right, d_other_ref[run, :, cols]))
             total = jnp.concatenate(totals, 1).astype(out_ref.dtype)
             for z in range(count):
                 out_ref[n, z] = total[z * rows : (z + 1) * rows]
@@ -341,11 +354,16 @@
     shape = (runs // 2, count, rows, lanes)
     flops = 4 * count * rows * tokens * lanes * (runs // 2)
     args = (mine, other, d, d_other)
+
+    def product(chosen, send, dtype):
+        out = (sds(shape, dtype),) * len(chosen)
+        return call(functools.partial(product_kernel, runs, chosen, send), out, *args, flops=len(chosen) * flops)
+
     got = [[] for _ in range(pieces)]
     for p in range(pieces):
-        send = call(functools.partial(product_kernel, runs, (p,), True), (sds(shape, BF),), *args, flops=flops)[0]
+        send = product((p,), True, BF)[0]
         got[p].append(exchange(send, runs, inner, 0))
-    keep = call(functools.partial(product_kernel, runs, tuple(range(pieces)), False), (sds(shape, F32),) * pieces, *args, flops=pieces * flops)
+    keep = product(tuple(range(pieces)), False, F32)
     for stage in range(1, stages):
         shape = (shape[0] // 2,) + shape[1:]
         for p in range(pieces):
@@ -422,43 +440,48 @@
         copies=10 + HEADS // 2,
     )
     theirs = to_partner(other, inner)
-    mixed_back = to_frames(mixed, count, held, patches)
-    block_out = call(out_kernel, sds((held * patches, width), BF), frames.reshape(-1, width), mixed_back.reshape(-1, width), w_out, flops=2 * tokens * width * width)
-    block_out = block_out.reshape(held, patches, width)
-    made = (((tokens, 3 * width), BF), ((runs, tokens, 4 * width // runs), BF))
-    dqkv, blocks = call(
+    made = ((runs, tokens, 4 * width // runs), BF)
+    blocks = call(
         functools.partial(backward_kernel, reach),
-        tuple(sds(*each) for each in made),
+        sds(*made),
         cot,
         w_out,
         q,
         kt,
         v,
         prob,
-        scratch=[*(vmem(*each) for each in (((width, width), BF), flat, turned, flat, probs) + made), vmem(*flat), vmem((width, tokens), F32)],
+        scratch=[*(vmem(*each) for each in (((width, width), BF), flat, turned, flat, probs)), vmem((tokens, 3 * width), BF), vmem(*flat), vmem((width, tokens), F32)],
         flops=2 * tokens * width * 4 * width,
         raw_in=range(1, 6),
-        raw_out=range(2),
-        copies=6 + runs,
+        copies=5,
     )
     blocks_other = to_partner(blocks, inner)
-    fgrad, gpart = call(
-        norm_kernel,
-        (sds((tokens, width), BF), sds((1, width), F32)),
+    extra = -(-2 // (tokens // count)) * LANES
+    back = call(
+        functools.partial(norm_kernel, inner),
+        sds((tokens, 2 * width + extra), BF),
         x,
         cot,
         gain,
-        dqkv,
+        blocks,
         w_qkv,
+        mixed,
+        scratch=[vmem((tokens, 3 * width), BF), vmem((tokens, extra), F32)],
         flops=2 * tokens * width * 3 * width,
     )
-    frames_grad = to_frames(fgrad, count, held, patches)
-    frames_grad = call(copy_kernel, sds((held * patches, width), BF), frames_grad.reshape(-1, width)).reshape(held, patches, width)
+    back = to_frames(back, count, held, patches).reshape(held * patches, -1)
+    owned = sds((held * patches, width), BF)
+    block_out, frames_grad, gain_grad = call(
+        functools.partial(finish_kernel, inv_root),
+        (owned, owned, sds((1, width // inner), F32)),
+        frames.reshape(-1, width),
+        w_out,
+        back,
+        flops=2 * tokens * width * width,
+    )
+    block_out, frames_grad = block_out.reshape(frames.shape), frames_grad.reshape(frames.shape)
     qkv_grad, out_grad = reduce_weights(mine, theirs, blocks, blocks_other, runs, inner, inv_root)
-    shares = jnp.broadcast_to(gpart.reshape(1, inner, width // inner), (runs, inner, width // inner))
-    shares = lax.all_to_all(shares.reshape(count, 1, -1), AXES, split_axis=0, concat_axis=0, tiled=True)
-    gain_grad = jnp.sum(shares, axis=(0, 1)) * inv_root
-    return block_out, frames_grad, qkv_grad, out_grad, gain_grad
+    return block_out, frames_grad, qkv_grad, out_grad, gain_grad.reshape(-1)
 
 
 def solution(mesh):

time: 117 us -> 97.8 us (0.84)
  Pallas kernels: 43.8 us -> 26 us
  waiting for transfers between devices: 11.4 us -> 26.1 us
  blocking collectives: 31.4 us -> 20.8 us
  local copies, waits for them, and re-layouts: 3.75 us -> 0.96 us
  other arithmetic: 1.55 us -> 0.29 us
    pallas_call x13 -> x12, Pallas kernels: 43.8 us -> 26 us  [call(): pl.pallas_call(kernel, out_shape=placed if isinstance(out_shape, (tuple,...]
    ppermute x4, waiting for transfers between devices: 3.61 us -> 19.6 us  [exchange(): return lax.ppermute(value, AXES, perm)]
    all_to_all x1 -> x0, blocking collectives: 10.7 us -> none  [shards(): lax.all_to_all(shares.reshape(count, 1, -1), AXES, split_axis=0, concat_a...]
    all_to_all x2 -> x1, waiting for transfers between devices: 5.48 us -> 0.01 us  [to_frames(): parts = lax.all_to_all(parts, AXES, split_axis=0, concat_axis=0, tiled=True)]
    all_to_all x2 -> x1, starting transfers between devices: 6.61 us -> 3.84 us  [to_frames(): parts = lax.all_to_all(parts, AXES, split_axis=0, concat_axis=0, tiled=True)]
    unnamed x30 -> x18, local copies, waits for them, and re-layouts: 3.67 us -> 0.96 us
    ppermute x6, waiting for transfers between devices: 0.15 us -> 2.55 us  [reduce_weights(): lax.ppermute(send, 'inner', [(i, (i + 2 * (k + 1)) % inner) for i in rang...]
    ppermute x2, waiting for transfers between devices: 0.01 us -> 1.75 us  [to_partner(): return lax.ppermute(value, 'inner', [(i, i ^ 1) for i in range(inner)])]
  transfers between devices with their start and end apart: 15 -> 14, of which waited for: 4 -> 5; matrix products, arithmetic and copies ran while one was open for 1% -> 0% of each run, Pallas kernels for 28% -> 18%
where the time goes in v5:
time: 97.8 us; the launch traced here: 97.4 us
  waiting for transfers between devices  26.1 us (27%)
  Pallas kernels  26 us (27%)
  starting transfers between devices  22.6 us (23%)
  blocking collectives  20.8 us (21%)
    pallas_call x12, Pallas kernels, call(): pl.pallas_call(kernel, out_shape=placed if isinstance(out_shape, (tuple,...  26 us
    all_to_all x1, blocking collectives, to_tubes(): parts = lax.all_to_all(parts, AXES, split_axis=0, concat_axis=0, tiled=True)  20.8 us
    ppermute x4, waiting for transfers between devices, exchange(): return lax.ppermute(value, AXES, perm)  19.6 us
    ppermute x6, starting transfers between devices, reduce_weights(): lax.ppermute(send, 'inner', [(i, (i + 2 * (k + 1)) % inner) for i in rang...  10.2 us
    ppermute x4, starting transfers between devices, exchange(): return lax.ppermute(value, AXES, perm)  5.46 us
    all_to_all x1, starting transfers between devices, to_frames(): parts = lax.all_to_all(parts, AXES, split_axis=0, concat_axis=0, tiled=True)  3.84 us
    all_to_all x1, starting transfers between devices, to_tubes(): parts = lax.all_to_all(parts, AXES, split_axis=0, concat_axis=0, tiled=True)  2.6 us
    ppermute x6, waiting for transfers between devices, reduce_weights(): lax.ppermute(send, 'inner', [(i, (i + 2 * (k + 1)) % inner) for i in rang...  2.55 us
  transfers between devices with their start and end apart: 14, of which 5 were waited for; matrix products, arithmetic and copies ran while one was open for 0% of the time, Pallas kernels for 18%

profile of v5, /device:TPU:0, one launch (start us, length us, event | category | flops | bytes accessed | tf_op | source)
XLA Modules:
  0.0 97.4 jit_solution(15812470940414140562)
XLA Ops:
  0.6 20.8 %all_to_all.15 = bf16[32,1,8,768]{3,2,1,0:T(8,128)(2,1)S(1)} all-to-all(bf16[32,1,8,768]{3,2,1,0:T(8,128)(2,1)} %bitcast.15), channel_id=1, replica_groups=mesh['tm'=4,'inner'=8] {'tm','inner'}, dimensions={0} | all-to-all | bytes 786432 | tf_op jit(solution)/shard_map/all_to_all | solution.py:386
  21.4 2.6 %all-to-all-start.1 = ((bf16[32,1,8,768]{3,2,1,0:T(8,128)(2,1)}), bf16[32,1,8,768]{3,2,1,0:T(8,128)(2,1)S(1)}, u32[]{:S(2)}, u32[]{:S(2)}) async-start(bf16[32,1,8,768]{3,2,1,0:T(8,128)(2,1)} %bitcast.19), calls=%async_computation.1 | async-start | bytes 786432 | tf_op jit(solution)/shard_map/all_to_all | solution.py:386
  24.1 0.3 fusion.15.bias_ref
  24.4 10.9 %shard_map.92 = (bf16[2,2,4,48,256]{4,3,2,1,0:T(8,128)(2,1)}, bf16[2,2,4,48,256]{4,3,2,1,0:T(8,128)(2,1)}, bf16[256,768]{1,0:T(8,128)(2,1)}, bf16[768,256]{1,0:T...) custom-call(bf16[256,768]{1,0:T(8,128)(2,1)S(1)} %bitcast.17, ...), custom_call_target="tpu_custom_call" | custom-call | flops 1207959552 | bytes 8522752 | tf_op jit(solution)/shard_map/pallas_call | solution.py:52
  35.3 2.2 %all-to-all-done.1 = bf16[32,1,8,768]{3,2,1,0:T(8,128)(2,1)S(1)} async-done(((bf16[32,1,8,768]{3,2,1,0:T(8,128)(2,1)}), bf16[32,1,8,768]{3,2,1,0:T(8,128)(2,1)S(1)}, u32[]{:S(2)}, u32[]{:S(2)}) %all-to-all-start.1) | async-done | bytes 393248 | tf_op jit(solution)/shard_map/all_to_all | solution.py:386
  37.4 7.7 %shard_map.93.blocks_ref.d_ref = bf16[4,256,768]{2,1,0:T(8,128)(2,1)S(1)} custom-call(bf16[256,768]{1,0:T(8,128)(2,1)S(1)} %bitcast.12, bf16[768,768]{1,0:T(8,128)(2,1)} %wout_ref.1, bf16[256,768]{1,0:T(8,128)(2,1)} %get-tuple-element.27.rest_1_, bf16[768,256]{1,0:T(8,128)(2,1)} %get-tuple-element.28.rest_2_, bf16[256,768]{1,0:T(8,128)(2,1)} %get-tuple-element.29.rest_3_, ...), custom_call_target="tpu_custom_call" | custom-call | flops 1207959552 | bytes 6291456 | tf_op jit(solution)/shard_map/pallas_call | solution.py:52
  45.1 0.2 collective-permute-start.1
  45.3 1.5 %shard_map.94 = bf16[256,1664]{1,0:T(8,128)(2,1)S(1)} custom-call(bf16[256,768]{1,0:T(8,128)(2,1)S(1)} %bitcast.18, bf16[256,768]{1,0:T(8,128)(2,1)S(1)} %bitcast.13, f32[1,768]{1,0:T(1,128)S(1)} %reshape.37.gain_ref, bf16[4,256,768]{2,1,0:T(8,128)(2,1)S(1)} %shard_map.93.blocks_ref.d_ref, bf16[768,2304]{1,0:T(8,128)(2,1)S(1)} %copy-done.1, ...), custom_call_target="tpu_custom_call" | custom-call | flops 905969664 | bytes 7146496 | tf_op jit(solution)/shard_map/pallas_call | solution.py:52
  46.8 0.9 copy-done.3
  47.8 3.8 %all-to-all-start.2 = ((bf16[32,1,8,1664]{3,2,1,0:T(8,128)(2,1)}), bf16[32,1,8,1664]{3,2,1,0:T(8,128)(2,1)}, u32[]{:S(2)}, u32[]{:S(2)}) async-start(bf16[32,1,8,1664]{3,2,1,0:T(8,128)(2,1)} %bitcast.14), calls=%async_computation.2 | async-start | bytes 1703936 | tf_op jit(solution)/shard_map/all_to_all | solution.py:393
  51.6 0.3 collective-permute-start
  51.9 1.7 %collective-permute-done.other_ref = bf16[2,2,4,48,256]{4,3,2,1,0:T(8,128)(2,1)S(1)} collective-permute-done((bf16[2,2,4,48,256]{4,3,2,1,0:T(8,128)(2,1)}, bf16[2,2,4,48,256]{4,3,2,1,0:T(8,128)(2,1)S(1)}, u32[]{:S(2)}, u32[]{:S(2)}) %collective-permute-start) | collective-permute-done | bytes 393248 | tf_op jit(solution)/shard_map/ppermute | solution.py:291
  53.6 0.6 shard_map.97
  54.3 1.8 %collective-permute-start.2 = (bf16[2,4,48,768]{3,2,1,0:T(8,128)(2,1)S(1)}, bf16[2,4,48,768]{3,2,1,0:T(8,128)(2,1)S(1)}, u32[]{:S(2)}, u32[]{:S(2)}) collective-permute-start(bf16[2,4,48,768]{3,2,1,0:T(8,128)(2,1)S(1)} %shard_map.97), channel_id=1, source_target_pairs={{0,8},{1,17},{2,10},{3,19},{4,12},{5,21},{6,14},{7,23},{8,0},{9,25... | collective-permute-start | bytes 1769480 | tf_op jit(solution)/shard_map/ppermute | solution.py:287
  56.0 0.6 shard_map.100
  56.7 0.4 collective-permute-start.7
  57.1 1.0 %shard_map.96 = (f32[2,4,48,768]{3,2,1,0:T(8,128)S(1)}, f32[2,4,48,768]{3,2,1,0:T(8,128)S(1)}) custom-call(bf16[2,2,4,48,256]{4,3,2,1,0:T(8,128)(2,1)S(1)} %copy-done.2, bf16[2,2,4,48,256]{4,3,2,1,0:T(8,128)(2,1)S(1)} %collective-permute-done.other_ref, bf16[4,256,768]{2,1,0:T(8,128)(2,1)S(1)} %shard_map.93.blocks_ref.d_ref, ...), custom_call_target="tpu_custom_call" | custom-call | flops 603979776 | bytes 6291456 | tf_op jit(solution)/shard_map/pallas_call | solution.py:52
  58.1 9.8 %collective-permute-done.2.rest_0_ = bf16[2,4,48,768]{3,2,1,0:T(8,128)(2,1)S(1)} collective-permute-done((bf16[2,4,48,768]{3,2,1,0:T(8,128)(2,1)S(1)}, bf16[2,4,48,768]{3,2,1,0:T(8,128)(2,1)S(1)}, u32[]{:S(2)}, u32[]{:S(2)}) %collective-permute-start.2) | collective-permute-done | bytes 589856 | tf_op jit(solution)/shard_map/ppermute | solution.py:287
  67.9 1.7 %collective-permute-start.3 = (bf16[1,4,48,768]{3,2,1,0:T(8,128)(2,1)S(1)}, bf16[1,4,48,768]{3,2,1,0:T(8,128)(2,1)S(1)}, u32[]{:S(2)}, u32[]{:S(2)}) collective-permute-start(bf16[1,4,48,768]{3,2,1,0:T(8,128)(2,1)S(1)} %shard_map.98), channel_id=1, source_target_pairs={{0,16},{1,9},{2,18},{3,11},{4,20},{5,13},{6,22},{7,15},{8,24},{9,1... | collective-permute-start | bytes 884744 | tf_op jit(solution)/shard_map/ppermute | solution.py:287
  69.6 9.8 %collective-permute-done.7.rest_0_ = bf16[2,4,48,768]{3,2,1,0:T(8,128)(2,1)S(1)} collective-permute-done((bf16[2,4,48,768]{3,2,1,0:T(8,128)(2,1)S(1)}, bf16[2,4,48,768]{3,2,1,0:T(8,128)(2,1)S(1)}, u32[]{:S(2)}, u32[]{:S(2)}) %collective-permute-start.7) | collective-permute-done | bytes 589856 | tf_op jit(solution)/shard_map/ppermute | solution.py:287
  79.5 1.6 %collective-permute-start.8 = (bf16[1,4,48,768]{3,2,1,0:T(8,128)(2,1)S(1)}, bf16[1,4,48,768]{3,2,1,0:T(8,128)(2,1)S(1)}, u32[]{:S(2)}, u32[]{:S(2)}) collective-permute-start(bf16[1,4,48,768]{3,2,1,0:T(8,128)(2,1)S(1)} %shard_map.101), channel_id=1, source_target_pairs={{0,16},{1,9},{2,18},{3,11},{4,20},{5,13},{6,22},{7,15},{8,24},{9,1... | collective-permute-start | bytes 884744 | tf_op jit(solution)/shard_map/ppermute | solution.py:287
  81.1 0.1 shard_map.99
  81.3 1.4 %collective-permute-start.4 = (bf16[48,768]{1,0:T(8,128)(2,1)S(1)}, bf16[48,768]{1,0:T(8,128)(2,1)S(1)}, u32[]{:S(2)}, u32[]{:S(2)}) collective-permute-start(bf16[48,768]{1,0:T(8,128)(2,1)S(1)} %get-tuple-element.38), channel_id=1, source_target_pairs={{0,2},{1,3},{2,4},{3,5},{4,6},{5,7},{6,0},{7,1},{8,10},{9,11},{10,... | collective-permute-start | bytes 221192 | tf_op jit(solution)/shard_map/ppermute | solution.py:378
  82.7 2.2 %collective-permute-start.5 = (bf16[48,768]{1,0:T(8,128)(2,1)S(1)}, bf16[48,768]{1,0:T(8,128)(2,1)S(1)}, u32[]{:S(2)}, u32[]{:S(2)}) collective-permute-start(bf16[48,768]{1,0:T(8,128)(2,1)S(1)} %get-tuple-element.39), channel_id=1, source_target_pairs={{0,4},{1,5},{2,6},{3,7},{4,0},{5,1},{6,2},{7,3},{8,12},{9,13},{10,... | collective-permute-start | bytes 221192 | tf_op jit(solution)/shard_map/ppermute | solution.py:378
  84.9 1.5 %collective-permute-start.6 = (bf16[48,768]{1,0:T(8,128)(2,1)S(1)}, bf16[48,768]{1,0:T(8,128)(2,1)S(1)}, u32[]{:S(2)}, u32[]{:S(2)}) collective-permute-start(bf16[48,768]{1,0:T(8,128)(2,1)S(1)} %get-tuple-element.40), channel_id=1, source_target_pairs={{0,6},{1,7},{2,0},{3,1},{4,2},{5,3},{6,4},{7,5},{8,14},{9,15},{10,... | collective-permute-start | bytes 221192 | tf_op jit(solution)/shard_map/ppermute | solution.py:378
  86.4 0.1 shard_map.102
  86.5 1.5 %collective-permute-start.9 = (bf16[48,768]{1,0:T(8,128)(2,1)S(1)}, bf16[48,768]{1,0:T(8,128)(2,1)S(1)}, u32[]{:S(2)}, u32[]{:S(2)}) collective-permute-start(bf16[48,768]{1,0:T(8,128)(2,1)S(1)} %get-tuple-element.43), channel_id=1, source_target_pairs={{0,2},{1,3},{2,4},{3,5},{4,6},{5,7},{6,0},{7,1},{8,10},{9,11},{10,... | collective-permute-start | bytes 221192 | tf_op jit(solution)/shard_map/ppermute | solution.py:378
  88.0 2.1 %collective-permute-start.10 = (bf16[48,768]{1,0:T(8,128)(2,1)S(1)}, bf16[48,768]{1,0:T(8,128)(2,1)S(1)}, u32[]{:S(2)}, u32[]{:S(2)}) collective-permute-start(bf16[48,768]{1,0:T(8,128)(2,1)S(1)} %get-tuple-element.44), channel_id=1, source_target_pairs={{0,4},{1,5},{2,6},{3,7},{4,0},{5,1},{6,2},{7,3},{8,12},{9,13},{10,... | collective-permute-start | bytes 221192 | tf_op jit(solution)/shard_map/ppermute | solution.py:378
  90.1 1.5 %collective-permute-start.11 = (bf16[48,768]{1,0:T(8,128)(2,1)S(1)}, bf16[48,768]{1,0:T(8,128)(2,1)S(1)}, u32[]{:S(2)}, u32[]{:S(2)}) collective-permute-start(bf16[48,768]{1,0:T(8,128)(2,1)S(1)} %get-tuple-element.45), channel_id=1, source_target_pairs={{0,6},{1,7},{2,0},{3,1},{4,2},{5,3},{6,4},{7,5},{8,14},{9,15},{10,... | collective-permute-start | bytes 221192 | tf_op jit(solution)/shard_map/ppermute | solution.py:378
  91.6 2.5 %shard_map.95 = (bf16[256,768]{1,0:T(8,128)(2,1)}, bf16[256,768]{1,0:T(8,128)(2,1)}, f32[1,96]{1,0:T(1,128)}) custom-call(bf16[256,768]{1,0:T(8,128)(2,1)S(1)} %bitcast.16, bf16[768,768]{1,0:T(8,128)(2,1)S(1)} %copy-done, bf16[256,1664]{1,0:T(8,128)(2,1)} %bitcast.7.back_ref), custom_call_target="tpu_custom_call" | custom-call | flops 301989888 | bytes 3211648 | tf_op jit(solution)/shard_map/pallas_call | solution.py:52
  94.1 2.5 %collective-permute-done.10.rest_6_ = bf16[48,768]{1,0:T(8,128)(2,1)S(1)} collective-permute-done((bf16[48,768]{1,0:T(8,128)(2,1)S(1)}, bf16[48,768]{1,0:T(8,128)(2,1)S(1)}, u32[]{:S(2)}, u32[]{:S(2)}) %collective-permute-start.10) | collective-permute-done | bytes 73760 | tf_op jit(solution)/shard_map/ppermute | solution.py:378
  96.6 0.8 shard_map.103
  (32 shorter events, 0.2 us)
Async XLA Ops:
  0.6 23.4 %copy-start.8 = (f32[768]{0:T(1024)S(1)}, f32[768]{0:T(1024)}, u32[]{:S(2)}) copy-start(f32[768]{0:T(1024)} %param.6) | copy-start | bytes 9220
  21.4 13.9 %copy-start.5 = (bf16[32,1,8,768]{3,2,1,0:T(8,128)(2,1)}, bf16[32,1,8,768]{3,2,1,0:T(8,128)(2,1)S(1)}, u32[]{:S(2)}) copy-start(bf16[32,1,8,768]{3,2,1,0:T(8,128)(2,1)S(1)} %all_to_all.15) | copy-start | bytes 1179652
  21.4 16.0 %all-to-all-start.1 = ((bf16[32,1,8,768]{3,2,1,0:T(8,128)(2,1)}), bf16[32,1,8,768]{3,2,1,0:T(8,128)(2,1)S(1)}, u32[]{:S(2)}, u32[]{:S(2)}) async-start(bf16[32,1,8,768]{3,2,1,0:T(8,128)(2,1)} %bitcast.19), calls=%async_computation.1 | async-start | bytes 786432 | tf_op jit(solution)/shard_map/all_to_all | solution.py:386
  37.4 7.9 %copy-start.1 = (bf16[768,2304]{1,0:T(8,128)(2,1)S(1)}, bf16[768,2304]{1,0:T(8,128)(2,1)}, u32[]{:S(2)}) copy-start(bf16[768,2304]{1,0:T(8,128)(2,1)} %wqkv_ref.1) | copy-start | bytes 10616836
  37.4 7.9 %copy-start.6 = (bf16[32,1,8,768]{3,2,1,0:T(8,128)(2,1)S(1)}, bf16[32,1,8,768]{3,2,1,0:T(8,128)(2,1)}, u32[]{:S(2)}) copy-start(bf16[32,1,8,768]{3,2,1,0:T(8,128)(2,1)} %copy-done.5) | copy-start | bytes 1179652
  37.4 7.9 %copy-start.7 = (bf16[256,768]{1,0:T(8,128)(2,1)S(1)}, bf16[256,768]{1,0:T(8,128)(2,1)}, u32[]{:S(2)}) copy-start(bf16[256,768]{1,0:T(8,128)(2,1)} %get-tuple-element.31.mixed_ref) | copy-start | bytes 1179652
  45.1 8.5 %collective-permute-start.1 = (bf16[4,256,768]{2,1,0:T(8,128)(2,1)S(1)}, bf16[4,256,768]{2,1,0:T(8,128)(2,1)S(1)}, u32[]{:S(2)}, u32[]{:S(2)}) collective-permute-start(bf16[4,256,768]{2,1,0:T(8,128)(2,1)S(1)} %shard_map.93.blocks_ref.d_ref), channel_id=1, source_target_pairs={{0,1},{1,0},{2,3},{3,2},{4,5},{5,4},{6,7},{7,6},{8,9},{9,8},{10,11... | collective-permute-start | bytes 4718600 | tf_op jit(solution)/shard_map/ppermute | solution.py:291
  46.8 0.9 copy-start.3
  47.8 5.9 %copy-start.2 = (bf16[2,2,4,48,256]{4,3,2,1,0:T(8,128)(2,1)S(1)}, bf16[2,2,4,48,256]{4,3,2,1,0:T(8,128)(2,1)}, u32[]{:S(2)}) copy-start(bf16[2,2,4,48,256]{4,3,2,1,0:T(8,128)(2,1)} %get-tuple-element.34.mine_ref) | copy-start | bytes 1179652
  47.8 43.8 %all-to-all-start.2 = ((bf16[32,1,8,1664]{3,2,1,0:T(8,128)(2,1)}), bf16[32,1,8,1664]{3,2,1,0:T(8,128)(2,1)}, u32[]{:S(2)}, u32[]{:S(2)}) async-start(bf16[32,1,8,1664]{3,2,1,0:T(8,128)(2,1)} %bitcast.14), calls=%async_computation.2 | async-start | bytes 1703936 | tf_op jit(solution)/shard_map/all_to_all | solution.py:393
  51.6 2.0 %collective-permute-start = (bf16[2,2,4,48,256]{4,3,2,1,0:T(8,128)(2,1)}, bf16[2,2,4,48,256]{4,3,2,1,0:T(8,128)(2,1)S(1)}, u32[]{:S(2)}, u32[]{:S(2)}) collective-permute-start(bf16[2,2,4,48,256]{4,3,2,1,0:T(8,128)(2,1)} %get-tuple-element.35), channel_id=1, source_target_pairs={{0,1},{1,0},{2,3},{3,2},{4,5},{5,4},{6,7},{7,6},{8,9},{9,8},{10,11... | collective-permute-start | bytes 1179656 | tf_op jit(solution)/shard_map/ppermute | solution.py:291
  54.3 13.6 %collective-permute-start.2 = (bf16[2,4,48,768]{3,2,1,0:T(8,128)(2,1)S(1)}, bf16[2,4,48,768]{3,2,1,0:T(8,128)(2,1)S(1)}, u32[]{:S(2)}, u32[]{:S(2)}) collective-permute-start(bf16[2,4,48,768]{3,2,1,0:T(8,128)(2,1)S(1)} %shard_map.97), channel_id=1, source_target_pairs={{0,8},{1,17},{2,10},{3,19},{4,12},{5,21},{6,14},{7,23},{8,0},{9,25... | collective-permute-start | bytes 1769480 | tf_op jit(solution)/shard_map/ppermute | solution.py:287
  56.7 22.8 %collective-permute-start.7 = (bf16[2,4,48,768]{3,2,1,0:T(8,128)(2,1)S(1)}, bf16[2,4,48,768]{3,2,1,0:T(8,128)(2,1)S(1)}, u32[]{:S(2)}, u32[]{:S(2)}) collective-permute-start(bf16[2,4,48,768]{3,2,1,0:T(8,128)(2,1)S(1)} %shard_map.100), channel_id=1, source_target_pairs={{0,8},{1,17},{2,10},{3,19},{4,12},{5,21},{6,14},{7,23},{8,0},{9,25... | collective-permute-start | bytes 1769480 | tf_op jit(solution)/shard_map/ppermute | solution.py:287
  67.9 13.2 %collective-permute-start.3 = (bf16[1,4,48,768]{3,2,1,0:T(8,128)(2,1)S(1)}, bf16[1,4,48,768]{3,2,1,0:T(8,128)(2,1)S(1)}, u32[]{:S(2)}, u32[]{:S(2)}) collective-permute-start(bf16[1,4,48,768]{3,2,1,0:T(8,128)(2,1)S(1)} %shard_map.98), channel_id=1, source_target_pairs={{0,16},{1,9},{2,18},{3,11},{4,20},{5,13},{6,22},{7,15},{8,24},{9,1... | collective-permute-start | bytes 884744 | tf_op jit(solution)/shard_map/ppermute | solution.py:287
  79.5 12.1 %copy-start = (bf16[768,768]{1,0:T(8,128)(2,1)S(1)}, bf16[768,768]{1,0:T(8,128)(2,1)}, u32[]{:S(2)}) copy-start(bf16[768,768]{1,0:T(8,128)(2,1)} %wout_ref.1) | copy-start | bytes 3538948
  79.5 12.1 %copy-start.4 = (bf16[1,256,768]{2,1,0:T(8,128)(2,1)S(1)}, bf16[1,256,768]{2,1,0:T(8,128)(2,1)}, u32[]{:S(2)}) copy-start(bf16[1,256,768]{2,1,0:T(8,128)(2,1)} %param.5) | copy-start | bytes 1179652
  79.5 6.8 %collective-permute-start.8 = (bf16[1,4,48,768]{3,2,1,0:T(8,128)(2,1)S(1)}, bf16[1,4,48,768]{3,2,1,0:T(8,128)(2,1)S(1)}, u32[]{:S(2)}, u32[]{:S(2)}) collective-permute-start(bf16[1,4,48,768]{3,2,1,0:T(8,128)(2,1)S(1)} %shard_map.101), channel_id=1, source_target_pairs={{0,16},{1,9},{2,18},{3,11},{4,20},{5,13},{6,22},{7,15},{8,24},{9,1... | collective-permute-start | bytes 884744 | tf_op jit(solution)/shard_map/ppermute | solution.py:287
  81.3 8.9 %collective-permute-start.4 = (bf16[48,768]{1,0:T(8,128)(2,1)S(1)}, bf16[48,768]{1,0:T(8,128)(2,1)S(1)}, u32[]{:S(2)}, u32[]{:S(2)}) collective-permute-start(bf16[48,768]{1,0:T(8,128)(2,1)S(1)} %get-tuple-element.38), channel_id=1, source_target_pairs={{0,2},{1,3},{2,4},{3,5},{4,6},{5,7},{6,0},{7,1},{8,10},{9,11},{10,... | collective-permute-start | bytes 221192 | tf_op jit(solution)/shard_map/ppermute | solution.py:378
  82.7 11.4 %collective-permute-start.5 = (bf16[48,768]{1,0:T(8,128)(2,1)S(1)}, bf16[48,768]{1,0:T(8,128)(2,1)S(1)}, u32[]{:S(2)}, u32[]{:S(2)}) collective-permute-start(bf16[48,768]{1,0:T(8,128)(2,1)S(1)} %get-tuple-element.39), channel_id=1, source_target_pairs={{0,4},{1,5},{2,6},{3,7},{4,0},{5,1},{6,2},{7,3},{8,12},{9,13},{10,... | collective-permute-start | bytes 221192 | tf_op jit(solution)/shard_map/ppermute | solution.py:378
  84.9 9.2 %collective-permute-start.6 = (bf16[48,768]{1,0:T(8,128)(2,1)S(1)}, bf16[48,768]{1,0:T(8,128)(2,1)S(1)}, u32[]{:S(2)}, u32[]{:S(2)}) collective-permute-start(bf16[48,768]{1,0:T(8,128)(2,1)S(1)} %get-tuple-element.40), channel_id=1, source_target_pairs={{0,6},{1,7},{2,0},{3,1},{4,2},{5,3},{6,4},{7,5},{8,14},{9,15},{10,... | collective-permute-start | bytes 221192 | tf_op jit(solution)/shard_map/ppermute | solution.py:378
  86.5 7.6 %collective-permute-start.9 = (bf16[48,768]{1,0:T(8,128)(2,1)S(1)}, bf16[48,768]{1,0:T(8,128)(2,1)S(1)}, u32[]{:S(2)}, u32[]{:S(2)}) collective-permute-start(bf16[48,768]{1,0:T(8,128)(2,1)S(1)} %get-tuple-element.43), channel_id=1, source_target_pairs={{0,2},{1,3},{2,4},{3,5},{4,6},{5,7},{6,0},{7,1},{8,10},{9,11},{10,... | collective-permute-start | bytes 221192 | tf_op jit(solution)/shard_map/ppermute | solution.py:378
  88.0 8.6 %collective-permute-start.10 = (bf16[48,768]{1,0:T(8,128)(2,1)S(1)}, bf16[48,768]{1,0:T(8,128)(2,1)S(1)}, u32[]{:S(2)}, u32[]{:S(2)}) collective-permute-start(bf16[48,768]{1,0:T(8,128)(2,1)S(1)} %get-tuple-element.44), channel_id=1, source_target_pairs={{0,4},{1,5},{2,6},{3,7},{4,0},{5,1},{6,2},{7,3},{8,12},{9,13},{10,... | collective-permute-start | bytes 221192 | tf_op jit(solution)/shard_map/ppermute | solution.py:378
  90.1 6.5 %collective-permute-start.11 = (bf16[48,768]{1,0:T(8,128)(2,1)S(1)}, bf16[48,768]{1,0:T(8,128)(2,1)S(1)}, u32[]{:S(2)}, u32[]{:S(2)}) collective-permute-start(bf16[48,768]{1,0:T(8,128)(2,1)S(1)} %get-tuple-element.45), channel_id=1, source_target_pairs={{0,6},{1,7},{2,0},{3,1},{4,2},{5,3},{6,4},{7,5},{8,14},{9,15},{10,... | collective-permute-start | bytes 221192 | tf_op jit(solution)/shard_map/ppermute | solution.py:378

commit v6 on v5

--- a/solution.py
+++ b/solution.py
@@ -22,8 +22,6 @@
 LANES = 128
 VMEM_SPARE = 8 * 1024 * 1024
 PIECES = 2
-FRONT_UNROLL = 1
-BACK_UNROLL = 2
 
 
 def mm(a, b):
@@ -34,7 +32,7 @@
     return lax.dot_general(a, b, (((1,), (1,)), ((), ())), preferred_element_type=F32)
 
 
-def call(kernel, out_shape, *args, scratch=(), flops=0, raw_in=(), raw_out=(), copies=0):
+def call(kernel, out_shape, *args, scratch=(), flops=0, raw_in=(), raw_out=(), copies=0, near_in=(), near_out=()):
     outs = jax.tree.leaves(out_shape)
 
     def size(arrays):
@@ -47,8 +45,8 @@
     out_specs = [spec(i in raw_out) for i in range(len(outs))]
     taken = size(a for i, a in enumerate(args) if i not in raw_in) + size(a for i, a in enumerate(outs) if i not in raw_out)
     semaphores = [pltpu.SemaphoreType.DMA((copies,))] if copies else []
-    placed = [pltpu.HBM(a.shape, a.dtype) if i in raw_out else a for i, a in enumerate(outs)]
-    args = [pltpu.with_memory_space_constraint(a, pltpu.HBM) if i in raw_in else a for i, a in enumerate(args)]
+    placed = [pltpu.HBM(a.shape, a.dtype) if i in raw_out else pltpu.VMEM(a.shape, a.dtype) if i in near_out else a for i, a in enumerate(outs)]
+    args = [pltpu.with_memory_space_constraint(a, pltpu.HBM) if i in raw_in else pltpu.with_memory_space_constraint(a, pltpu.VMEM) if i in near_in else a for i, a in enumerate(args)]
     return pl.pallas_call(
         kernel,
         out_shape=placed if isinstance(out_shape, (tuple, list)) else placed[0],
@@ -86,7 +84,7 @@
 
 
 def forward_kernel(reach, x_ref, gain_ref, bias_ref, wqkv_hbm, *rest):
-    outs, (wqkv_ref, mine_ref, other_ref, q_ref, kt_ref, v_ref, prob_ref, mixed_ref, n_ref, k_ref, t_ref, sem) = rest[:7], rest[7:]
+    outs, (wqkv_ref, mine_ref, other_ref, q_ref, kt_ref, v_ref, prob_ref, mixed_ref, n_ref, k_ref, vt_ref, t_ref, weight_ref, sem) = rest[:7], rest[7:]
     tokens, width = x_ref.shape
     core = lax.axis_index("inner") & 1
     loads = []
@@ -114,45 +112,46 @@
         heads = pl.ds(2 * i, 2)
         return pltpu.make_async_copy(prob_ref.at[heads], outs[5].at[heads], sem.at[10 + i])
 
-    def pair(i, carry):
-        cols = pl.ds(pl.multiple_of(i * 128, 128), 128)
-        q2, k2, v2 = q_ref[:, cols], k_ref[:, cols], v_ref[:, cols]
+    spans = key_spans(tokens, reach)
+    for i in range(HEADS // 2):
+        cols = slice(i * 128, i * 128 + 128)
+        q2, k2 = q_ref[:, cols], k_ref[:, cols]
         kt_ref[cols, :] = (k2.astype(F32).T * SCALE).astype(BF)
-        v2t = v2.astype(F32).T.astype(BF)
+        vt_ref[cols, :] = v_ref[:, cols].astype(F32).T.astype(BF)
         for half in range(2):
             span = slice(half * 64, half * 64 + 64)
-            for b, (start, low, high) in enumerate(key_spans(tokens, reach)):
+            for b, (start, low, high) in enumerate(spans):
                 block = slice(start, start + LANES)
-                scores = mm_t(k2[low:high, span], q2[block, span]) + bias_ref[low:high, block]
-                grown = jnp.exp(scores - jnp.max(scores, axis=0, keepdims=True))
-                probs = grown * (1.0 / jnp.sum(grown, axis=0, keepdims=True))
-                prob_ref[2 * i + half, b, : high - low] = probs
-                rows = pl.ds(pl.multiple_of(i * 128 + half * 64, 64), 64)
-                mixt = mm(v2t[span, low:high], probs.astype(BF))
-                t_ref[rows, block] = mixt
-        prob_store(i).start()
-        return carry
-
-    lax.fori_loop(0, HEADS // 2, pair, 0, unroll=FRONT_UNROLL)
+                prob_ref[2 * i + half, b, : high - low] = mm_t(k2[low:high, span], q2[block, span])
     stores[3].start()
+    for h in range(HEADS):
+        for b, (start, low, high) in enumerate(spans):
+            scores = prob_ref[h, b, : high - low] + bias_ref[low:high, start : start + LANES]
+            grown = jnp.exp(scores - jnp.max(scores, axis=0, keepdims=True))
+            probs = grown * (1.0 / jnp.sum(grown, axis=0, keepdims=True))
+            prob_ref[h, b, : high - low] = probs
+            weight_ref[h, b, : high - low] = probs.astype(BF)
+        if h % 2:
+            prob_store(h // 2).start()
+    for h in range(HEADS):
+        rows = slice(h * HEAD_DIM, (h + 1) * HEAD_DIM)
+        for b, (start, low, high) in enumerate(spans):
+            t_ref[rows, start : start + LANES] = mm(vt_ref[rows, :][:, low:high], weight_ref[h, b, : high - low])
     mixed_ref[...] = t_ref[...].T.astype(BF)
     stores[6].start()
     split_rows(mine_ref, other_ref, 1, t_ref, core)
     stores[0].start()
     stores[1].start()
 
-    def finish(i, carry):
+    for i in range(HEADS // 2):
         prob_store(i).wait()
-        return carry
-
-    lax.fori_loop(0, HEADS // 2, finish, 0)
     for store in stores.values():
         store.wait()
 
 
 def backward_kernel(reach, cot_ref, *rest):
     sources, blocks_ref, rest = rest[:5], rest[5], rest[6:]
-    wout_ref, q_ref, kt_ref, v_ref, prob_ref, dqkv_ref, gm_ref, dqt_ref, sem = rest
+    wout_ref, q_ref, kt_ref, v_ref, prob_ref, dqkv_ref, gm_ref, dqt_ref, dots_ref, grad_ref, weight_ref, sem = rest
     tokens, width = cot_ref.shape
     targets = (wout_ref, q_ref, kt_ref, v_ref, prob_ref)
     loads = [pltpu.make_async_copy(src, dst, sem.at[i]) for i, (src, dst) in enumerate(zip(sources, targets))]
@@ -164,39 +163,30 @@
         load.wait()
     spans = key_spans(tokens, reach)
 
-    def widen(parts):
-        cols = []
-        for part, (_, low, high) in zip(parts, spans):
-            rows = [jnp.zeros((low, LANES), BF)] if low else []
-            rows += [part]
-            rows += [jnp.zeros((tokens - high, LANES), BF)] if high < tokens else []
-            cols.append(jnp.concatenate(rows, 0) if len(rows) > 1 else part)
-        return jnp.concatenate(cols, 1) if len(cols) > 1 else cols[0]
-
-    def pair(i, carry):
-        cols = pl.ds(pl.multiple_of(i * 128, 128), 128)
-        q2, g2, v2, kt2 = q_ref[:, cols], gm_ref[:, cols], v_ref[:, cols], kt_ref[cols, :]
-        dks, dvs = [], []
-        for half in range(2):
-            span = slice(half * 64, half * 64 + 64)
-            weights, grads = [], []
-            for b, (start, low, high) in enumerate(spans):
-                block = slice(start, start + LANES)
-                probs = prob_ref[2 * i + half, b, : high - low]
-                dots = mm_t(v2[low:high, span], g2[block, span])
-                centre = jnp.sum(probs * dots, axis=0, keepdims=True)
-                sgrad = (probs * (dots - centre)).astype(BF)
-                rows = pl.ds(pl.multiple_of(i * 128 + half * 64, 64), 64)
-                dqt_ref[rows, block] = mm(kt2[span, low:high], sgrad)
-                weights.append(probs.astype(BF))
-                grads.append(sgrad)
-            dks.append(mm(widen(grads), q2[:, span]))
-            dvs.append(mm(widen(weights), g2[:, span]))
-        dqkv_ref[:, pl.ds(pl.multiple_of(width + i * 128, 128), 128)] = jnp.concatenate(dks, 1).astype(BF)
-        dqkv_ref[:, pl.ds(pl.multiple_of(2 * width + i * 128, 128), 128)] = jnp.concatenate(dvs, 1).astype(BF)
-        return carry
-
-    lax.fori_loop(0, HEADS // 2, pair, 0, unroll=BACK_UNROLL)
+    for h in range(HEADS):
+        cols = slice(h * HEAD_DIM, (h + 1) * HEAD_DIM)
+        for b, (start, low, high) in enumerate(spans):
+            dots_ref[h, b, : high - low] = mm_t(v_ref[low:high, cols], gm_ref[start : start + LANES, cols])
+    for h in range(HEADS):
+        for b, (start, low, high) in enumerate(spans):
+            block = slice(start, start + LANES)
+            probs, dots = prob_ref[h, b, : high - low], dots_ref[h, b, : high - low]
+            centre = jnp.sum(probs * dots, axis=0, keepdims=True)
+            for dst, value in ((grad_ref, probs * (dots - centre)), (weight_ref, probs)):
+                dst[h, low:high, block] = value.astype(BF)
+                if low:
+                    dst[h, :low, block] = jnp.zeros((low, LANES), BF)
+                if high < tokens:
+                    dst[h, high:, block] = jnp.zeros((tokens - high, LANES), BF)
+    for i in range(HEADS // 2):
+        cols = slice(i * 128, i * 128 + 128)
+        q2, g2 = q_ref[:, cols], gm_ref[:, cols]
+        for at, source, right in ((1, grad_ref, q2), (2, weight_ref, g2)):
+            pair = [mm(source[2 * i + half], right[:, half * 64 : half * 64 + 64]) for half in range(2)]
+            dqkv_ref[:, at * width + i * 128 : at * width + i * 128 + 128] = jnp.concatenate(pair, 1).astype(BF)
+        for h in (2 * i, 2 * i + 1):
+            rows = slice(h * HEAD_DIM, (h + 1) * HEAD_DIM)
+            dqt_ref[rows, :] = mm(kt_ref[rows, :], grad_ref[h])
     dqkv_ref[:, :width] = dqt_ref[...].T.astype(BF)
     runs = blocks_ref.shape[0]
     wide, thin = 3 * width // runs, width // runs
@@ -322,26 +312,28 @@
             out_ref[n, z] = partial_sum(runs, run, keep_ref, got_refs, z).astype(BF)
 
 
-def rows_kernel(runs, keep_ref, *rest):
-    stages = runs.bit_length() - 1
-    got_refs, own_ref, send_refs = rest[:stages], rest[stages], rest[stages + 1 :]
-    count = keep_ref.shape[1]
+def first_row_kernel(runs, keep_ref, *rest):
+    got_refs, (send_ref, rest_ref) = rest[:-2], rest[-2:]
     me, run = lax.axis_index("inner") >> 1, lax.axis_index("tm")
-    for k, ref in enumerate(send_refs):
-        ref[...] = partial_sum(runs, run, keep_ref, got_refs, lax.rem(me + k + 1, count)).astype(BF)
-    own_ref[...] = partial_sum(runs, run, keep_ref, got_refs, me)
+    for n in range(send_ref.shape[0]):
+        z = spread_bits(n, [0])
+        rest_ref[n] = partial_sum(runs, run, keep_ref, got_refs, z | (me & 1))
+        send_ref[n] = partial_sum(runs, run, keep_ref, got_refs, z | (1 - (me & 1))).astype(BF)
+
+
+def row_kernel(stage, keep_ref, got_ref, send_ref, rest_ref):
+    bit = (lax.axis_index("inner") >> (stage + 1)) & 1
+    for n in range(send_ref.shape[0]):
+        rest_ref[n] = keep_ref[2 * n + bit] + got_ref[2 * n + bit].astype(F32)
+        other = 2 * n + 1 - bit
+        send_ref[n] = (keep_ref[other] + got_ref[other].astype(F32)).astype(BF)
 
 
 def last_kernel(inv_root, pieces, *rest):
-    got, (q_ref, o_ref) = rest[:-2], rest[-2:]
+    parts, (q_ref, o_ref) = rest[:-2], rest[-2:]
     rows, wide = q_ref.shape[0] // pieces, q_ref.shape[1]
-    each = len(got) // pieces
     for p in range(pieces):
-        own_ref, *others = got[p * each : (p + 1) * each]
-        total = own_ref[...]
-        for ref in others:
-            total = total + ref[...].astype(F32)
-        total = total * inv_root
+        total = (parts[2 * p][0] + parts[2 * p + 1][0].astype(F32)) * inv_root
         q_ref[p * rows : (p + 1) * rows] = total[:, :wide]
         o_ref[p * rows : (p + 1) * rows] = total[:, wide:]
 
@@ -357,25 +349,29 @@
 
     def product(chosen, send, dtype):
         out = (sds(shape, dtype),) * len(chosen)
-        return call(functools.partial(product_kernel, runs, chosen, send), out, *args, flops=len(chosen) * flops)
+        return call(functools.partial(product_kernel, runs, chosen, send), out, *args, flops=len(chosen) * flops, near_in=range(4), near_out=range(2))
 
     got = [[] for _ in range(pieces)]
     for p in range(pieces):
         send = product((p,), True, BF)[0]
         got[p].append(exchange(send, runs, inner, 0))
-    keep = product(tuple(range(pieces)), False, F32)
+    keep = list(product(tuple(range(pieces)), False, F32))
     for stage in range(1, stages):
         shape = (shape[0] // 2,) + shape[1:]
         for p in range(pieces):
             send = call(functools.partial(stage_kernel, runs, stage), sds(shape, BF), keep[p], *got[p])
             got[p].append(exchange(send, runs, inner, stage))
+    for stage in range(count.bit_length() - 1):
+        shape = (count >> (stage + 1), rows, lanes)
+        out = (sds(shape, BF), sds(shape, F32))
+        perm = [(i, i ^ (2 << stage)) for i in range(inner)]
+        for p in range(pieces):
+            body = functools.partial(row_kernel, stage) if stage else functools.partial(first_row_kernel, runs)
+            send, keep[p] = call(body, out, keep[p], *got[p])
+            got[p] = [lax.ppermute(send, "inner", perm)]
     last = []
-    block = (rows, lanes)
     for p in range(pieces):
-        own, *sends = call(functools.partial(rows_kernel, runs), (sds(block, F32),) + (sds(block, BF),) * (count - 1), keep[p], *got[p])
-        last.append(own)
-        for k, send in enumerate(sends):
-            last.append(lax.ppermute(send, "inner", [(i, (i + 2 * (k + 1)) % inner) for i in range(inner)]))
+        last += [keep[p], *got[p]]
     out = (sds((pieces * rows, lanes * 3 // 4), F32), sds((pieces * rows, lanes // 4), F32))
     return call(functools.partial(last_kernel, inv_root, pieces), out, *last)
 
@@ -402,6 +398,51 @@
     inside = (key % patches == query % patches) & (abs(key_f - query_f) <= WINDOW)
     inside = inside & (key_f // clip_len == query_f // clip_len)
     return jnp.where(inside, 0.0, -1e30).astype(F32)
+
+
+def attend(x, gain, w_qkv, bias, reach, inner):
+    tokens, width = x.shape
+    spans = key_spans(tokens, reach)
+    longest = max(high - low for _, low, high in spans)
+    sds, vmem = jax.ShapeDtypeStruct, pltpu.VMEM
+    halves = ((2, PIECES, inner // 2, width // inner // PIECES, tokens), BF)
+    flat, turned = ((tokens, width), BF), ((width, tokens), BF)
+    probs = ((HEADS, len(spans), longest, LANES), F32)
+    made = (halves, halves, flat, turned, flat, probs, flat)
+    return call(
+        functools.partial(forward_kernel, reach),
+        tuple(sds(*each) for each in made),
+        x,
+        gain,
+        bias,
+        w_qkv,
+        scratch=[vmem((3, width, width), BF), *(vmem(*each) for each in made), vmem(*flat), vmem(*flat), vmem(*turned), vmem((width, tokens), F32), vmem(probs[0], BF)],
+        flops=2 * tokens * width * 4 * width,
+        raw_in=(3,),
+        raw_out=range(7),
+        copies=10 + HEADS // 2,
+    )
+
+
+def attend_back(cot, w_out, q, kt, v, prob, reach, runs):
+    tokens, width = cot.shape
+    sds, vmem = jax.ShapeDtypeStruct, pltpu.VMEM
+    flat, turned, probs = (q.shape, BF), (kt.shape, BF), (prob.shape, F32)
+    made = ((runs, tokens, 4 * width // runs), BF)
+    return call(
+        functools.partial(backward_kernel, reach),
+        sds(*made),
+        cot,
+        w_out,
+        q,
+        kt,
+        v,
+        prob,
+        scratch=[*(vmem(*each) for each in (((width, width), BF), flat, turned, flat, probs)), vmem((tokens, 3 * width), BF), vmem(*flat), vmem((width, tokens), F32), vmem(*probs), vmem((HEADS, tokens, tokens), BF), vmem((HEADS, tokens, tokens), BF)],
+        flops=2 * tokens * width * 4 * width,
+        raw_in=range(1, 6),
+        copies=5,
+    )
 
 
 def shards(frames, norm_gain, w_qkv, w_out, cotangent):
@@ -422,39 +463,9 @@
 
     x = to_tubes(frames, count)
     cot = to_tubes(cotangent, count)
-    halves = ((2, PIECES, inner // 2, width // inner // PIECES, tokens), BF)
-    flat, turned = ((tokens, width), BF), ((width, tokens), BF)
-    probs = ((HEADS, len(spans), longest, LANES), F32)
-    made = (halves, halves, flat, turned, flat, probs, flat)
-    mine, other, q, kt, v, prob, mixed = call(
-        functools.partial(forward_kernel, reach),
-        tuple(sds(*each) for each in made),
-        x,
-        gain,
-        bias,
-        w_qkv,
-        scratch=[vmem((3, width, width), BF), *(vmem(*each) for each in made), vmem(*flat), vmem(*flat), vmem((width, tokens), F32)],
-        flops=2 * tokens * width * 4 * width,
-        raw_in=(3,),
-        raw_out=range(7),
-        copies=10 + HEADS // 2,
-    )
+    mine, other, q, kt, v, prob, mixed = attend(x, gain, w_qkv, bias, reach, inner)
     theirs = to_partner(other, inner)
-    made = ((runs, tokens, 4 * width // runs), BF)
-    blocks = call(
-        functools.partial(backward_kernel, reach),
-        sds(*made),
-        cot,
-        w_out,
-        q,
-        kt,
-        v,
-        prob,
-        scratch=[*(vmem(*each) for each in (((width, width), BF), flat, turned, flat, probs)), vmem((tokens, 3 * width), BF), vmem(*flat), vmem((width, tokens), F32)],
-        flops=2 * tokens * width * 4 * width,
-        raw_in=range(1, 6),
-        copies=5,
-    )
+    blocks = attend_back(cot, w_out, q, kt, v, prob, reach, runs)
     blocks_other = to_partner(blocks, inner)
     extra = -(-2 // (tokens // count)) * LANES
     back = call(

time: 97.8 us -> 95.5 us (0.976)
  waiting for transfers between devices: 26.1 us -> 35 us
  Pallas kernels: 26 us -> 17.9 us
  starting transfers between devices: 22.6 us -> 19.4 us
    pallas_call x12 -> x14, Pallas kernels: 26 us -> 17.9 us  [call(): pl.pallas_call(kernel, out_shape=placed if isinstance(out_shape, (tuple,...]
    all_to_all x1, waiting for transfers between devices: 2.16 us -> 7.24 us  [to_tubes(): parts = lax.all_to_all(parts, AXES, split_axis=0, concat_axis=0, tiled=True)]
    ppermute x4, waiting for transfers between devices: 19.6 us -> 23.2 us  [exchange(): return lax.ppermute(value, AXES, perm)]
    ppermute x6 -> x4, starting transfers between devices: 10.2 us -> 7.53 us  [reduce_weights(): got[p] = [lax.ppermute(send, 'inner', perm)]]
    ppermute x6 -> x4, waiting for transfers between devices: 2.55 us -> 2.72 us  [reduce_weights(): got[p] = [lax.ppermute(send, 'inner', perm)]]
  transfers between devices with their start and end apart: 14 -> 12, of which waited for: 5 -> 7; matrix products, arithmetic and copies ran while one was open for 0% -> 0% of each run, Pallas kernels for 18% -> 13%
where the time goes in v6:
time: 95.5 us; the launch traced here: 95.1 us
  waiting for transfers between devices  35 us (37%)
  blocking collectives  20.8 us (22%)
  starting transfers between devices  19.4 us (20%)
  Pallas kernels  17.9 us (19%)
  local copies, waits for them, and re-layouts  0.96 us (1%)
    ppermute x4, waiting for transfers between devices, exchange(): return lax.ppermute(value, AXES, perm)  23.2 us
    all_to_all x1, blocking collectives, to_tubes(): parts = lax.all_to_all(parts, AXES, split_axis=0, concat_axis=0, tiled=True)  20.8 us
    pallas_call x14, Pallas kernels, call(): pl.pallas_call(kernel, out_shape=placed if isinstance(out_shape, (tuple,...  17.9 us
    ppermute x4, starting transfers between devices, reduce_weights(): got[p] = [lax.ppermute(send, 'inner', perm)]  7.53 us
    all_to_all x1, waiting for transfers between devices, to_tubes(): parts = lax.all_to_all(parts, AXES, split_axis=0, concat_axis=0, tiled=True)  7.24 us
    ppermute x4, starting transfers between devices, exchange(): return lax.ppermute(value, AXES, perm)  5.38 us
    all_to_all x1, starting transfers between devices, to_frames(): parts = lax.all_to_all(parts, AXES, split_axis=0, concat_axis=0, tiled=True)  3.48 us
    ppermute x4, waiting for transfers between devices, reduce_weights(): got[p] = [lax.ppermute(send, 'inner', perm)]  2.72 us
  transfers between devices with their start and end apart: 12, of which 7 were waited for; matrix products, arithmetic and copies ran while one was open for 0% of the time, Pallas kernels for 13%

profile of v6, /device:TPU:0, one launch (start us, length us, event | category | flops | bytes accessed | tf_op | source)
XLA Modules:
  0.0 95.1 jit_solution(13868933906898673974)
XLA Ops:
  0.6 20.8 %all_to_all.15 = bf16[32,1,8,768]{3,2,1,0:T(8,128)(2,1)S(1)} all-to-all(bf16[32,1,8,768]{3,2,1,0:T(8,128)(2,1)} %bitcast.15), channel_id=1, replica_groups=mesh['tm'=4,'inner'=8] {'tm','inner'}, dimensions={0} | all-to-all | bytes 786432 | tf_op jit(solution)/shard_map/all_to_all | solution.py:382
  21.4 2.6 %all-to-all-start.1 = ((bf16[32,1,8,768]{3,2,1,0:T(8,128)(2,1)}), bf16[32,1,8,768]{3,2,1,0:T(8,128)(2,1)S(1)}, u32[]{:S(2)}, u32[]{:S(2)}) async-start(bf16[32,1,8,768]{3,2,1,0:T(8,128)(2,1)} %bitcast.19), calls=%async_computation.1 | async-start | bytes 786432 | tf_op jit(solution)/shard_map/all_to_all | solution.py:382
  24.1 0.3 fusion.15.bias_ref
  24.4 5.8 %shard_map.92 = (bf16[2,2,4,48,256]{4,3,2,1,0:T(8,128)(2,1)}, bf16[2,2,4,48,256]{4,3,2,1,0:T(8,128)(2,1)}, bf16[256,768]{1,0:T(8,128)(2,1)}, bf16[768,256]{1,0:T...) custom-call(bf16[256,768]{1,0:T(8,128)(2,1)S(1)} %bitcast.17, ...), custom_call_target="tpu_custom_call" | custom-call | flops 1207959552 | bytes 8522752 | tf_op jit(solution)/shard_map/pallas_call | solution.py:50
  30.2 7.2 %all-to-all-done.1 = bf16[32,1,8,768]{3,2,1,0:T(8,128)(2,1)S(1)} async-done(((bf16[32,1,8,768]{3,2,1,0:T(8,128)(2,1)}), bf16[32,1,8,768]{3,2,1,0:T(8,128)(2,1)S(1)}, u32[]{:S(2)}, u32[]{:S(2)}) %all-to-all-start.1) | async-done | bytes 393248 | tf_op jit(solution)/shard_map/all_to_all | solution.py:382
  37.4 4.7 %shard_map.93.blocks_ref.d_ref = bf16[4,256,768]{2,1,0:T(8,128)(2,1)S(1)} custom-call(bf16[256,768]{1,0:T(8,128)(2,1)S(1)} %bitcast.12, bf16[768,768]{1,0:T(8,128)(2,1)} %wout_ref.1, bf16[256,768]{1,0:T(8,128)(2,1)} %get-tuple-element.27.rest_1_, bf16[768,256]{1,0:T(8,128)(2,1)} %get-tuple-element.28.rest_2_, bf16[256,768]{1,0:T(8,128)(2,1)} %get-tuple-element.29.rest_3_, ...), custom_call_target="tpu_custom_call" | custom-call | flops 1207959552 | bytes 6291456 | tf_op jit(solution)/shard_map/pallas_call | solution.py:50
  42.1 0.2 collective-permute-start.1
  42.3 1.5 %shard_map.94 = bf16[256,1664]{1,0:T(8,128)(2,1)S(1)} custom-call(bf16[256,768]{1,0:T(8,128)(2,1)S(1)} %bitcast.18, bf16[256,768]{1,0:T(8,128)(2,1)S(1)} %bitcast.13, f32[1,768]{1,0:T(1,128)S(1)} %reshape.37.gain_ref, bf16[4,256,768]{2,1,0:T(8,128)(2,1)S(1)} %shard_map.93.blocks_ref.d_ref, bf16[768,2304]{1,0:T(8,128)(2,1)S(1)} %copy-done.1, ...), custom_call_target="tpu_custom_call" | custom-call | flops 905969664 | bytes 7146496 | tf_op jit(solution)/shard_map/pallas_call | solution.py:50
  43.8 0.9 copy-done.3
  44.8 3.5 %all-to-all-start.2 = ((bf16[32,1,8,1664]{3,2,1,0:T(8,128)(2,1)}), bf16[32,1,8,1664]{3,2,1,0:T(8,128)(2,1)}, u32[]{:S(2)}, u32[]{:S(2)}) async-start(bf16[32,1,8,1664]{3,2,1,0:T(8,128)(2,1)} %bitcast.14), calls=%async_computation.2 | async-start | bytes 1703936 | tf_op jit(solution)/shard_map/all_to_all | solution.py:389
  48.3 0.2 collective-permute-start
  48.5 1.8 %collective-permute-done.other_ref = bf16[2,2,4,48,256]{4,3,2,1,0:T(8,128)(2,1)S(1)} collective-permute-done((bf16[2,2,4,48,256]{4,3,2,1,0:T(8,128)(2,1)}, bf16[2,2,4,48,256]{4,3,2,1,0:T(8,128)(2,1)S(1)}, u32[]{:S(2)}, u32[]{:S(2)}) %collective-permute-start) | collective-permute-done | bytes 393248 | tf_op jit(solution)/shard_map/ppermute | solution.py:281
  50.3 0.6 shard_map.97
  50.9 1.6 %collective-permute-start.2 = (bf16[2,4,48,768]{3,2,1,0:T(8,128)(2,1)S(1)}, bf16[2,4,48,768]{3,2,1,0:T(8,128)(2,1)S(1)}, u32[]{:S(2)}, u32[]{:S(2)}) collective-permute-start(bf16[2,4,48,768]{3,2,1,0:T(8,128)(2,1)S(1)} %shard_map.97), channel_id=1, source_target_pairs={{0,8},{1,17},{2,10},{3,19},{4,12},{5,21},{6,14},{7,23},{8,0},{9,25... | collective-permute-start | bytes 1769480 | tf_op jit(solution)/shard_map/ppermute | solution.py:277
  52.5 0.6 shard_map.101
  53.2 0.5 collective-permute-start.6
  53.7 1.0 %shard_map.96 = (f32[2,4,48,768]{3,2,1,0:T(8,128)S(1)}, f32[2,4,48,768]{3,2,1,0:T(8,128)S(1)}) custom-call(bf16[2,2,4,48,256]{4,3,2,1,0:T(8,128)(2,1)S(1)} %copy-done.2, bf16[2,2,4,48,256]{4,3,2,1,0:T(8,128)(2,1)S(1)} %collective-permute-done.other_ref, bf16[4,256,768]{2,1,0:T(8,128)(2,1)S(1)} %shard_map.93.blocks_ref.d_ref, ...), custom_call_target="tpu_custom_call" | custom-call | flops 603979776 | bytes 6291456 | tf_op jit(solution)/shard_map/pallas_call | solution.py:50
  54.7 9.7 %collective-permute-done.2.rest_0_ = bf16[2,4,48,768]{3,2,1,0:T(8,128)(2,1)S(1)} collective-permute-done((bf16[2,4,48,768]{3,2,1,0:T(8,128)(2,1)S(1)}, bf16[2,4,48,768]{3,2,1,0:T(8,128)(2,1)S(1)}, u32[]{:S(2)}, u32[]{:S(2)}) %collective-permute-start.2) | collective-permute-done | bytes 589856 | tf_op jit(solution)/shard_map/ppermute | solution.py:277
  64.5 1.6 %collective-permute-start.3 = (bf16[1,4,48,768]{3,2,1,0:T(8,128)(2,1)S(1)}, bf16[1,4,48,768]{3,2,1,0:T(8,128)(2,1)S(1)}, u32[]{:S(2)}, u32[]{:S(2)}) collective-permute-start(bf16[1,4,48,768]{3,2,1,0:T(8,128)(2,1)S(1)} %shard_map.98), channel_id=1, source_target_pairs={{0,16},{1,9},{2,18},{3,11},{4,20},{5,13},{6,22},{7,15},{8,24},{9,1... | collective-permute-start | bytes 884744 | tf_op jit(solution)/shard_map/ppermute | solution.py:277
  66.1 9.9 %collective-permute-done.6.rest_0_ = bf16[2,4,48,768]{3,2,1,0:T(8,128)(2,1)S(1)} collective-permute-done((bf16[2,4,48,768]{3,2,1,0:T(8,128)(2,1)S(1)}, bf16[2,4,48,768]{3,2,1,0:T(8,128)(2,1)S(1)}, u32[]{:S(2)}, u32[]{:S(2)}) %collective-permute-start.6) | collective-permute-done | bytes 589856 | tf_op jit(solution)/shard_map/ppermute | solution.py:277
  76.1 1.6 %collective-permute-start.7 = (bf16[1,4,48,768]{3,2,1,0:T(8,128)(2,1)S(1)}, bf16[1,4,48,768]{3,2,1,0:T(8,128)(2,1)S(1)}, u32[]{:S(2)}, u32[]{:S(2)}) collective-permute-start(bf16[1,4,48,768]{3,2,1,0:T(8,128)(2,1)S(1)} %shard_map.102), channel_id=1, source_target_pairs={{0,16},{1,9},{2,18},{3,11},{4,20},{5,13},{6,22},{7,15},{8,24},{9,1... | collective-permute-start | bytes 884744 | tf_op jit(solution)/shard_map/ppermute | solution.py:277
  77.7 0.1 shard_map.99
  77.8 1.5 %collective-permute-start.4 = (bf16[2,48,768]{2,1,0:T(8,128)(2,1)S(1)}, bf16[2,48,768]{2,1,0:T(8,128)(2,1)S(1)}, u32[]{:S(2)}, u32[]{:S(2)}) collective-permute-start(bf16[2,48,768]{2,1,0:T(8,128)(2,1)S(1)} %get-tuple-element.38), channel_id=1, source_target_pairs={{0,2},{1,3},{2,0},{3,1},{4,6},{5,7},{6,4},{7,5},{8,10},{9,11},{10,... | collective-permute-start | bytes 442376 | tf_op jit(solution)/shard_map/ppermute | solution.py:371
  79.3 3.6 %collective-permute-done.7.rest_1_ = bf16[1,4,48,768]{3,2,1,0:T(8,128)(2,1)S(1)} collective-permute-done((bf16[1,4,48,768]{3,2,1,0:T(8,128)(2,1)S(1)}, bf16[1,4,48,768]{3,2,1,0:T(8,128)(2,1)S(1)}, u32[]{:S(2)}, u32[]{:S(2)}) %collective-permute-start.7) | collective-permute-done | bytes 294944 | tf_op jit(solution)/shard_map/ppermute | solution.py:277
  82.9 0.1 shard_map.103
  83.0 1.5 %collective-permute-start.8 = (bf16[2,48,768]{2,1,0:T(8,128)(2,1)S(1)}, bf16[2,48,768]{2,1,0:T(8,128)(2,1)S(1)}, u32[]{:S(2)}, u32[]{:S(2)}) collective-permute-start(bf16[2,48,768]{2,1,0:T(8,128)(2,1)S(1)} %get-tuple-element.43), channel_id=1, source_target_pairs={{0,2},{1,3},{2,0},{3,1},{4,6},{5,7},{6,4},{7,5},{8,10},{9,11},{10,... | collective-permute-start | bytes 442376 | tf_op jit(solution)/shard_map/ppermute | solution.py:371
  84.5 2.2 %collective-permute-start.5 = (bf16[1,48,768]{2,1,0:T(8,128)(2,1)S(1)}, bf16[1,48,768]{2,1,0:T(8,128)(2,1)S(1)}, u32[]{:S(2)}, u32[]{:S(2)}) collective-permute-start(bf16[1,48,768]{2,1,0:T(8,128)(2,1)S(1)} %get-tuple-element.40), channel_id=1, source_target_pairs={{0,4},{1,5},{2,6},{3,7},{4,0},{5,1},{6,2},{7,3},{8,12},{9,13},{10,... | collective-permute-start | bytes 221192 | tf_op jit(solution)/shard_map/ppermute | solution.py:371
  86.7 2.3 %collective-permute-done.8.got_ref = bf16[2,48,768]{2,1,0:T(8,128)(2,1)S(1)} collective-permute-done((bf16[2,48,768]{2,1,0:T(8,128)(2,1)S(1)}, bf16[2,48,768]{2,1,0:T(8,128)(2,1)S(1)}, u32[]{:S(2)}, u32[]{:S(2)}) %collective-permute-start.8) | collective-permute-done | bytes 147488 | tf_op jit(solution)/shard_map/ppermute | solution.py:371
  89.0 2.4 %collective-permute-start.9 = (bf16[1,48,768]{2,1,0:T(8,128)(2,1)S(1)}, bf16[1,48,768]{2,1,0:T(8,128)(2,1)S(1)}, u32[]{:S(2)}, u32[]{:S(2)}) collective-permute-start(bf16[1,48,768]{2,1,0:T(8,128)(2,1)S(1)} %get-tuple-element.45), channel_id=1, source_target_pairs={{0,4},{1,5},{2,6},{3,7},{4,0},{5,1},{6,2},{7,3},{8,12},{9,13},{10,... | collective-permute-start | bytes 221192 | tf_op jit(solution)/shard_map/ppermute | solution.py:371
  91.4 2.5 %shard_map.95 = (bf16[256,768]{1,0:T(8,128)(2,1)}, bf16[256,768]{1,0:T(8,128)(2,1)}, f32[1,96]{1,0:T(1,128)}) custom-call(bf16[256,768]{1,0:T(8,128)(2,1)S(1)} %bitcast.16, bf16[768,768]{1,0:T(8,128)(2,1)S(1)} %copy-done, bf16[256,1664]{1,0:T(8,128)(2,1)} %bitcast.7.back_ref), custom_call_target="tpu_custom_call" | custom-call | flops 301989888 | bytes 3211648 | tf_op jit(solution)/shard_map/pallas_call | solution.py:50
  93.9 0.4 collective-permute-done.9.rest_3_
  94.3 0.8 shard_map.105
  (30 shorter events, 0.2 us)
Async XLA Ops:
  0.6 23.4 %copy-start.8 = (f32[768]{0:T(1024)S(1)}, f32[768]{0:T(1024)}, u32[]{:S(2)}) copy-start(f32[768]{0:T(1024)} %param.6) | copy-start | bytes 9220
  21.4 8.8 %copy-start.5 = (bf16[32,1,8,768]{3,2,1,0:T(8,128)(2,1)}, bf16[32,1,8,768]{3,2,1,0:T(8,128)(2,1)S(1)}, u32[]{:S(2)}) copy-start(bf16[32,1,8,768]{3,2,1,0:T(8,128)(2,1)S(1)} %all_to_all.15) | copy-start | bytes 1179652
  21.4 16.0 %all-to-all-start.1 = ((bf16[32,1,8,768]{3,2,1,0:T(8,128)(2,1)}), bf16[32,1,8,768]{3,2,1,0:T(8,128)(2,1)S(1)}, u32[]{:S(2)}, u32[]{:S(2)}) async-start(bf16[32,1,8,768]{3,2,1,0:T(8,128)(2,1)} %bitcast.19), calls=%async_computation.1 | async-start | bytes 786432 | tf_op jit(solution)/shard_map/all_to_all | solution.py:382
  37.4 4.9 %copy-start.1 = (bf16[768,2304]{1,0:T(8,128)(2,1)S(1)}, bf16[768,2304]{1,0:T(8,128)(2,1)}, u32[]{:S(2)}) copy-start(bf16[768,2304]{1,0:T(8,128)(2,1)} %wqkv_ref.1) | copy-start | bytes 10616836
  37.4 4.9 %copy-start.6 = (bf16[32,1,8,768]{3,2,1,0:T(8,128)(2,1)S(1)}, bf16[32,1,8,768]{3,2,1,0:T(8,128)(2,1)}, u32[]{:S(2)}) copy-start(bf16[32,1,8,768]{3,2,1,0:T(8,128)(2,1)} %copy-done.5) | copy-start | bytes 1179652
  37.4 4.9 %copy-start.7 = (bf16[256,768]{1,0:T(8,128)(2,1)S(1)}, bf16[256,768]{1,0:T(8,128)(2,1)}, u32[]{:S(2)}) copy-start(bf16[256,768]{1,0:T(8,128)(2,1)} %get-tuple-element.31.mixed_ref) | copy-start | bytes 1179652
  42.1 8.1 %collective-permute-start.1 = (bf16[4,256,768]{2,1,0:T(8,128)(2,1)S(1)}, bf16[4,256,768]{2,1,0:T(8,128)(2,1)S(1)}, u32[]{:S(2)}, u32[]{:S(2)}) collective-permute-start(bf16[4,256,768]{2,1,0:T(8,128)(2,1)S(1)} %shard_map.93.blocks_ref.d_ref), channel_id=1, source_target_pairs={{0,1},{1,0},{2,3},{3,2},{4,5},{5,4},{6,7},{7,6},{8,9},{9,8},{10,11... | collective-permute-start | bytes 4718600 | tf_op jit(solution)/shard_map/ppermute | solution.py:281
  43.8 0.9 copy-start.3
  44.8 5.5 %copy-start.2 = (bf16[2,2,4,48,256]{4,3,2,1,0:T(8,128)(2,1)S(1)}, bf16[2,2,4,48,256]{4,3,2,1,0:T(8,128)(2,1)}, u32[]{:S(2)}) copy-start(bf16[2,2,4,48,256]{4,3,2,1,0:T(8,128)(2,1)} %get-tuple-element.34.mine_ref) | copy-start | bytes 1179652
  44.8 46.7 %all-to-all-start.2 = ((bf16[32,1,8,1664]{3,2,1,0:T(8,128)(2,1)}), bf16[32,1,8,1664]{3,2,1,0:T(8,128)(2,1)}, u32[]{:S(2)}, u32[]{:S(2)}) async-start(bf16[32,1,8,1664]{3,2,1,0:T(8,128)(2,1)} %bitcast.14), calls=%async_computation.2 | async-start | bytes 1703936 | tf_op jit(solution)/shard_map/all_to_all | solution.py:389
  48.3 2.0 %collective-permute-start = (bf16[2,2,4,48,256]{4,3,2,1,0:T(8,128)(2,1)}, bf16[2,2,4,48,256]{4,3,2,1,0:T(8,128)(2,1)S(1)}, u32[]{:S(2)}, u32[]{:S(2)}) collective-permute-start(bf16[2,2,4,48,256]{4,3,2,1,0:T(8,128)(2,1)} %get-tuple-element.35), channel_id=1, source_target_pairs={{0,1},{1,0},{2,3},{3,2},{4,5},{5,4},{6,7},{7,6},{8,9},{9,8},{10,11... | collective-permute-start | bytes 1179656 | tf_op jit(solution)/shard_map/ppermute | solution.py:281
  50.9 13.5 %collective-permute-start.2 = (bf16[2,4,48,768]{3,2,1,0:T(8,128)(2,1)S(1)}, bf16[2,4,48,768]{3,2,1,0:T(8,128)(2,1)S(1)}, u32[]{:S(2)}, u32[]{:S(2)}) collective-permute-start(bf16[2,4,48,768]{3,2,1,0:T(8,128)(2,1)S(1)} %shard_map.97), channel_id=1, source_target_pairs={{0,8},{1,17},{2,10},{3,19},{4,12},{5,21},{6,14},{7,23},{8,0},{9,25... | collective-permute-start | bytes 1769480 | tf_op jit(solution)/shard_map/ppermute | solution.py:277
  53.2 22.9 %collective-permute-start.6 = (bf16[2,4,48,768]{3,2,1,0:T(8,128)(2,1)S(1)}, bf16[2,4,48,768]{3,2,1,0:T(8,128)(2,1)S(1)}, u32[]{:S(2)}, u32[]{:S(2)}) collective-permute-start(bf16[2,4,48,768]{3,2,1,0:T(8,128)(2,1)S(1)} %shard_map.101), channel_id=1, source_target_pairs={{0,8},{1,17},{2,10},{3,19},{4,12},{5,21},{6,14},{7,23},{8,0},{9,25... | collective-permute-start | bytes 1769480 | tf_op jit(solution)/shard_map/ppermute | solution.py:277
  64.5 13.2 %collective-permute-start.3 = (bf16[1,4,48,768]{3,2,1,0:T(8,128)(2,1)S(1)}, bf16[1,4,48,768]{3,2,1,0:T(8,128)(2,1)S(1)}, u32[]{:S(2)}, u32[]{:S(2)}) collective-permute-start(bf16[1,4,48,768]{3,2,1,0:T(8,128)(2,1)S(1)} %shard_map.98), channel_id=1, source_target_pairs={{0,16},{1,9},{2,18},{3,11},{4,20},{5,13},{6,22},{7,15},{8,24},{9,1... | collective-permute-start | bytes 884744 | tf_op jit(solution)/shard_map/ppermute | solution.py:277
  76.1 6.8 %collective-permute-start.7 = (bf16[1,4,48,768]{3,2,1,0:T(8,128)(2,1)S(1)}, bf16[1,4,48,768]{3,2,1,0:T(8,128)(2,1)S(1)}, u32[]{:S(2)}, u32[]{:S(2)}) collective-permute-start(bf16[1,4,48,768]{3,2,1,0:T(8,128)(2,1)S(1)} %shard_map.102), channel_id=1, source_target_pairs={{0,16},{1,9},{2,18},{3,11},{4,20},{5,13},{6,22},{7,15},{8,24},{9,1... | collective-permute-start | bytes 884744 | tf_op jit(solution)/shard_map/ppermute | solution.py:277
  77.8 13.6 %copy-start = (bf16[768,768]{1,0:T(8,128)(2,1)S(1)}, bf16[768,768]{1,0:T(8,128)(2,1)}, u32[]{:S(2)}) copy-start(bf16[768,768]{1,0:T(8,128)(2,1)} %wout_ref.1) | copy-start | bytes 3538948
  77.8 13.6 %copy-start.4 = (bf16[1,256,768]{2,1,0:T(8,128)(2,1)S(1)}, bf16[1,256,768]{2,1,0:T(8,128)(2,1)}, u32[]{:S(2)}) copy-start(bf16[1,256,768]{2,1,0:T(8,128)(2,1)} %param.5) | copy-start | bytes 1179652
  77.8 6.7 %collective-permute-start.4 = (bf16[2,48,768]{2,1,0:T(8,128)(2,1)S(1)}, bf16[2,48,768]{2,1,0:T(8,128)(2,1)S(1)}, u32[]{:S(2)}, u32[]{:S(2)}) collective-permute-start(bf16[2,48,768]{2,1,0:T(8,128)(2,1)S(1)} %get-tuple-element.38), channel_id=1, source_target_pairs={{0,2},{1,3},{2,0},{3,1},{4,6},{5,7},{6,4},{7,5},{8,10},{9,11},{10,... | collective-permute-start | bytes 442376 | tf_op jit(solution)/shard_map/ppermute | solution.py:371
  83.0 6.0 %collective-permute-start.8 = (bf16[2,48,768]{2,1,0:T(8,128)(2,1)S(1)}, bf16[2,48,768]{2,1,0:T(8,128)(2,1)S(1)}, u32[]{:S(2)}, u32[]{:S(2)}) collective-permute-start(bf16[2,48,768]{2,1,0:T(8,128)(2,1)S(1)} %get-tuple-element.43), channel_id=1, source_target_pairs={{0,2},{1,3},{2,0},{3,1},{4,6},{5,7},{6,4},{7,5},{8,10},{9,11},{10,... | collective-permute-start | bytes 442376 | tf_op jit(solution)/shard_map/ppermute | solution.py:371
  84.5 9.4 %collective-permute-start.5 = (bf16[1,48,768]{2,1,0:T(8,128)(2,1)S(1)}, bf16[1,48,768]{2,1,0:T(8,128)(2,1)S(1)}, u32[]{:S(2)}, u32[]{:S(2)}) collective-permute-start(bf16[1,48,768]{2,1,0:T(8,128)(2,1)S(1)} %get-tuple-element.40), channel_id=1, source_target_pairs={{0,4},{1,5},{2,6},{3,7},{4,0},{5,1},{6,2},{7,3},{8,12},{9,13},{10,... | collective-permute-start | bytes 221192 | tf_op jit(solution)/shard_map/ppermute | solution.py:371
  89.0 5.3 %collective-permute-start.9 = (bf16[1,48,768]{2,1,0:T(8,128)(2,1)S(1)}, bf16[1,48,768]{2,1,0:T(8,128)(2,1)S(1)}, u32[]{:S(2)}, u32[]{:S(2)}) collective-permute-start(bf16[1,48,768]{2,1,0:T(8,128)(2,1)S(1)} %get-tuple-element.45), channel_id=1, source_target_pairs={{0,4},{1,5},{2,6},{3,7},{4,0},{5,1},{6,2},{7,3},{8,12},{9,13},{10,... | collective-permute-start | bytes 221192 | tf_op jit(solution)/shard_map/ppermute | solution.py:371

commit v7 on v6

--- a/solution.py
+++ b/solution.py
@@ -21,7 +21,6 @@
 AXES = ("tm", "inner")
 LANES = 128
 VMEM_SPARE = 8 * 1024 * 1024
-PIECES = 2
 
 
 def mm(a, b):
@@ -74,13 +73,11 @@
 
 
 def split_rows(mine_ref, other_ref, slot, src_ref, core):
-    pieces, count, rows = mine_ref.shape[1:4]
+    count, rows = mine_ref.shape[1:3]
     for z in range(count):
         for dst, which in ((mine_ref, core), (other_ref, 1 - core)):
-            start = pl.multiple_of((2 * z + which) * pieces * rows, 8)
-            block = src_ref[pl.ds(start, pieces * rows), :].astype(BF)
-            for p in range(pieces):
-                dst[slot, p, z] = block[p * rows : (p + 1) * rows]
+            start = pl.multiple_of((2 * z + which) * rows, 8)
+            dst[slot, z] = src_ref[pl.ds(start, rows), :].astype(BF)
 
 
 def forward_kernel(reach, x_ref, gain_ref, bias_ref, wqkv_hbm, *rest):
@@ -281,44 +278,50 @@
     return lax.ppermute(value, "inner", [(i, i ^ 1) for i in range(inner)])
 
 
-def product_kernel(runs, pieces, send, mine_ref, other_ref, d_ref, d_other_ref, *out_refs):
-    _, _, count, rows, tokens = mine_ref.shape
-    for piece, out_ref in zip(pieces, out_refs):
-        wide = out_ref.shape[3] * 3 // 4
-        for n in range(out_ref.shape[0]):
-            run = run_of(runs, 0, n, send)
-            totals = []
-            for slot, cols in ((0, slice(0, wide)), (1, slice(wide, None))):
-                left = mine_ref[slot, piece].reshape(count * rows, tokens)
-                right = other_ref[slot, piece].reshape(count * rows, tokens)
-                totals.append(mm(left, d_ref[run, :, cols]) + mm(right, d_other_ref[run, :, cols]))
-            total = jnp.concatenate(totals, 1).astype(out_ref.dtype)
-            for z in range(count):
-                out_ref[n, z] = total[z * rows : (z + 1) * rows]
-
-
-def partial_sum(runs, run, keep_ref, got_refs, z):
-    total = keep_ref[place_of(runs, 0, run), z]
+def pieces_of(rows):
+    cut = rows // 2
+    return ((0, cut), (cut, rows))
+
+
+def product_kernel(pieces, choose, mine_ref, other_ref, d_ref, d_other_ref, *out_refs):
+    _, count, _, tokens = mine_ref.shape
+    for index, (low, high) in enumerate(pieces):
+        refs = out_refs[index * len(out_refs) // len(pieces) : (index + 1) * len(out_refs) // len(pieces)]
+        wide = d_ref.shape[2] * 3 // 4
+        for out_ref, runs in zip(refs, choose()):
+            for n, run in enumerate(runs):
+                totals = []
+                for slot, cols in ((0, slice(0, wide)), (1, slice(wide, None))):
+                    left = mine_ref[slot, :, low:high].reshape(count * (high - low), tokens)
+                    right = other_ref[slot, :, low:high].reshape(count * (high - low), tokens)
+                    totals.append(mm(left, d_ref[run, :, cols]) + mm(right, d_other_ref[run, :, cols]))
+                total = jnp.concatenate(totals, 1).astype(out_ref.dtype)
+                for z in range(count):
+                    out_ref[n, z] = total[z * (high - low) : (z + 1) * (high - low)]
+
+
+def partial_sum(runs, run, own_ref, n, got_refs, z):
+    total = own_ref[n, z]
     for stage, ref in enumerate(got_refs):
         total = total + ref[place_of(runs, stage, run), z].astype(F32)
     return total
 
 
-def stage_kernel(runs, stage, keep_ref, *rest):
+def stage_kernel(runs, stage, own_ref, *rest):
     got_refs, out_ref = rest[:-1], rest[-1]
     for n in range(out_ref.shape[0]):
         run = run_of(runs, stage, n, True)
         for z in range(out_ref.shape[1]):
-            out_ref[n, z] = partial_sum(runs, run, keep_ref, got_refs, z).astype(BF)
-
-
-def first_row_kernel(runs, keep_ref, *rest):
+            out_ref[n, z] = partial_sum(runs, run, own_ref, n, got_refs, z).astype(BF)
+
+
+def first_row_kernel(runs, own_ref, *rest):
     got_refs, (send_ref, rest_ref) = rest[:-2], rest[-2:]
     me, run = lax.axis_index("inner") >> 1, lax.axis_index("tm")
     for n in range(send_ref.shape[0]):
         z = spread_bits(n, [0])
-        rest_ref[n] = partial_sum(runs, run, keep_ref, got_refs, z | (me & 1))
-        send_ref[n] = partial_sum(runs, run, keep_ref, got_refs, z | (1 - (me & 1))).astype(BF)
+        rest_ref[n] = partial_sum(runs, run, own_ref, 0, got_refs, z | (me & 1))
+        send_ref[n] = partial_sum(runs, run, own_ref, 0, got_refs, z | (1 - (me & 1))).astype(BF)
 
 
 def row_kernel(stage, keep_ref, got_ref, send_ref, rest_ref):
@@ -329,51 +332,58 @@
         send_ref[n] = (keep_ref[other] + got_ref[other].astype(F32)).astype(BF)
 
 
-def last_kernel(inv_root, pieces, *rest):
+def last_kernel(inv_root, *rest):
     parts, (q_ref, o_ref) = rest[:-2], rest[-2:]
-    rows, wide = q_ref.shape[0] // pieces, q_ref.shape[1]
-    for p in range(pieces):
+    wide = q_ref.shape[1]
+    for p, (low, high) in enumerate(pieces_of(q_ref.shape[0])):
         total = (parts[2 * p][0] + parts[2 * p + 1][0].astype(F32)) * inv_root
-        q_ref[p * rows : (p + 1) * rows] = total[:, :wide]
-        o_ref[p * rows : (p + 1) * rows] = total[:, wide:]
+        q_ref[low:high] = total[:, :wide]
+        o_ref[low:high] = total[:, wide:]
 
 
 def reduce_weights(mine, other, d, d_other, runs, inner, inv_root):
     sds = jax.ShapeDtypeStruct
-    _, pieces, count, rows, tokens = mine.shape
+    _, count, rows, tokens = mine.shape
     lanes = d.shape[2]
     stages = runs.bit_length() - 1
-    shape = (runs // 2, count, rows, lanes)
-    flops = 4 * count * rows * tokens * lanes * (runs // 2)
+    pieces = pieces_of(rows)
     args = (mine, other, d, d_other)
 
-    def product(chosen, send, dtype):
-        out = (sds(shape, dtype),) * len(chosen)
-        return call(functools.partial(product_kernel, runs, chosen, send), out, *args, flops=len(chosen) * flops, near_in=range(4), near_out=range(2))
-
-    got = [[] for _ in range(pieces)]
-    for p in range(pieces):
-        send = product((p,), True, BF)[0]
+    def wanted(stage):
+        if stage == stages:
+            return [lax.axis_index("tm")]
+        return [run_of(runs, stage, n, True) for n in range(runs >> (stage + 1))]
+
+    def product(chosen, which, dtype):
+        shapes = [(max(runs >> (stage + 1), 1), count, high - low, lanes) for low, high in chosen for stage in which]
+        flops = sum(4 * math.prod(shape) * tokens for shape in shapes)
+        body = functools.partial(product_kernel, chosen, lambda: [wanted(stage) for stage in which])
+        return call(body, tuple(sds(shape, dtype) for shape in shapes), *args, flops=flops, near_in=range(4), near_out=range(len(shapes)))
+
+    got = [[] for _ in pieces]
+    for p, piece in enumerate(pieces):
+        send = product((piece,), (0,), BF)[0]
         got[p].append(exchange(send, runs, inner, 0))
-    keep = list(product(tuple(range(pieces)), False, F32))
+    later = product(pieces, tuple(range(1, stages + 1)), F32)
+    own = [later[p * stages : (p + 1) * stages] for p in range(len(pieces))]
     for stage in range(1, stages):
-        shape = (shape[0] // 2,) + shape[1:]
-        for p in range(pieces):
-            send = call(functools.partial(stage_kernel, runs, stage), sds(shape, BF), keep[p], *got[p])
+        for p in range(len(pieces)):
+            body = functools.partial(stage_kernel, runs, stage)
+            send = call(body, sds(own[p][stage - 1].shape, BF), own[p][stage - 1], *got[p])
             got[p].append(exchange(send, runs, inner, stage))
+    keep = [each[-1] for each in own]
     for stage in range(count.bit_length() - 1):
-        shape = (count >> (stage + 1), rows, lanes)
-        out = (sds(shape, BF), sds(shape, F32))
         perm = [(i, i ^ (2 << stage)) for i in range(inner)]
-        for p in range(pieces):
+        for p, (low, high) in enumerate(pieces):
+            shape = (count >> (stage + 1), high - low, lanes)
             body = functools.partial(row_kernel, stage) if stage else functools.partial(first_row_kernel, runs)
-            send, keep[p] = call(body, out, keep[p], *got[p])
+            send, keep[p] = call(body, (sds(shape, BF), sds(shape, F32)), keep[p], *got[p])
             got[p] = [lax.ppermute(send, "inner", perm)]
     last = []
-    for p in range(pieces):
+    for p in range(len(pieces)):
         last += [keep[p], *got[p]]
-    out = (sds((pieces * rows, lanes * 3 // 4), F32), sds((pieces * rows, lanes // 4), F32))
-    return call(functools.partial(last_kernel, inv_root, pieces), out, *last)
+    out = (sds((rows, lanes * 3 // 4), F32), sds((rows, lanes // 4), F32))
+    return call(functools.partial(last_kernel, inv_root), out, *last)
 
 
 def to_tubes(rows, count):
@@ -405,7 +415,7 @@
     spans = key_spans(tokens, reach)
     longest = max(high - low for _, low, high in spans)
     sds, vmem = jax.ShapeDtypeStruct, pltpu.VMEM
-    halves = ((2, PIECES, inner // 2, width // inner // PIECES, tokens), BF)
+    halves = ((2, inner // 2, width // inner, tokens), BF)
     flat, turned = ((tokens, width), BF), ((width, tokens), BF)
     probs = ((HEADS, len(spans), longest, LANES), F32)
     made = (halves, halves, flat, turned, flat, probs, flat)

time: 95.5 us -> 95.5 us (level)
  no operation moved by 1% of the time
where the time goes in v7:
time: 95.5 us; the launch traced here: 95.1 us
  waiting for transfers between devices  35 us (37%)
  blocking collectives  20.8 us (22%)
  starting transfers between devices  19.4 us (20%)
  Pallas kernels  17.9 us (19%)
  local copies, waits for them, and re-layouts  0.96 us (1%)
    ppermute x4, waiting for transfers between devices, exchange(): return lax.ppermute(value, AXES, perm)  23.2 us
    all_to_all x1, blocking collectives, to_tubes(): parts = lax.all_to_all(parts, AXES, split_axis=0, concat_axis=0, tiled=True)  20.8 us
    pallas_call x14, Pallas kernels, call(): pl.pallas_call(kernel, out_shape=placed if isinstance(out_shape, (tuple,...  17.9 us
    ppermute x4, starting transfers between devices, reduce_weights(): got[p] = [lax.ppermute(send, 'inner', perm)]  7.54 us
    all_to_all x1, waiting for transfers between devices, to_tubes(): parts = lax.all_to_all(parts, AXES, split_axis=0, concat_axis=0, tiled=True)  7.24 us
    ppermute x4, starting transfers between devices, exchange(): return lax.ppermute(value, AXES, perm)  5.39 us
    all_to_all x1, starting transfers between devices, to_frames(): parts = lax.all_to_all(parts, AXES, split_axis=0, concat_axis=0, tiled=True)  3.48 us
    ppermute x4, waiting for transfers between devices, reduce_weights(): got[p] = [lax.ppermute(send, 'inner', perm)]  2.71 us
  transfers between devices with their start and end apart: 12, of which 7 were waited for; matrix products, arithmetic and copies ran while one was open for 0% of the time, Pallas kernels for 13%

profile of v7, /device:TPU:0, one launch (start us, length us, event | category | flops | bytes accessed | tf_op | source)
XLA Modules:
  0.0 95.1 jit_solution(10676194857470414967)
XLA Ops:
  0.6 20.8 %all_to_all.15 = bf16[32,1,8,768]{3,2,1,0:T(8,128)(2,1)S(1)} all-to-all(bf16[32,1,8,768]{3,2,1,0:T(8,128)(2,1)} %bitcast.15), channel_id=1, replica_groups=mesh['tm'=4,'inner'=8] {'tm','inner'}, dimensions={0} | all-to-all | bytes 786432 | tf_op jit(solution)/shard_map/all_to_all | solution.py:392
  21.4 2.6 %all-to-all-start.1 = ((bf16[32,1,8,768]{3,2,1,0:T(8,128)(2,1)}), bf16[32,1,8,768]{3,2,1,0:T(8,128)(2,1)S(1)}, u32[]{:S(2)}, u32[]{:S(2)}) async-start(bf16[32,1,8,768]{3,2,1,0:T(8,128)(2,1)} %bitcast.19), calls=%async_computation.1 | async-start | bytes 786432 | tf_op jit(solution)/shard_map/all_to_all | solution.py:392
  24.1 0.3 fusion.15.bias_ref
  24.4 5.8 %shard_map.92 = (bf16[2,4,96,256]{3,2,1,0:T(8,128)(2,1)}, bf16[2,4,96,256]{3,2,1,0:T(8,128)(2,1)}, bf16[256,768]{1,0:T(8,128)(2,1)}, bf16[768,256]{1,0:T(8,128)(...) custom-call(bf16[256,768]{1,0:T(8,128)(2,1)S(1)} %bitcast.17, ...), custom_call_target="tpu_custom_call" | custom-call | flops 1207959552 | bytes 8522752 | tf_op jit(solution)/shard_map/pallas_call | solution.py:49
  30.2 7.2 %all-to-all-done.1 = bf16[32,1,8,768]{3,2,1,0:T(8,128)(2,1)S(1)} async-done(((bf16[32,1,8,768]{3,2,1,0:T(8,128)(2,1)}), bf16[32,1,8,768]{3,2,1,0:T(8,128)(2,1)S(1)}, u32[]{:S(2)}, u32[]{:S(2)}) %all-to-all-start.1) | async-done | bytes 393248 | tf_op jit(solution)/shard_map/all_to_all | solution.py:392
  37.4 4.7 %shard_map.93.blocks_ref.d_ref = bf16[4,256,768]{2,1,0:T(8,128)(2,1)S(1)} custom-call(bf16[256,768]{1,0:T(8,128)(2,1)S(1)} %bitcast.12, bf16[768,768]{1,0:T(8,128)(2,1)} %wout_ref.1, bf16[256,768]{1,0:T(8,128)(2,1)} %get-tuple-element.29.rest_1_, bf16[768,256]{1,0:T(8,128)(2,1)} %get-tuple-element.30.rest_2_, bf16[256,768]{1,0:T(8,128)(2,1)} %get-tuple-element.31.rest_3_, ...), custom_call_target="tpu_custom_call" | custom-call | flops 1207959552 | bytes 6291456 | tf_op jit(solution)/shard_map/pallas_call | solution.py:49
  42.1 0.2 collective-permute-start.1
  42.3 1.5 %shard_map.94 = bf16[256,1664]{1,0:T(8,128)(2,1)S(1)} custom-call(bf16[256,768]{1,0:T(8,128)(2,1)S(1)} %bitcast.18, bf16[256,768]{1,0:T(8,128)(2,1)S(1)} %bitcast.13, f32[1,768]{1,0:T(1,128)S(1)} %reshape.37.gain_ref, bf16[4,256,768]{2,1,0:T(8,128)(2,1)S(1)} %shard_map.93.blocks_ref.d_ref, bf16[768,2304]{1,0:T(8,128)(2,1)S(1)} %copy-done.1, ...), custom_call_target="tpu_custom_call" | custom-call | flops 905969664 | bytes 7146496 | tf_op jit(solution)/shard_map/pallas_call | solution.py:49
  43.8 0.9 copy-done.3
  44.8 3.5 %all-to-all-start.2 = ((bf16[32,1,8,1664]{3,2,1,0:T(8,128)(2,1)}), bf16[32,1,8,1664]{3,2,1,0:T(8,128)(2,1)}, u32[]{:S(2)}, u32[]{:S(2)}) async-start(bf16[32,1,8,1664]{3,2,1,0:T(8,128)(2,1)} %bitcast.14), calls=%async_computation.2 | async-start | bytes 1703936 | tf_op jit(solution)/shard_map/all_to_all | solution.py:399
  48.3 0.2 collective-permute-start
  48.5 1.8 %collective-permute-done.other_ref = bf16[2,4,96,256]{3,2,1,0:T(8,128)(2,1)S(1)} collective-permute-done((bf16[2,4,96,256]{3,2,1,0:T(8,128)(2,1)}, bf16[2,4,96,256]{3,2,1,0:T(8,128)(2,1)S(1)}, u32[]{:S(2)}, u32[]{:S(2)}) %collective-permute-start) | collective-permute-done | bytes 393248 | tf_op jit(solution)/shard_map/ppermute | solution.py:278
  50.3 0.6 shard_map.97
  50.9 1.6 %collective-permute-start.2 = (bf16[2,4,48,768]{3,2,1,0:T(8,128)(2,1)S(1)}, bf16[2,4,48,768]{3,2,1,0:T(8,128)(2,1)S(1)}, u32[]{:S(2)}, u32[]{:S(2)}) collective-permute-start(bf16[2,4,48,768]{3,2,1,0:T(8,128)(2,1)S(1)} %shard_map.97), channel_id=1, source_target_pairs={{0,8},{1,17},{2,10},{3,19},{4,12},{5,21},{6,14},{7,23},{8,0},{9,25... | collective-permute-start | bytes 1769480 | tf_op jit(solution)/shard_map/ppermute | solution.py:274
  52.5 0.6 shard_map.101
  53.2 0.5 collective-permute-start.6
  53.7 1.0 %shard_map.96 = (f32[1,4,48,768]{3,2,1,0:T(8,128)S(1)}, f32[1,4,48,768]{3,2,1,0:T(8,128)S(1)}, f32[1,4,48,768]{3,2,1,0:T(8,128)S(1)}, f32[1,4,48,768]{3,2,1,0:T(8,128)S(1)}) custom-call(bf16[2,4,96,256]{3,2,1,0:T(8,128)(2,1)S(1)} %copy-done.2, bf16[2,4,96,256]{3,2,1,0:T(8,128)(2,1)S(1)} %collective-permute-done.other_ref, ...), custom_call_target="tpu_custom_call" | custom-call | flops 603979776 | bytes 6291456 | tf_op jit(solution)/shard_map/pallas_call | solution.py:49
  54.7 9.7 %collective-permute-done.2.rest_0_ = bf16[2,4,48,768]{3,2,1,0:T(8,128)(2,1)S(1)} collective-permute-done((bf16[2,4,48,768]{3,2,1,0:T(8,128)(2,1)S(1)}, bf16[2,4,48,768]{3,2,1,0:T(8,128)(2,1)S(1)}, u32[]{:S(2)}, u32[]{:S(2)}) %collective-permute-start.2) | collective-permute-done | bytes 589856 | tf_op jit(solution)/shard_map/ppermute | solution.py:274
  64.5 1.6 %collective-permute-start.3 = (bf16[1,4,48,768]{3,2,1,0:T(8,128)(2,1)S(1)}, bf16[1,4,48,768]{3,2,1,0:T(8,128)(2,1)S(1)}, u32[]{:S(2)}, u32[]{:S(2)}) collective-permute-start(bf16[1,4,48,768]{3,2,1,0:T(8,128)(2,1)S(1)} %shard_map.98), channel_id=1, source_target_pairs={{0,16},{1,9},{2,18},{3,11},{4,20},{5,13},{6,22},{7,15},{8,24},{9,1... | collective-permute-start | bytes 884744 | tf_op jit(solution)/shard_map/ppermute | solution.py:274
  66.1 9.9 %collective-permute-done.6.rest_0_ = bf16[2,4,48,768]{3,2,1,0:T(8,128)(2,1)S(1)} collective-permute-done((bf16[2,4,48,768]{3,2,1,0:T(8,128)(2,1)S(1)}, bf16[2,4,48,768]{3,2,1,0:T(8,128)(2,1)S(1)}, u32[]{:S(2)}, u32[]{:S(2)}) %collective-permute-start.6) | collective-permute-done | bytes 589856 | tf_op jit(solution)/shard_map/ppermute | solution.py:274
  76.1 1.6 %collective-permute-start.7 = (bf16[1,4,48,768]{3,2,1,0:T(8,128)(2,1)S(1)}, bf16[1,4,48,768]{3,2,1,0:T(8,128)(2,1)S(1)}, u32[]{:S(2)}, u32[]{:S(2)}) collective-permute-start(bf16[1,4,48,768]{3,2,1,0:T(8,128)(2,1)S(1)} %shard_map.102), channel_id=1, source_target_pairs={{0,16},{1,9},{2,18},{3,11},{4,20},{5,13},{6,22},{7,15},{8,24},{9,1... | collective-permute-start | bytes 884744 | tf_op jit(solution)/shard_map/ppermute | solution.py:274
  77.7 0.1 shard_map.99
  77.8 1.5 %collective-permute-start.4 = (bf16[2,48,768]{2,1,0:T(8,128)(2,1)S(1)}, bf16[2,48,768]{2,1,0:T(8,128)(2,1)S(1)}, u32[]{:S(2)}, u32[]{:S(2)}) collective-permute-start(bf16[2,48,768]{2,1,0:T(8,128)(2,1)S(1)} %get-tuple-element.41), channel_id=1, source_target_pairs={{0,2},{1,3},{2,0},{3,1},{4,6},{5,7},{6,4},{7,5},{8,10},{9,11},{10,... | collective-permute-start | bytes 442376 | tf_op jit(solution)/shard_map/ppermute | solution.py:381
  79.3 3.6 %collective-permute-done.7.rest_1_ = bf16[1,4,48,768]{3,2,1,0:T(8,128)(2,1)S(1)} collective-permute-done((bf16[1,4,48,768]{3,2,1,0:T(8,128)(2,1)S(1)}, bf16[1,4,48,768]{3,2,1,0:T(8,128)(2,1)S(1)}, u32[]{:S(2)}, u32[]{:S(2)}) %collective-permute-start.7) | collective-permute-done | bytes 294944 | tf_op jit(solution)/shard_map/ppermute | solution.py:274
  82.9 0.1 shard_map.103
  83.0 1.5 %collective-permute-start.8 = (bf16[2,48,768]{2,1,0:T(8,128)(2,1)S(1)}, bf16[2,48,768]{2,1,0:T(8,128)(2,1)S(1)}, u32[]{:S(2)}, u32[]{:S(2)}) collective-permute-start(bf16[2,48,768]{2,1,0:T(8,128)(2,1)S(1)} %get-tuple-element.47), channel_id=1, source_target_pairs={{0,2},{1,3},{2,0},{3,1},{4,6},{5,7},{6,4},{7,5},{8,10},{9,11},{10,... | collective-permute-start | bytes 442376 | tf_op jit(solution)/shard_map/ppermute | solution.py:381
  84.5 2.2 %collective-permute-start.5 = (bf16[1,48,768]{2,1,0:T(8,128)(2,1)S(1)}, bf16[1,48,768]{2,1,0:T(8,128)(2,1)S(1)}, u32[]{:S(2)}, u32[]{:S(2)}) collective-permute-start(bf16[1,48,768]{2,1,0:T(8,128)(2,1)S(1)} %get-tuple-element.43), channel_id=1, source_target_pairs={{0,4},{1,5},{2,6},{3,7},{4,0},{5,1},{6,2},{7,3},{8,12},{9,13},{10,... | collective-permute-start | bytes 221192 | tf_op jit(solution)/shard_map/ppermute | solution.py:381
  86.7 2.3 %collective-permute-done.8.got_ref = bf16[2,48,768]{2,1,0:T(8,128)(2,1)S(1)} collective-permute-done((bf16[2,48,768]{2,1,0:T(8,128)(2,1)S(1)}, bf16[2,48,768]{2,1,0:T(8,128)(2,1)S(1)}, u32[]{:S(2)}, u32[]{:S(2)}) %collective-permute-start.8) | collective-permute-done | bytes 147488 | tf_op jit(solution)/shard_map/ppermute | solution.py:381
  89.0 2.4 %collective-permute-start.9 = (bf16[1,48,768]{2,1,0:T(8,128)(2,1)S(1)}, bf16[1,48,768]{2,1,0:T(8,128)(2,1)S(1)}, u32[]{:S(2)}, u32[]{:S(2)}) collective-permute-start(bf16[1,48,768]{2,1,0:T(8,128)(2,1)S(1)} %get-tuple-element.49), channel_id=1, source_target_pairs={{0,4},{1,5},{2,6},{3,7},{4,0},{5,1},{6,2},{7,3},{8,12},{9,13},{10,... | collective-permute-start | bytes 221192 | tf_op jit(solution)/shard_map/ppermute | solution.py:381
  91.4 2.5 %shard_map.95 = (bf16[256,768]{1,0:T(8,128)(2,1)}, bf16[256,768]{1,0:T(8,128)(2,1)}, f32[1,96]{1,0:T(1,128)}) custom-call(bf16[256,768]{1,0:T(8,128)(2,1)S(1)} %bitcast.16, bf16[768,768]{1,0:T(8,128)(2,1)S(1)} %copy-done, bf16[256,1664]{1,0:T(8,128)(2,1)} %bitcast.7.back_ref), custom_call_target="tpu_custom_call" | custom-call | flops 301989888 | bytes 3211648 | tf_op jit(solution)/shard_map/pallas_call | solution.py:49
  93.9 0.4 collective-permute-done.9.rest_3_
  94.3 0.8 shard_map.105
  (30 shorter events, 0.2 us)
Async XLA Ops:
  0.6 23.4 %copy-start.8 = (f32[768]{0:T(1024)S(1)}, f32[768]{0:T(1024)}, u32[]{:S(2)}) copy-start(f32[768]{0:T(1024)} %param.6) | copy-start | bytes 9220
  21.4 8.8 %copy-start.5 = (bf16[32,1,8,768]{3,2,1,0:T(8,128)(2,1)}, bf16[32,1,8,768]{3,2,1,0:T(8,128)(2,1)S(1)}, u32[]{:S(2)}) copy-start(bf16[32,1,8,768]{3,2,1,0:T(8,128)(2,1)S(1)} %all_to_all.15) | copy-start | bytes 1179652
  21.4 16.0 %all-to-all-start.1 = ((bf16[32,1,8,768]{3,2,1,0:T(8,128)(2,1)}), bf16[32,1,8,768]{3,2,1,0:T(8,128)(2,1)S(1)}, u32[]{:S(2)}, u32[]{:S(2)}) async-start(bf16[32,1,8,768]{3,2,1,0:T(8,128)(2,1)} %bitcast.19), calls=%async_computation.1 | async-start | bytes 786432 | tf_op jit(solution)/shard_map/all_to_all | solution.py:392
  37.4 4.9 %copy-start.1 = (bf16[768,2304]{1,0:T(8,128)(2,1)S(1)}, bf16[768,2304]{1,0:T(8,128)(2,1)}, u32[]{:S(2)}) copy-start(bf16[768,2304]{1,0:T(8,128)(2,1)} %wqkv_ref.1) | copy-start | bytes 10616836
  37.4 4.9 %copy-start.6 = (bf16[32,1,8,768]{3,2,1,0:T(8,128)(2,1)S(1)}, bf16[32,1,8,768]{3,2,1,0:T(8,128)(2,1)}, u32[]{:S(2)}) copy-start(bf16[32,1,8,768]{3,2,1,0:T(8,128)(2,1)} %copy-done.5) | copy-start | bytes 1179652
  37.4 4.9 %copy-start.7 = (bf16[256,768]{1,0:T(8,128)(2,1)S(1)}, bf16[256,768]{1,0:T(8,128)(2,1)}, u32[]{:S(2)}) copy-start(bf16[256,768]{1,0:T(8,128)(2,1)} %get-tuple-element.33.mixed_ref) | copy-start | bytes 1179652
  42.1 8.1 %collective-permute-start.1 = (bf16[4,256,768]{2,1,0:T(8,128)(2,1)S(1)}, bf16[4,256,768]{2,1,0:T(8,128)(2,1)S(1)}, u32[]{:S(2)}, u32[]{:S(2)}) collective-permute-start(bf16[4,256,768]{2,1,0:T(8,128)(2,1)S(1)} %shard_map.93.blocks_ref.d_ref), channel_id=1, source_target_pairs={{0,1},{1,0},{2,3},{3,2},{4,5},{5,4},{6,7},{7,6},{8,9},{9,8},{10,11... | collective-permute-start | bytes 4718600 | tf_op jit(solution)/shard_map/ppermute | solution.py:278
  43.8 0.9 copy-start.3
  44.8 5.5 %copy-start.2 = (bf16[2,4,96,256]{3,2,1,0:T(8,128)(2,1)S(1)}, bf16[2,4,96,256]{3,2,1,0:T(8,128)(2,1)}, u32[]{:S(2)}) copy-start(bf16[2,4,96,256]{3,2,1,0:T(8,128)(2,1)} %get-tuple-element.36.mine_ref) | copy-start | bytes 1179652
  44.8 46.7 %all-to-all-start.2 = ((bf16[32,1,8,1664]{3,2,1,0:T(8,128)(2,1)}), bf16[32,1,8,1664]{3,2,1,0:T(8,128)(2,1)}, u32[]{:S(2)}, u32[]{:S(2)}) async-start(bf16[32,1,8,1664]{3,2,1,0:T(8,128)(2,1)} %bitcast.14), calls=%async_computation.2 | async-start | bytes 1703936 | tf_op jit(solution)/shard_map/all_to_all | solution.py:399
  48.3 2.0 %collective-permute-start = (bf16[2,4,96,256]{3,2,1,0:T(8,128)(2,1)}, bf16[2,4,96,256]{3,2,1,0:T(8,128)(2,1)S(1)}, u32[]{:S(2)}, u32[]{:S(2)}) collective-permute-start(bf16[2,4,96,256]{3,2,1,0:T(8,128)(2,1)} %get-tuple-element.37), channel_id=1, source_target_pairs={{0,1},{1,0},{2,3},{3,2},{4,5},{5,4},{6,7},{7,6},{8,9},{9,8},{10,11... | collective-permute-start | bytes 1179656 | tf_op jit(solution)/shard_map/ppermute | solution.py:278
  50.9 13.5 %collective-permute-start.2 = (bf16[2,4,48,768]{3,2,1,0:T(8,128)(2,1)S(1)}, bf16[2,4,48,768]{3,2,1,0:T(8,128)(2,1)S(1)}, u32[]{:S(2)}, u32[]{:S(2)}) collective-permute-start(bf16[2,4,48,768]{3,2,1,0:T(8,128)(2,1)S(1)} %shard_map.97), channel_id=1, source_target_pairs={{0,8},{1,17},{2,10},{3,19},{4,12},{5,21},{6,14},{7,23},{8,0},{9,25... | collective-permute-start | bytes 1769480 | tf_op jit(solution)/shard_map/ppermute | solution.py:274
  53.2 22.9 %collective-permute-start.6 = (bf16[2,4,48,768]{3,2,1,0:T(8,128)(2,1)S(1)}, bf16[2,4,48,768]{3,2,1,0:T(8,128)(2,1)S(1)}, u32[]{:S(2)}, u32[]{:S(2)}) collective-permute-start(bf16[2,4,48,768]{3,2,1,0:T(8,128)(2,1)S(1)} %shard_map.101), channel_id=1, source_target_pairs={{0,8},{1,17},{2,10},{3,19},{4,12},{5,21},{6,14},{7,23},{8,0},{9,25... | collective-permute-start | bytes 1769480 | tf_op jit(solution)/shard_map/ppermute | solution.py:274
  64.5 13.2 %collective-permute-start.3 = (bf16[1,4,48,768]{3,2,1,0:T(8,128)(2,1)S(1)}, bf16[1,4,48,768]{3,2,1,0:T(8,128)(2,1)S(1)}, u32[]{:S(2)}, u32[]{:S(2)}) collective-permute-start(bf16[1,4,48,768]{3,2,1,0:T(8,128)(2,1)S(1)} %shard_map.98), channel_id=1, source_target_pairs={{0,16},{1,9},{2,18},{3,11},{4,20},{5,13},{6,22},{7,15},{8,24},{9,1... | collective-permute-start | bytes 884744 | tf_op jit(solution)/shard_map/ppermute | solution.py:274
  76.1 6.8 %collective-permute-start.7 = (bf16[1,4,48,768]{3,2,1,0:T(8,128)(2,1)S(1)}, bf16[1,4,48,768]{3,2,1,0:T(8,128)(2,1)S(1)}, u32[]{:S(2)}, u32[]{:S(2)}) collective-permute-start(bf16[1,4,48,768]{3,2,1,0:T(8,128)(2,1)S(1)} %shard_map.102), channel_id=1, source_target_pairs={{0,16},{1,9},{2,18},{3,11},{4,20},{5,13},{6,22},{7,15},{8,24},{9,1... | collective-permute-start | bytes 884744 | tf_op jit(solution)/shard_map/ppermute | solution.py:274
  77.7 13.7 %copy-start = (bf16[768,768]{1,0:T(8,128)(2,1)S(1)}, bf16[768,768]{1,0:T(8,128)(2,1)}, u32[]{:S(2)}) copy-start(bf16[768,768]{1,0:T(8,128)(2,1)} %wout_ref.1) | copy-start | bytes 3538948
  77.7 13.7 %copy-start.4 = (bf16[1,256,768]{2,1,0:T(8,128)(2,1)S(1)}, bf16[1,256,768]{2,1,0:T(8,128)(2,1)}, u32[]{:S(2)}) copy-start(bf16[1,256,768]{2,1,0:T(8,128)(2,1)} %param.5) | copy-start | bytes 1179652
  77.8 6.7 %collective-permute-start.4 = (bf16[2,48,768]{2,1,0:T(8,128)(2,1)S(1)}, bf16[2,48,768]{2,1,0:T(8,128)(2,1)S(1)}, u32[]{:S(2)}, u32[]{:S(2)}) collective-permute-start(bf16[2,48,768]{2,1,0:T(8,128)(2,1)S(1)} %get-tuple-element.41), channel_id=1, source_target_pairs={{0,2},{1,3},{2,0},{3,1},{4,6},{5,7},{6,4},{7,5},{8,10},{9,11},{10,... | collective-permute-start | bytes 442376 | tf_op jit(solution)/shard_map/ppermute | solution.py:381
  83.0 6.0 %collective-permute-start.8 = (bf16[2,48,768]{2,1,0:T(8,128)(2,1)S(1)}, bf16[2,48,768]{2,1,0:T(8,128)(2,1)S(1)}, u32[]{:S(2)}, u32[]{:S(2)}) collective-permute-start(bf16[2,48,768]{2,1,0:T(8,128)(2,1)S(1)} %get-tuple-element.47), channel_id=1, source_target_pairs={{0,2},{1,3},{2,0},{3,1},{4,6},{5,7},{6,4},{7,5},{8,10},{9,11},{10,... | collective-permute-start | bytes 442376 | tf_op jit(solution)/shard_map/ppermute | solution.py:381
  84.5 9.4 %collective-permute-start.5 = (bf16[1,48,768]{2,1,0:T(8,128)(2,1)S(1)}, bf16[1,48,768]{2,1,0:T(8,128)(2,1)S(1)}, u32[]{:S(2)}, u32[]{:S(2)}) collective-permute-start(bf16[1,48,768]{2,1,0:T(8,128)(2,1)S(1)} %get-tuple-element.43), channel_id=1, source_target_pairs={{0,4},{1,5},{2,6},{3,7},{4,0},{5,1},{6,2},{7,3},{8,12},{9,13},{10,... | collective-permute-start | bytes 221192 | tf_op jit(solution)/shard_map/ppermute | solution.py:381
  89.0 5.3 %collective-permute-start.9 = (bf16[1,48,768]{2,1,0:T(8,128)(2,1)S(1)}, bf16[1,48,768]{2,1,0:T(8,128)(2,1)S(1)}, u32[]{:S(2)}, u32[]{:S(2)}) collective-permute-start(bf16[1,48,768]{2,1,0:T(8,128)(2,1)S(1)} %get-tuple-element.49), channel_id=1, source_target_pairs={{0,4},{1,5},{2,6},{3,7},{4,0},{5,1},{6,2},{7,3},{8,12},{9,13},{10,... | collective-permute-start | bytes 221192 | tf_op jit(solution)/shard_map/ppermute | solution.py:381

commit v8 on v7

--- a/solution.py
+++ b/solution.py
@@ -21,6 +21,8 @@
 AXES = ("tm", "inner")
 LANES = 128
 VMEM_SPARE = 8 * 1024 * 1024
+DIRECT_FROM = 1
+PARTS = 2
 
 
 def mm(a, b):
@@ -31,7 +33,7 @@
     return lax.dot_general(a, b, (((1,), (1,)), ((), ())), preferred_element_type=F32)
 
 
-def call(kernel, out_shape, *args, scratch=(), flops=0, raw_in=(), raw_out=(), copies=0, near_in=(), near_out=()):
+def call(kernel, out_shape, *args, scratch=(), flops=0, raw_in=(), raw_out=(), copies=0, near_in=(), near_out=(), far_out=False):
     outs = jax.tree.leaves(out_shape)
 
     def size(arrays):
@@ -44,7 +46,7 @@
     out_specs = [spec(i in raw_out) for i in range(len(outs))]
     taken = size(a for i, a in enumerate(args) if i not in raw_in) + size(a for i, a in enumerate(outs) if i not in raw_out)
     semaphores = [pltpu.SemaphoreType.DMA((copies,))] if copies else []
-    placed = [pltpu.HBM(a.shape, a.dtype) if i in raw_out else pltpu.VMEM(a.shape, a.dtype) if i in near_out else a for i, a in enumerate(outs)]
+    placed = [pltpu.HBM(a.shape, a.dtype) if i in raw_out or far_out else pltpu.VMEM(a.shape, a.dtype) if i in near_out else a for i, a in enumerate(outs)]
     args = [pltpu.with_memory_space_constraint(a, pltpu.HBM) if i in raw_in else pltpu.with_memory_space_constraint(a, pltpu.VMEM) if i in near_in else a for i, a in enumerate(args)]
     return pl.pallas_call(
         kernel,
@@ -240,38 +242,32 @@
     return value
 
 
-def bit_orders(runs):
+def bit_order(runs, part):
     bits = list(range(runs.bit_length() - 1))
-    return bits, bits[1:] + bits[:1]
-
-
-def by_core(values):
-    return jnp.where(lax.axis_index("inner") & 1 == 0, *values)
-
-
-def run_of(runs, stage, n, send):
+    shift = part % len(bits)
+    return bits[shift:] + bits[:shift]
+
+
+def run_of(runs, part, stage, n):
     me = lax.axis_index("tm")
+    order = bit_order(runs, part)
+    past, bit = order[:stage], order[stage]
+    run = spread_bits(n, past + [bit])
+    for b in past:
+        run = run | (me & (1 << b))
+    return run | ((me ^ (1 << bit)) & (1 << bit))
+
+
+def place_of(runs, part, stage, run):
+    return squeeze_bits(run, bit_order(runs, part)[: stage + 1])
+
+
+def exchange(values, runs, stage):
     found = []
-    for order in bit_orders(runs):
-        past, bit = order[:stage], order[stage]
-        run = spread_bits(n, past + [bit])
-        for b in past:
-            run = run | (me & (1 << b))
-        found.append(run | ((me ^ (1 << bit) if send else me) & (1 << bit)))
-    return by_core(found)
-
-
-def place_of(runs, stage, run):
-    return by_core([squeeze_bits(run, order[: stage + 1]) for order in bit_orders(runs)])
-
-
-def exchange(value, runs, inner, stage):
-    perm = []
-    for t in range(runs):
-        for i in range(inner):
-            t2 = t ^ (1 << bit_orders(runs)[i & 1][stage])
-            perm.append((t * inner + i, t2 * inner + i))
-    return lax.ppermute(value, AXES, perm)
+    for part, value in enumerate(values):
+        bit = bit_order(runs, part)[stage]
+        found.append(lax.ppermute(value, "tm", [(t, t ^ (1 << bit)) for t in range(runs)]))
+    return found
 
 
 def to_partner(value, inner):
@@ -283,45 +279,59 @@
     return ((0, cut), (cut, rows))
 
 
-def product_kernel(pieces, choose, mine_ref, other_ref, d_ref, d_other_ref, *out_refs):
+def product_kernel(choose, mine_ref, other_ref, d_ref, d_other_ref, *out_refs):
     _, count, _, tokens = mine_ref.shape
-    for index, (low, high) in enumerate(pieces):
-        refs = out_refs[index * len(out_refs) // len(pieces) : (index + 1) * len(out_refs) // len(pieces)]
-        wide = d_ref.shape[2] * 3 // 4
-        for out_ref, runs in zip(refs, choose()):
-            for n, run in enumerate(runs):
-                totals = []
-                for slot, cols in ((0, slice(0, wide)), (1, slice(wide, None))):
+    wide = d_ref.shape[2] * 3 // 4
+    for out_ref, ((low, high), (first, last), runs) in zip(out_refs, choose()):
+        cuts = ((0, first, min(last, wide)), (1, max(first, wide), last))
+        for n, run in enumerate(runs):
+            totals = []
+            for slot, start, stop in cuts:
+                if start < stop:
                     left = mine_ref[slot, :, low:high].reshape(count * (high - low), tokens)
                     right = other_ref[slot, :, low:high].reshape(count * (high - low), tokens)
-                    totals.append(mm(left, d_ref[run, :, cols]) + mm(right, d_other_ref[run, :, cols]))
-                total = jnp.concatenate(totals, 1).astype(out_ref.dtype)
-                for z in range(count):
-                    out_ref[n, z] = total[z * (high - low) : (z + 1) * (high - low)]
-
-
-def partial_sum(runs, run, own_ref, n, got_refs, z):
-    total = own_ref[n, z]
+                    totals.append(mm(left, d_ref[run, :, start:stop]) + mm(right, d_other_ref[run, :, start:stop]))
+            total = jnp.concatenate(totals, 1) if len(totals) > 1 else totals[0]
+            total = total.astype(out_ref.dtype)
+            for z in range(count):
+                out_ref[n, z] = total[z * (high - low) : (z + 1) * (high - low)]
+
+
+def with_received(runs, part, run, total, got_refs, z):
     for stage, ref in enumerate(got_refs):
-        total = total + ref[place_of(runs, stage, run), z].astype(F32)
+        total = total + ref[place_of(runs, part, stage, run), z].astype(F32)
     return total
 
 
-def stage_kernel(runs, stage, own_ref, *rest):
-    got_refs, out_ref = rest[:-1], rest[-1]
-    for n in range(out_ref.shape[0]):
-        run = run_of(runs, stage, n, True)
-        for z in range(out_ref.shape[1]):
-            out_ref[n, z] = partial_sum(runs, run, own_ref, n, got_refs, z).astype(BF)
-
-
-def first_row_kernel(runs, own_ref, *rest):
-    got_refs, (send_ref, rest_ref) = rest[:-2], rest[-2:]
-    me, run = lax.axis_index("inner") >> 1, lax.axis_index("tm")
+def stage_kernel(runs, stage, final, *refs):
+    own_refs, refs = refs[:PARTS], refs[PARTS:]
+    if final:
+        mine_ref, rest_ref, refs = refs[0], refs[-1], refs[1:-1]
+    got_refs, out_refs = refs[:-PARTS], refs[-PARTS:]
+    run = lax.axis_index("tm")
+    for part, (own_ref, out_ref) in enumerate(zip(own_refs, out_refs)):
+        for n in range(out_ref.shape[0]):
+            other = run_of(runs, part, stage, n)
+            for z in range(out_ref.shape[1]):
+                out_ref[n, z] = with_received(runs, part, other, own_ref[n, z], got_refs[part::PARTS], z).astype(BF)
+        if final:
+            lanes = out_ref.shape[3]
+            cols = slice(part * lanes, (part + 1) * lanes)
+            for z in range(out_ref.shape[1]):
+                rest_ref[0, z, :, cols] = with_received(runs, part, run, mine_ref[0, z, :, cols], got_refs[part::PARTS], z)
+
+
+def first_row_kernel(mine_ref, *refs):
+    got_refs, (send_ref, rest_ref) = refs[:-2], refs[-2:]
+    me = lax.axis_index("inner") >> 1
+
+    def total(z):
+        return mine_ref[0, z] + jnp.concatenate([ref[0, z].astype(F32) for ref in got_refs], 1)
+
     for n in range(send_ref.shape[0]):
         z = spread_bits(n, [0])
-        rest_ref[n] = partial_sum(runs, run, own_ref, 0, got_refs, z | (me & 1))
-        send_ref[n] = partial_sum(runs, run, own_ref, 0, got_refs, z | (1 - (me & 1))).astype(BF)
+        rest_ref[n] = total(z | (me & 1))
+        send_ref[n] = total(z | (1 - (me & 1))).astype(BF)
 
 
 def row_kernel(stage, keep_ref, got_ref, send_ref, rest_ref):
@@ -332,11 +342,28 @@
         send_ref[n] = (keep_ref[other] + got_ref[other].astype(F32)).astype(BF)
 
 
-def last_kernel(inv_root, *rest):
+def owners_kernel(mine_ref, *refs):
+    got_refs, (own_ref, *send_refs) = refs[:PARTS], refs[PARTS:]
+    count = mine_ref.shape[1]
+    me = lax.axis_index("inner") >> 1
+
+    def total(z):
+        return mine_ref[0, z] + jnp.concatenate([ref[0, z].astype(F32) for ref in got_refs], 1)
+
+    for k, ref in enumerate(send_refs):
+        ref[0] = total(lax.rem(me + k + 1, count)).astype(BF)
+    own_ref[0] = total(me)
+
+
+def last_kernel(inv_root, sizes, *rest):
     parts, (q_ref, o_ref) = rest[:-2], rest[-2:]
     wide = q_ref.shape[1]
-    for p, (low, high) in enumerate(pieces_of(q_ref.shape[0])):
-        total = (parts[2 * p][0] + parts[2 * p + 1][0].astype(F32)) * inv_root
+    for size, (low, high) in zip(sizes, pieces_of(q_ref.shape[0])):
+        (own_ref, *others), parts = parts[:size], parts[size:]
+        total = own_ref[0]
+        for ref in others:
+            total = total + ref[0].astype(F32)
+        total = total * inv_root
         q_ref[low:high] = total[:, :wide]
         o_ref[low:high] = total[:, wide:]
 
@@ -349,41 +376,66 @@
     pieces = pieces_of(rows)
     args = (mine, other, d, d_other)
 
-    def wanted(stage):
-        if stage == stages:
-            return [lax.axis_index("tm")]
-        return [run_of(runs, stage, n, True) for n in range(runs >> (stage + 1))]
-
-    def product(chosen, which, dtype):
-        shapes = [(max(runs >> (stage + 1), 1), count, high - low, lanes) for low, high in chosen for stage in which]
+    each = lanes // PARTS
+
+    def block(piece, part, stage):
+        if part is None:
+            return piece, (0, lanes), [lax.axis_index("tm")]
+        return piece, (part * each, (part + 1) * each), [run_of(runs, part, stage, n) for n in range(runs >> (stage + 1))]
+
+    def shape_of(piece, part, stage):
+        (low, high), wide = piece, lanes if part is None else each
+        return (1 if part is None else runs >> (stage + 1), count, high - low, wide)
+
+    def product(wanted, dtype):
+        shapes = [shape_of(*each) for each in wanted]
         flops = sum(4 * math.prod(shape) * tokens for shape in shapes)
-        body = functools.partial(product_kernel, chosen, lambda: [wanted(stage) for stage in which])
-        return call(body, tuple(sds(shape, dtype) for shape in shapes), *args, flops=flops, near_in=range(4), near_out=range(len(shapes)))
+        body = functools.partial(product_kernel, lambda: [block(*each) for each in wanted])
+        near = range(len(shapes)) if dtype == BF else ()
+        return call(body, tuple(sds(shape, dtype) for shape in shapes), *args, flops=flops, near_in=range(4), near_out=near, far_out=dtype == F32)
 
     got = [[] for _ in pieces]
     for p, piece in enumerate(pieces):
-        send = product((piece,), (0,), BF)[0]
-        got[p].append(exchange(send, runs, inner, 0))
-    later = product(pieces, tuple(range(1, stages + 1)), F32)
-    own = [later[p * stages : (p + 1) * stages] for p in range(len(pieces))]
+        sends = product([(piece, part, 0) for part in range(PARTS)], BF)
+        got[p].append(exchange(sends, runs, 0))
+    wanted = [(piece, part, stage) for piece in pieces for stage in range(1, stages) for part in range(PARTS)]
+    wanted += [(piece, None, stages) for piece in pieces]
+    later = list(product(wanted, F32))
+    own = [[[later.pop(0) for _ in range(PARTS)] for _ in range(1, stages)] for _ in pieces]
+    keep = later
     for stage in range(1, stages):
+        final = stage == stages - 1
         for p in range(len(pieces)):
-            body = functools.partial(stage_kernel, runs, stage)
-            send = call(body, sds(own[p][stage - 1].shape, BF), own[p][stage - 1], *got[p])
-            got[p].append(exchange(send, runs, inner, stage))
-    keep = [each[-1] for each in own]
+            now = own[p][stage - 1]
+            out = [sds(array.shape, BF) for array in now] + ([sds(keep[p].shape, F32)] if final else [])
+            held = [keep[p]] if final else []
+            received = [array for arrays in got[p] for array in arrays]
+            sends = call(functools.partial(stage_kernel, runs, stage, final), tuple(out), *now, *held, *received)
+            if final:
+                keep[p], got[p] = sends[-1], []
+            got[p].append(exchange(sends[:PARTS], runs, stage))
+    got = [arrays[-1] for arrays in got]
     for stage in range(count.bit_length() - 1):
         perm = [(i, i ^ (2 << stage)) for i in range(inner)]
         for p, (low, high) in enumerate(pieces):
             shape = (count >> (stage + 1), high - low, lanes)
-            body = functools.partial(row_kernel, stage) if stage else functools.partial(first_row_kernel, runs)
+            if p >= DIRECT_FROM and count <= 4:
+                if stage == 0:
+                    owned = (1, high - low, lanes)
+                    out = (sds(owned, F32),) + (sds(owned, BF),) * (count - 1)
+                    keep[p], *sends = call(owners_kernel, out, keep[p], *got[p])
+                    got[p] = []
+                    for k, send in enumerate(sends):
+                        got[p].append(lax.ppermute(send, "inner", [(i, (i + 2 * (k + 1)) % inner) for i in range(inner)]))
+                continue
+            body = functools.partial(row_kernel, stage) if stage else first_row_kernel
             send, keep[p] = call(body, (sds(shape, BF), sds(shape, F32)), keep[p], *got[p])
             got[p] = [lax.ppermute(send, "inner", perm)]
     last = []
     for p in range(len(pieces)):
         last += [keep[p], *got[p]]
     out = (sds((rows, lanes * 3 // 4), F32), sds((rows, lanes // 4), F32))
-    return call(functools.partial(last_kernel, inv_root), out, *last)
+    return call(functools.partial(last_kernel, inv_root, tuple(1 + len(arrays) for arrays in got)), out, *last)
 
 
 def to_tubes(rows, count):

time: 95.5 us -> 94.2 us (0.986)
  waiting for transfers between devices: 35 us -> 27 us
  local copies, waits for them, and re-layouts: 0.96 us -> 3.94 us
  starting transfers between devices: 19.4 us -> 21.9 us
  Pallas kernels: 17.9 us -> 18.9 us
    ppermute x4 -> x11, starting transfers between devices: 5.39 us -> 14 us  [the longest x8 8.28 us: exchange(): lax.ppermute(value, 'tm', [(t, t ^ 1 << bit) for t in range(runs)])]
    ppermute x4 -> x11, waiting for transfers between devices: 23.2 us -> 15 us  [the longest x8 13.6 us: exchange(): lax.ppermute(value, 'tm', [(t, t ^ 1 << bit) for t in range(runs)])]
    ppermute x4 -> x2, starting transfers between devices: 7.54 us -> 1.41 us  [reduce_weights(): got[p] = [lax.ppermute(send, 'inner', perm)]]
    unnamed x18 -> x30, local copies, waits for them, and re-layouts: 0.95 us -> 3.93 us
    pallas_call x14 -> x13, Pallas kernels: 17.9 us -> 18.9 us  [call(): pl.pallas_call(kernel, out_shape=placed if isinstance(out_shape, (tuple,...]
    ppermute x4 -> x2, waiting for transfers between devices: 2.71 us -> 3.04 us  [reduce_weights(): got[p] = [lax.ppermute(send, 'inner', perm)]]
  transfers between devices with their start and end apart: 12 -> 17, of which waited for: 7 -> 11; matrix products, arithmetic and copies ran while one was open for 0% -> 0% of each run, Pallas kernels for 13% -> 14%
where the time goes in v8:
time: 94.2 us; the launch traced here: 93.7 us
  waiting for transfers between devices  27 us (29%)
  starting transfers between devices  21.9 us (23%)
  blocking collectives  20.8 us (22%)
  Pallas kernels  18.9 us (20%)
  local copies, waits for them, and re-layouts  3.94 us (4%)
    all_to_all x1, blocking collectives, to_tubes(): parts = lax.all_to_all(parts, AXES, split_axis=0, concat_axis=0, tiled=True)  20.8 us
    pallas_call x13, Pallas kernels, call(): pl.pallas_call(kernel, out_shape=placed if isinstance(out_shape, (tuple,...  18.9 us
    ppermute x8, waiting for transfers between devices, exchange(): lax.ppermute(value, 'tm', [(t, t ^ 1 << bit) for t in range(runs)])  13.6 us
    ppermute x8, starting transfers between devices, exchange(): lax.ppermute(value, 'tm', [(t, t ^ 1 << bit) for t in range(runs)])  8.28 us
    all_to_all x1, waiting for transfers between devices, to_tubes(): parts = lax.all_to_all(parts, AXES, split_axis=0, concat_axis=0, tiled=True)  7.23 us
    ppermute x3, starting transfers between devices, reduce_weights(): lax.ppermute(send, 'inner', [(i, (i + 2 * (k + 1)) % inner) for i in rang...  5.71 us
    unnamed x30, local copies, waits for them, and re-layouts  3.93 us
    all_to_all x1, starting transfers between devices, to_frames(): parts = lax.all_to_all(parts, AXES, split_axis=0, concat_axis=0, tiled=True)  3.48 us
  transfers between devices with their start and end apart: 17, of which 11 were waited for; matrix products, arithmetic and copies ran while one was open for 0% of the time, Pallas kernels for 14%

profile of v8, /device:TPU:0, one launch (start us, length us, event | category | flops | bytes accessed | tf_op | source)
XLA Modules:
  0.0 93.7 jit_solution(15208997894635350422)
XLA Ops:
  0.6 20.8 %all_to_all.15 = bf16[32,1,8,768]{3,2,1,0:T(8,128)(2,1)S(1)} all-to-all(bf16[32,1,8,768]{3,2,1,0:T(8,128)(2,1)} %bitcast.15), channel_id=1, replica_groups=mesh['tm'=4,'inner'=8] {'tm','inner'}, dimensions={0} | all-to-all | bytes 786432 | tf_op jit(solution)/shard_map/all_to_all | solution.py:444
  21.4 2.6 %all-to-all-start.1 = ((bf16[32,1,8,768]{3,2,1,0:T(8,128)(2,1)}), bf16[32,1,8,768]{3,2,1,0:T(8,128)(2,1)S(1)}, u32[]{:S(2)}, u32[]{:S(2)}) async-start(bf16[32,1,8,768]{3,2,1,0:T(8,128)(2,1)} %bitcast.19), calls=%async_computation.1 | async-start | bytes 786432 | tf_op jit(solution)/shard_map/all_to_all | solution.py:444
  24.4 5.8 %shard_map.92 = (bf16[2,4,96,256]{3,2,1,0:T(8,128)(2,1)}, bf16[2,4,96,256]{3,2,1,0:T(8,128)(2,1)}, bf16[256,768]{1,0:T(8,128)(2,1)}, bf16[768,256]{1,0:T(8,128)(...) custom-call(bf16[256,768]{1,0:T(8,128)(2,1)S(1)} %bitcast.17, ...), custom_call_target="tpu_custom_call" | custom-call | flops 1207959552 | bytes 8522752 | tf_op jit(solution)/shard_map/pallas_call | solution.py:51
  30.2 7.2 %all-to-all-done.1 = bf16[32,1,8,768]{3,2,1,0:T(8,128)(2,1)S(1)} async-done(((bf16[32,1,8,768]{3,2,1,0:T(8,128)(2,1)}), bf16[32,1,8,768]{3,2,1,0:T(8,128)(2,1)S(1)}, u32[]{:S(2)}, u32[]{:S(2)}) %all-to-all-start.1) | async-done | bytes 393248 | tf_op jit(solution)/shard_map/all_to_all | solution.py:444
  37.4 4.7 %shard_map.93.blocks_ref.d_ref = bf16[4,256,768]{2,1,0:T(8,128)(2,1)S(1)} custom-call(bf16[256,768]{1,0:T(8,128)(2,1)S(1)} %bitcast.12, bf16[768,768]{1,0:T(8,128)(2,1)} %wout_ref.1, bf16[256,768]{1,0:T(8,128)(2,1)} %get-tuple-element.41.rest_1_, bf16[768,256]{1,0:T(8,128)(2,1)} %get-tuple-element.42.rest_2_, bf16[256,768]{1,0:T(8,128)(2,1)} %get-tuple-element.43.rest_3_, ...), custom_call_target="tpu_custom_call" | custom-call | flops 1207959552 | bytes 6291456 | tf_op jit(solution)/shard_map/pallas_call | solution.py:51
  42.3 1.5 %shard_map.94 = bf16[256,1664]{1,0:T(8,128)(2,1)S(1)} custom-call(bf16[256,768]{1,0:T(8,128)(2,1)S(1)} %bitcast.18, bf16[256,768]{1,0:T(8,128)(2,1)S(1)} %bitcast.13, f32[1,768]{1,0:T(1,128)S(1)} %reshape.37.gain_ref, bf16[4,256,768]{2,1,0:T(8,128)(2,1)S(1)} %shard_map.93.blocks_ref.d_ref, bf16[768,2304]{1,0:T(8,128)(2,1)S(1)} %copy-done.1, ...), custom_call_target="tpu_custom_call" | custom-call | flops 905969664 | bytes 7146496 | tf_op jit(solution)/shard_map/pallas_call | solution.py:51
  43.8 0.9 copy-done.3
  44.7 3.5 %all-to-all-start.2 = ((bf16[32,1,8,1664]{3,2,1,0:T(8,128)(2,1)}), bf16[32,1,8,1664]{3,2,1,0:T(8,128)(2,1)}, u32[]{:S(2)}, u32[]{:S(2)}) async-start(bf16[32,1,8,1664]{3,2,1,0:T(8,128)(2,1)} %bitcast.14), calls=%async_computation.2 | async-start | bytes 1703936 | tf_op jit(solution)/shard_map/all_to_all | solution.py:451
  48.4 1.8 %collective-permute-done.other_ref = bf16[2,4,96,256]{3,2,1,0:T(8,128)(2,1)S(1)} collective-permute-done((bf16[2,4,96,256]{3,2,1,0:T(8,128)(2,1)}, bf16[2,4,96,256]{3,2,1,0:T(8,128)(2,1)S(1)}, u32[]{:S(2)}, u32[]{:S(2)}) %collective-permute-start) | collective-permute-done | bytes 393248 | tf_op jit(solution)/shard_map/ppermute | solution.py:274
  50.9 1.6 %collective-permute-start.2 = (bf16[2,4,48,384]{3,2,1,0:T(8,128)(2,1)S(1)}, bf16[2,4,48,384]{3,2,1,0:T(8,128)(2,1)S(1)}, u32[]{:S(2)}, u32[]{:S(2)}) collective-permute-start(bf16[2,4,48,384]{3,2,1,0:T(8,128)(2,1)S(1)} %get-tuple-element.53), channel_id=1, source_target_pairs={{0,8},{8,0},{16,24},{24,16},{1,9},{9,1},{17,25},{25,17},{2,10},{10... | collective-permute-start | bytes 884744 | tf_op jit(solution)/shard_map/ppermute | solution.py:269
  52.5 1.5 %collective-permute-start.3 = (bf16[2,4,48,384]{3,2,1,0:T(8,128)(2,1)S(1)}, bf16[2,4,48,384]{3,2,1,0:T(8,128)(2,1)S(1)}, u32[]{:S(2)}, u32[]{:S(2)}) collective-permute-start(bf16[2,4,48,384]{3,2,1,0:T(8,128)(2,1)S(1)} %get-tuple-element.54), channel_id=1, source_target_pairs={{0,16},{8,24},{16,0},{24,8},{1,17},{9,25},{17,1},{25,9},{2,18},{10... | collective-permute-start | bytes 884744 | tf_op jit(solution)/shard_map/ppermute | solution.py:269
  55.7 2.1 %shard_map.96 = (f32[1,4,48,384]{3,2,1,0:T(8,128)}, f32[1,4,48,384]{3,2,1,0:T(8,128)}, f32[1,4,48,384]{3,2,1,0:T(8,128)}, f32[1,4,48,384]{3,2,1,0:T(8,128)}, f32...) custom-call(bf16[2,4,96,256]{3,2,1,0:T(8,128)(2,1)S(1)} %copy-done.2, ...), custom_call_target="tpu_custom_call" | custom-call | flops 603979776 | bytes 6291456 | tf_op jit(solution)/shard_map/pallas_call | solution.py:51
  57.7 6.6 %collective-permute-done.2.refs_3_ = bf16[2,4,48,384]{3,2,1,0:T(8,128)(2,1)S(1)} collective-permute-done((bf16[2,4,48,384]{3,2,1,0:T(8,128)(2,1)S(1)}, bf16[2,4,48,384]{3,2,1,0:T(8,128)(2,1)S(1)}, u32[]{:S(2)}, u32[]{:S(2)}) %collective-permute-start.2) | collective-permute-done | bytes 294944 | tf_op jit(solution)/shard_map/ppermute | solution.py:269
  64.4 1.9 %collective-permute-done.3.refs_4_ = bf16[2,4,48,384]{3,2,1,0:T(8,128)(2,1)S(1)} collective-permute-done((bf16[2,4,48,384]{3,2,1,0:T(8,128)(2,1)S(1)}, bf16[2,4,48,384]{3,2,1,0:T(8,128)(2,1)S(1)}, u32[]{:S(2)}, u32[]{:S(2)}) %collective-permute-start.3) | collective-permute-done | bytes 294944 | tf_op jit(solution)/shard_map/ppermute | solution.py:269
  66.3 1.1 %copy-done.8 = f32[1,4,48,768]{3,2,1,0:T(8,128)S(1)} copy-done((f32[1,4,48,768]{3,2,1,0:T(8,128)S(1)}, f32[1,4,48,768]{3,2,1,0:T(8,128)}, u32[]{:S(2)}) %copy-start.8) | copy-done | bytes 589848
  67.4 1.0 %copy-done.12 = f32[1,4,48,384]{3,2,1,0:T(8,128)S(1)} copy-done((f32[1,4,48,384]{3,2,1,0:T(8,128)S(1)}, f32[1,4,48,384]{3,2,1,0:T(8,128)}, u32[]{:S(2)}) %copy-start.12) | copy-done | bytes 294936
  68.3 1.0 %copy-done.13 = f32[1,4,48,384]{3,2,1,0:T(8,128)S(1)} copy-done((f32[1,4,48,384]{3,2,1,0:T(8,128)S(1)}, f32[1,4,48,384]{3,2,1,0:T(8,128)}, u32[]{:S(2)}) %copy-start.13) | copy-done | bytes 294936
  69.4 0.9 collective-permute-start.4
  70.2 1.4 %collective-permute-start.5 = (bf16[1,4,48,384]{3,2,1,0:T(8,128)(2,1)S(1)}, bf16[1,4,48,384]{3,2,1,0:T(8,128)(2,1)S(1)}, u32[]{:S(2)}, u32[]{:S(2)}) collective-permute-start(bf16[1,4,48,384]{3,2,1,0:T(8,128)(2,1)S(1)} %get-tuple-element.57), channel_id=1, source_target_pairs={{0,8},{8,0},{16,24},{24,16},{1,9},{9,1},{17,25},{25,17},{2,10},{10... | collective-permute-start | bytes 442376 | tf_op jit(solution)/shard_map/ppermute | solution.py:269
  71.6 1.2 %collective-permute-done.8.refs_3_ = bf16[2,4,48,384]{3,2,1,0:T(8,128)(2,1)S(1)} collective-permute-done((bf16[2,4,48,384]{3,2,1,0:T(8,128)(2,1)S(1)}, bf16[2,4,48,384]{3,2,1,0:T(8,128)(2,1)S(1)}, u32[]{:S(2)}, u32[]{:S(2)}) %collective-permute-start.8) | collective-permute-done | bytes 294944 | tf_op jit(solution)/shard_map/ppermute | solution.py:269
  72.8 0.9 collective-permute-done.9.refs_4_
  73.9 0.9 collective-permute-start.10
  74.8 1.0 %collective-permute-start.11 = (bf16[1,4,48,384]{3,2,1,0:T(8,128)(2,1)S(1)}, bf16[1,4,48,384]{3,2,1,0:T(8,128)(2,1)S(1)}, u32[]{:S(2)}, u32[]{:S(2)}) collective-permute-start(bf16[1,4,48,384]{3,2,1,0:T(8,128)(2,1)S(1)} %get-tuple-element.69), channel_id=1, source_target_pairs={{0,8},{8,0},{16,24},{24,16},{1,9},{9,1},{17,25},{25,17},{2,10},{10... | collective-permute-start | bytes 442376 | tf_op jit(solution)/shard_map/ppermute | solution.py:269
  75.8 1.2 %collective-permute-done.4.refs_0_ = bf16[1,4,48,384]{3,2,1,0:T(8,128)(2,1)S(1)} collective-permute-done((bf16[1,4,48,384]{3,2,1,0:T(8,128)(2,1)S(1)}, bf16[1,4,48,384]{3,2,1,0:T(8,128)(2,1)S(1)}, u32[]{:S(2)}, u32[]{:S(2)}) %collective-permute-start.4) | collective-permute-done | bytes 147488 | tf_op jit(solution)/shard_map/ppermute | solution.py:269
  77.0 1.2 %collective-permute-start.6 = (bf16[2,48,768]{2,1,0:T(8,128)(2,1)S(1)}, bf16[2,48,768]{2,1,0:T(8,128)(2,1)S(1)}, u32[]{:S(2)}, u32[]{:S(2)}) collective-permute-start(bf16[2,48,768]{2,1,0:T(8,128)(2,1)S(1)} %get-tuple-element.59), channel_id=1, source_target_pairs={{0,2},{1,3},{2,0},{3,1},{4,6},{5,7},{6,4},{7,5},{8,10},{9,11},{10,... | collective-permute-start | bytes 442376 | tf_op jit(solution)/shard_map/ppermute | solution.py:433
  78.1 1.2 %collective-permute-done.10.refs_0_ = bf16[1,4,48,384]{3,2,1,0:T(8,128)(2,1)S(1)} collective-permute-done((bf16[1,4,48,384]{3,2,1,0:T(8,128)(2,1)S(1)}, bf16[1,4,48,384]{3,2,1,0:T(8,128)(2,1)S(1)}, u32[]{:S(2)}, u32[]{:S(2)}) %collective-permute-start.10) | collective-permute-done | bytes 147488 | tf_op jit(solution)/shard_map/ppermute | solution.py:269
  80.0 1.5 %collective-permute-start.12 = (bf16[1,48,768]{2,1,0:T(8,128)(2,1)S(1)}, bf16[1,48,768]{2,1,0:T(8,128)(2,1)S(1)}, u32[]{:S(2)}, u32[]{:S(2)}) collective-permute-start(bf16[1,48,768]{2,1,0:T(8,128)(2,1)S(1)} %get-tuple-element.71), channel_id=1, source_target_pairs={{0,2},{1,3},{2,4},{3,5},{4,6},{5,7},{6,0},{7,1},{8,10},{9,11},{10,... | collective-permute-start | bytes 221192 | tf_op jit(solution)/shard_map/ppermute | solution.py:429
  81.5 2.2 %collective-permute-start.13 = (bf16[1,48,768]{2,1,0:T(8,128)(2,1)S(1)}, bf16[1,48,768]{2,1,0:T(8,128)(2,1)S(1)}, u32[]{:S(2)}, u32[]{:S(2)}) collective-permute-start(bf16[1,48,768]{2,1,0:T(8,128)(2,1)S(1)} %get-tuple-element.72), channel_id=1, source_target_pairs={{0,4},{1,5},{2,6},{3,7},{4,0},{5,1},{6,2},{7,3},{8,12},{9,13},{10,... | collective-permute-start | bytes 221192 | tf_op jit(solution)/shard_map/ppermute | solution.py:429
  83.7 2.0 %collective-permute-start.14 = (bf16[1,48,768]{2,1,0:T(8,128)(2,1)S(1)}, bf16[1,48,768]{2,1,0:T(8,128)(2,1)S(1)}, u32[]{:S(2)}, u32[]{:S(2)}) collective-permute-start(bf16[1,48,768]{2,1,0:T(8,128)(2,1)S(1)} %get-tuple-element.73), channel_id=1, source_target_pairs={{0,6},{1,7},{2,0},{3,1},{4,2},{5,3},{6,4},{7,5},{8,14},{9,15},{10,... | collective-permute-start | bytes 221192 | tf_op jit(solution)/shard_map/ppermute | solution.py:429
  86.0 2.5 %shard_map.95 = (bf16[256,768]{1,0:T(8,128)(2,1)}, bf16[256,768]{1,0:T(8,128)(2,1)}, f32[1,96]{1,0:T(1,128)}) custom-call(bf16[256,768]{1,0:T(8,128)(2,1)S(1)} %bitcast.16, bf16[768,768]{1,0:T(8,128)(2,1)S(1)} %copy-done, bf16[256,1664]{1,0:T(8,128)(2,1)} %bitcast.7.back_ref), custom_call_target="tpu_custom_call" | custom-call | flops 301989888 | bytes 3211648 | tf_op jit(solution)/shard_map/pallas_call | solution.py:51
  88.5 1.4 %collective-permute-done.13.rest_4_ = bf16[1,48,768]{2,1,0:T(8,128)(2,1)S(1)} collective-permute-done((bf16[1,48,768]{2,1,0:T(8,128)(2,1)S(1)}, bf16[1,48,768]{2,1,0:T(8,128)(2,1)S(1)}, u32[]{:S(2)}, u32[]{:S(2)}) %collective-permute-start.13) | collective-permute-done | bytes 73760 | tf_op jit(solution)/shard_map/ppermute | solution.py:429
  89.8 3.0 %collective-permute-done.7.rest_1_ = bf16[1,48,768]{2,1,0:T(8,128)(2,1)S(1)} collective-permute-done((bf16[1,48,768]{2,1,0:T(8,128)(2,1)S(1)}, bf16[1,48,768]{2,1,0:T(8,128)(2,1)S(1)}, u32[]{:S(2)}, u32[]{:S(2)}) %collective-permute-start.7) | collective-permute-done | bytes 73760 | tf_op jit(solution)/shard_map/ppermute | solution.py:433
  (51 shorter events, 5.1 us)
Async XLA Ops:
  0.6 23.4 %copy-start.14 = (f32[768]{0:T(1024)S(1)}, f32[768]{0:T(1024)}, u32[]{:S(2)}) copy-start(f32[768]{0:T(1024)} %param.6) | copy-start | bytes 9220
  21.4 8.8 %copy-start.5 = (bf16[32,1,8,768]{3,2,1,0:T(8,128)(2,1)}, bf16[32,1,8,768]{3,2,1,0:T(8,128)(2,1)S(1)}, u32[]{:S(2)}) copy-start(bf16[32,1,8,768]{3,2,1,0:T(8,128)(2,1)S(1)} %all_to_all.15) | copy-start | bytes 1179652
  21.4 16.0 %all-to-all-start.1 = ((bf16[32,1,8,768]{3,2,1,0:T(8,128)(2,1)}), bf16[32,1,8,768]{3,2,1,0:T(8,128)(2,1)S(1)}, u32[]{:S(2)}, u32[]{:S(2)}) async-start(bf16[32,1,8,768]{3,2,1,0:T(8,128)(2,1)} %bitcast.19), calls=%async_computation.1 | async-start | bytes 786432 | tf_op jit(solution)/shard_map/all_to_all | solution.py:444
  37.4 4.9 %copy-start.1 = (bf16[768,2304]{1,0:T(8,128)(2,1)S(1)}, bf16[768,2304]{1,0:T(8,128)(2,1)}, u32[]{:S(2)}) copy-start(bf16[768,2304]{1,0:T(8,128)(2,1)} %wqkv_ref.1) | copy-start | bytes 10616836
  37.4 4.9 %copy-start.6 = (bf16[32,1,8,768]{3,2,1,0:T(8,128)(2,1)S(1)}, bf16[32,1,8,768]{3,2,1,0:T(8,128)(2,1)}, u32[]{:S(2)}) copy-start(bf16[32,1,8,768]{3,2,1,0:T(8,128)(2,1)} %copy-done.5) | copy-start | bytes 1179652
  37.4 4.9 %copy-start.9 = (bf16[256,768]{1,0:T(8,128)(2,1)S(1)}, bf16[256,768]{1,0:T(8,128)(2,1)}, u32[]{:S(2)}) copy-start(bf16[256,768]{1,0:T(8,128)(2,1)} %get-tuple-element.45.mixed_ref) | copy-start | bytes 1179652
  42.1 8.1 %collective-permute-start.1 = (bf16[4,256,768]{2,1,0:T(8,128)(2,1)S(1)}, bf16[4,256,768]{2,1,0:T(8,128)(2,1)S(1)}, u32[]{:S(2)}, u32[]{:S(2)}) collective-permute-start(bf16[4,256,768]{2,1,0:T(8,128)(2,1)S(1)} %shard_map.93.blocks_ref.d_ref), channel_id=1, source_target_pairs={{0,1},{1,0},{2,3},{3,2},{4,5},{5,4},{6,7},{7,6},{8,9},{9,8},{10,11... | collective-permute-start | bytes 4718600 | tf_op jit(solution)/shard_map/ppermute | solution.py:274
  43.8 0.9 copy-start.3
  44.7 5.5 %copy-start.2 = (bf16[2,4,96,256]{3,2,1,0:T(8,128)(2,1)S(1)}, bf16[2,4,96,256]{3,2,1,0:T(8,128)(2,1)}, u32[]{:S(2)}) copy-start(bf16[2,4,96,256]{3,2,1,0:T(8,128)(2,1)} %get-tuple-element.48.mine_ref) | copy-start | bytes 1179652
  44.7 41.3 %all-to-all-start.2 = ((bf16[32,1,8,1664]{3,2,1,0:T(8,128)(2,1)}), bf16[32,1,8,1664]{3,2,1,0:T(8,128)(2,1)}, u32[]{:S(2)}, u32[]{:S(2)}) async-start(bf16[32,1,8,1664]{3,2,1,0:T(8,128)(2,1)} %bitcast.14), calls=%async_computation.2 | async-start | bytes 1703936 | tf_op jit(solution)/shard_map/all_to_all | solution.py:451
  48.2 2.0 %collective-permute-start = (bf16[2,4,96,256]{3,2,1,0:T(8,128)(2,1)}, bf16[2,4,96,256]{3,2,1,0:T(8,128)(2,1)S(1)}, u32[]{:S(2)}, u32[]{:S(2)}) collective-permute-start(bf16[2,4,96,256]{3,2,1,0:T(8,128)(2,1)} %get-tuple-element.49), channel_id=1, source_target_pairs={{0,1},{1,0},{2,3},{3,2},{4,5},{5,4},{6,7},{7,6},{8,9},{9,8},{10,11... | collective-permute-start | bytes 1179656 | tf_op jit(solution)/shard_map/ppermute | solution.py:274
  50.9 13.5 %collective-permute-start.2 = (bf16[2,4,48,384]{3,2,1,0:T(8,128)(2,1)S(1)}, bf16[2,4,48,384]{3,2,1,0:T(8,128)(2,1)S(1)}, u32[]{:S(2)}, u32[]{:S(2)}) collective-permute-start(bf16[2,4,48,384]{3,2,1,0:T(8,128)(2,1)S(1)} %get-tuple-element.53), channel_id=1, source_target_pairs={{0,8},{8,0},{16,24},{24,16},{1,9},{9,1},{17,25},{25,17},{2,10},{10... | collective-permute-start | bytes 884744 | tf_op jit(solution)/shard_map/ppermute | solution.py:269
  52.5 13.8 %collective-permute-start.3 = (bf16[2,4,48,384]{3,2,1,0:T(8,128)(2,1)S(1)}, bf16[2,4,48,384]{3,2,1,0:T(8,128)(2,1)S(1)}, u32[]{:S(2)}, u32[]{:S(2)}) collective-permute-start(bf16[2,4,48,384]{3,2,1,0:T(8,128)(2,1)S(1)} %get-tuple-element.54), channel_id=1, source_target_pairs={{0,16},{8,24},{16,0},{24,8},{1,17},{9,25},{17,1},{25,9},{2,18},{10... | collective-permute-start | bytes 884744 | tf_op jit(solution)/shard_map/ppermute | solution.py:269
  54.6 18.2 %collective-permute-start.8 = (bf16[2,4,48,384]{3,2,1,0:T(8,128)(2,1)S(1)}, bf16[2,4,48,384]{3,2,1,0:T(8,128)(2,1)S(1)}, u32[]{:S(2)}, u32[]{:S(2)}) collective-permute-start(bf16[2,4,48,384]{3,2,1,0:T(8,128)(2,1)S(1)} %get-tuple-element.65), channel_id=1, source_target_pairs={{0,8},{8,0},{16,24},{24,16},{1,9},{9,1},{17,25},{25,17},{2,10},{10... | collective-permute-start | bytes 884744 | tf_op jit(solution)/shard_map/ppermute | solution.py:269
  55.2 18.5 %collective-permute-start.9 = (bf16[2,4,48,384]{3,2,1,0:T(8,128)(2,1)S(1)}, bf16[2,4,48,384]{3,2,1,0:T(8,128)(2,1)S(1)}, u32[]{:S(2)}, u32[]{:S(2)}) collective-permute-start(bf16[2,4,48,384]{3,2,1,0:T(8,128)(2,1)S(1)} %get-tuple-element.66), channel_id=1, source_target_pairs={{0,16},{8,24},{16,0},{24,8},{1,17},{9,25},{17,1},{25,9},{2,18},{10... | collective-permute-start | bytes 884744 | tf_op jit(solution)/shard_map/ppermute | solution.py:269
  57.7 16.0 %copy-start.7 = (f32[1,4,48,768]{3,2,1,0:T(8,128)S(1)}, f32[1,4,48,768]{3,2,1,0:T(8,128)}, u32[]{:S(2)}) copy-start(f32[1,4,48,768]{3,2,1,0:T(8,128)} %get-tuple-element.64.refs_2_) | copy-start | bytes 1769476
  66.3 1.1 %copy-start.8 = (f32[1,4,48,768]{3,2,1,0:T(8,128)S(1)}, f32[1,4,48,768]{3,2,1,0:T(8,128)}, u32[]{:S(2)}) copy-start(f32[1,4,48,768]{3,2,1,0:T(8,128)} %get-tuple-element.52.refs_2_) | copy-start | bytes 1769476
  67.4 1.0 %copy-start.12 = (f32[1,4,48,384]{3,2,1,0:T(8,128)S(1)}, f32[1,4,48,384]{3,2,1,0:T(8,128)}, u32[]{:S(2)}) copy-start(f32[1,4,48,384]{3,2,1,0:T(8,128)} %get-tuple-element.50.refs_0_) | copy-start | bytes 884740
  68.3 1.0 %copy-start.13 = (f32[1,4,48,384]{3,2,1,0:T(8,128)S(1)}, f32[1,4,48,384]{3,2,1,0:T(8,128)}, u32[]{:S(2)}) copy-start(f32[1,4,48,384]{3,2,1,0:T(8,128)} %get-tuple-element.51.refs_1_) | copy-start | bytes 884740
  69.3 4.5 %copy-start.10 = (f32[1,4,48,384]{3,2,1,0:T(8,128)S(1)}, f32[1,4,48,384]{3,2,1,0:T(8,128)}, u32[]{:S(2)}) copy-start(f32[1,4,48,384]{3,2,1,0:T(8,128)} %get-tuple-element.62.refs_0_) | copy-start | bytes 884740
  69.3 4.5 %copy-start.11 = (f32[1,4,48,384]{3,2,1,0:T(8,128)S(1)}, f32[1,4,48,384]{3,2,1,0:T(8,128)}, u32[]{:S(2)}) copy-start(f32[1,4,48,384]{3,2,1,0:T(8,128)} %get-tuple-element.63.refs_1_) | copy-start | bytes 884740
  69.4 7.5 %collective-permute-start.4 = (bf16[1,4,48,384]{3,2,1,0:T(8,128)(2,1)S(1)}, bf16[1,4,48,384]{3,2,1,0:T(8,128)(2,1)S(1)}, u32[]{:S(2)}, u32[]{:S(2)}) collective-permute-start(bf16[1,4,48,384]{3,2,1,0:T(8,128)(2,1)S(1)} %get-tuple-element.56), channel_id=1, source_target_pairs={{0,16},{8,24},{16,0},{24,8},{1,17},{9,25},{17,1},{25,9},{2,18},{10... | collective-permute-start | bytes 442376 | tf_op jit(solution)/shard_map/ppermute | solution.py:269
  70.2 6.7 %collective-permute-start.5 = (bf16[1,4,48,384]{3,2,1,0:T(8,128)(2,1)S(1)}, bf16[1,4,48,384]{3,2,1,0:T(8,128)(2,1)S(1)}, u32[]{:S(2)}, u32[]{:S(2)}) collective-permute-start(bf16[1,4,48,384]{3,2,1,0:T(8,128)(2,1)S(1)} %get-tuple-element.57), channel_id=1, source_target_pairs={{0,8},{8,0},{16,24},{24,16},{1,9},{9,1},{17,25},{25,17},{2,10},{10... | collective-permute-start | bytes 442376 | tf_op jit(solution)/shard_map/ppermute | solution.py:269
  73.8 12.2 %copy-start = (bf16[768,768]{1,0:T(8,128)(2,1)S(1)}, bf16[768,768]{1,0:T(8,128)(2,1)}, u32[]{:S(2)}) copy-start(bf16[768,768]{1,0:T(8,128)(2,1)} %wout_ref.1) | copy-start | bytes 3538948
  73.8 12.2 %copy-start.4 = (bf16[1,256,768]{2,1,0:T(8,128)(2,1)S(1)}, bf16[1,256,768]{2,1,0:T(8,128)(2,1)}, u32[]{:S(2)}) copy-start(bf16[1,256,768]{2,1,0:T(8,128)(2,1)} %param.5) | copy-start | bytes 1179652
  73.9 5.4 %collective-permute-start.10 = (bf16[1,4,48,384]{3,2,1,0:T(8,128)(2,1)S(1)}, bf16[1,4,48,384]{3,2,1,0:T(8,128)(2,1)S(1)}, u32[]{:S(2)}, u32[]{:S(2)}) collective-permute-start(bf16[1,4,48,384]{3,2,1,0:T(8,128)(2,1)S(1)} %get-tuple-element.68), channel_id=1, source_target_pairs={{0,16},{8,24},{16,0},{24,8},{1,17},{9,25},{17,1},{25,9},{2,18},{10... | collective-permute-start | bytes 442376 | tf_op jit(solution)/shard_map/ppermute | solution.py:269
  74.8 5.1 %collective-permute-start.11 = (bf16[1,4,48,384]{3,2,1,0:T(8,128)(2,1)S(1)}, bf16[1,4,48,384]{3,2,1,0:T(8,128)(2,1)S(1)}, u32[]{:S(2)}, u32[]{:S(2)}) collective-permute-start(bf16[1,4,48,384]{3,2,1,0:T(8,128)(2,1)S(1)} %get-tuple-element.69), channel_id=1, source_target_pairs={{0,8},{8,0},{16,24},{24,16},{1,9},{9,1},{17,25},{25,17},{2,10},{10... | collective-permute-start | bytes 442376 | tf_op jit(solution)/shard_map/ppermute | solution.py:269
  77.0 8.7 %collective-permute-start.6 = (bf16[2,48,768]{2,1,0:T(8,128)(2,1)S(1)}, bf16[2,48,768]{2,1,0:T(8,128)(2,1)S(1)}, u32[]{:S(2)}, u32[]{:S(2)}) collective-permute-start(bf16[2,48,768]{2,1,0:T(8,128)(2,1)S(1)} %get-tuple-element.59), channel_id=1, source_target_pairs={{0,2},{1,3},{2,0},{3,1},{4,6},{5,7},{6,4},{7,5},{8,10},{9,11},{10,... | collective-permute-start | bytes 442376 | tf_op jit(solution)/shard_map/ppermute | solution.py:433
  80.0 8.5 %collective-permute-start.12 = (bf16[1,48,768]{2,1,0:T(8,128)(2,1)S(1)}, bf16[1,48,768]{2,1,0:T(8,128)(2,1)S(1)}, u32[]{:S(2)}, u32[]{:S(2)}) collective-permute-start(bf16[1,48,768]{2,1,0:T(8,128)(2,1)S(1)} %get-tuple-element.71), channel_id=1, source_target_pairs={{0,2},{1,3},{2,4},{3,5},{4,6},{5,7},{6,0},{7,1},{8,10},{9,11},{10,... | collective-permute-start | bytes 221192 | tf_op jit(solution)/shard_map/ppermute | solution.py:429
  81.5 8.4 %collective-permute-start.13 = (bf16[1,48,768]{2,1,0:T(8,128)(2,1)S(1)}, bf16[1,48,768]{2,1,0:T(8,128)(2,1)S(1)}, u32[]{:S(2)}, u32[]{:S(2)}) collective-permute-start(bf16[1,48,768]{2,1,0:T(8,128)(2,1)S(1)} %get-tuple-element.72), channel_id=1, source_target_pairs={{0,4},{1,5},{2,6},{3,7},{4,0},{5,1},{6,2},{7,3},{8,12},{9,13},{10,... | collective-permute-start | bytes 221192 | tf_op jit(solution)/shard_map/ppermute | solution.py:429
  83.7 6.1 %collective-permute-start.14 = (bf16[1,48,768]{2,1,0:T(8,128)(2,1)S(1)}, bf16[1,48,768]{2,1,0:T(8,128)(2,1)S(1)}, u32[]{:S(2)}, u32[]{:S(2)}) collective-permute-start(bf16[1,48,768]{2,1,0:T(8,128)(2,1)S(1)} %get-tuple-element.73), channel_id=1, source_target_pairs={{0,6},{1,7},{2,0},{3,1},{4,2},{5,3},{6,4},{7,5},{8,14},{9,15},{10,... | collective-permute-start | bytes 221192 | tf_op jit(solution)/shard_map/ppermute | solution.py:429
  85.7 7.2 %collective-permute-start.7 = (bf16[1,48,768]{2,1,0:T(8,128)(2,1)S(1)}, bf16[1,48,768]{2,1,0:T(8,128)(2,1)S(1)}, u32[]{:S(2)}, u32[]{:S(2)}) collective-permute-start(bf16[1,48,768]{2,1,0:T(8,128)(2,1)S(1)} %get-tuple-element.61), channel_id=1, source_target_pairs={{0,4},{1,5},{2,6},{3,7},{4,0},{5,1},{6,2},{7,3},{8,12},{9,13},{10,... | collective-permute-start | bytes 221192 | tf_op jit(solution)/shard_map/ppermute | solution.py:433
